TPU v7x, 512 devices: a whole 4x8x8 slice. The times are simulated.
512 devices in a mesh: rows: 128 (over z, y, core), vec: 4 (over x).
Axes of the slice: x: 4, y: 8, z: 8, core: 2. Of those that a mesh axis runs over, the one named last changes fastest.
Arguments:
- self_tiles: bfloat16 [1024, 256, 256], P('rows'), may hold values from 0.01 to 1, as said below
- link_tiles: bfloat16 [1024, 3, 256, 256], P('rows'), may hold values from 0.01 to 1, as said below
- links: int32 [1024, 3], replicated, may hold values from 0 to 1023, as said below
- coarse_row: int32 [1024], replicated, may hold values from 0 to 511, as said below
- vectors: float32 [16, 262144], P('vec', 'rows'), may hold values from -70 to 70
- directions: float32 [16, 262144], P('vec', 'rows'), may hold values from -70 to 70
Outputs:
- residual: float32 [16, 262144], P('vec', 'rows')
- corrected: float32 [16, 262144], P('vec', 'rows')
- projected: float32 [48, 48], replicated
Inputs may be any that keep to these rules, and one draw needn't show every extreme that they name: For each slot s, links[., s] pairs the row blocks: links[links[b, s], s] = b and links[b, s] != b; the linked block lies on the same slab of 8 blocks as b or on the slab just before or after it (blocks numbered slab by slab). `coarse_row`: each coarse row numbers exactly two row blocks. `self_tiles`: each tile is symmetric, entries positive. link_tiles[b, s] is the transpose of link_tiles[links[b, s], s]; entries positive.
All inputs are finite; a program needn't handle non-finite values.
Results may differ from a plain program's by a relative error of at most 0.0029.
Values may be sent and summed in bfloat16 or wider, within the bound.
No kernel may reach another device: no remote copies, remote signals or barrier semaphores. Data moves between devices by JAX's collectives and lax.ppermute only.
A program may use at most 128 MiB of HBM per device.

v0:
```python
import jax
import jax.numpy as jnp
from jax import lax
from jax.sharding import PartitionSpec as P

spectral_shift = 0.25
damping = 0.6


def padded_2(block, sides, width):
    for axis, dim in sides:
        count = lax.axis_size(axis)
        forward = [(i, i + 1) for i in range(count - 1)]
        backward = [(target, source) for source, target in forward]
        low = lax.ppermute(
            lax.slice_in_dim(block, block.shape[dim] - width, None, axis=dim), axis, forward
        )
        high = lax.ppermute(lax.slice_in_dim(block, 0, width, axis=dim), axis, backward)
        block = jnp.concatenate([low, block, high], axis=dim)
    return block


def for_sending(shard):
    return jax.tree.map(lambda a: a.astype(jnp.bfloat16) if a.dtype == jnp.float32 else a, shard)


def spd_solve(matrix, rhs):
    factor = jnp.linalg.cholesky(matrix)
    return jax.scipy.linalg.cho_solve((factor, True), rhs)


def highest(left, right):
    return jnp.dot(left, right, precision=lax.Precision.HIGHEST)


def body(self_tiles, link_tiles, links, coarse_row, vectors, directions):
    block_count = self_tiles.shape[0]
    block_rows = self_tiles.shape[1]
    vec_count = vectors.shape[0]
    slab_rows = block_count * block_rows
    coarse_count = coarse_row.shape[0] // 2
    block_start = lax.axis_index("rows") * block_count
    degree = (
        jnp.sum(self_tiles, axis=2, dtype=jnp.float32)
        + jnp.sum(link_tiles, axis=(1, 3), dtype=jnp.float32)
    ).reshape(slab_rows)
    root_degree = jnp.sqrt(degree)
    my_links = lax.dynamic_slice_in_dim(links, block_start, block_count, 0)
    window_index = my_links - (block_start - block_count)
    my_coarse = lax.dynamic_slice_in_dim(coarse_row, block_start, block_count, 0)

    def operate(field):
        scaled = (field / root_degree).astype(jnp.bfloat16)
        padded = padded_2(scaled, (("rows", 1),), slab_rows)
        windowed = padded.reshape(vec_count, 3 * block_count, block_rows)
        summed = jnp.einsum(
            "kbj,bij->kbi",
            scaled.reshape(vec_count, block_count, block_rows),
            self_tiles,
            preferred_element_type=jnp.float32,
        )
        remote = jnp.take(windowed, window_index, axis=1)
        summed = summed + jnp.einsum(
            "kbsj,bsij->kbi", remote, link_tiles, preferred_element_type=jnp.float32
        )
        return field - summed.reshape(vec_count, slab_rows) / root_degree

    self_sum = jnp.sum(self_tiles, axis=(1, 2), dtype=jnp.float32)
    link_sum = jnp.sum(link_tiles, axis=(2, 3), dtype=jnp.float32)
    block_degree = degree.reshape(block_count, block_rows).sum(axis=1)
    link_coarse = coarse_row[my_links]
    coarse_part = (
        jnp.zeros((coarse_count, coarse_count), jnp.float32).at[my_coarse, my_coarse].add(self_sum)
    )
    coarse_part = coarse_part.at[my_coarse[:, None], link_coarse].add(link_sum)
    degree_part = jnp.zeros((coarse_count,), jnp.float32).at[my_coarse].add(block_degree)
    tile_sum, agg_degree = lax.psum((coarse_part, degree_part), "rows")
    inv_scale = 1.0 / jnp.sqrt(agg_degree)
    coarse_matrix = (
        ((1.0 + spectral_shift) * jnp.diag(agg_degree) - tile_sum)
        * inv_scale[:, None]
        * inv_scale[None, :]
    )
    coarse_factor = jnp.linalg.cholesky(coarse_matrix)
    image_x = operate(vectors)
    image_p = operate(directions)
    full_x, full_image_x, full_p, full_image_p = (
        lax.all_gather(vectors, "vec", axis=0, tiled=True),
        lax.all_gather(image_x, "vec", axis=0, tiled=True),
        lax.all_gather(directions, "vec", axis=0, tiled=True),
        lax.all_gather(image_p, "vec", axis=0, tiled=True),
    )
    gram_part = highest(full_x, full_x.T)
    cross_part = highest(full_x, full_image_x.T)
    gram_x, cross = lax.psum((gram_part, cross_part), "rows")
    ritz_coef = spd_solve(gram_x, cross)
    ritz_mine = lax.dynamic_slice_in_dim(ritz_coef, lax.axis_index("vec") * vec_count, vec_count, 1)
    residual = image_x - highest(ritz_mine.T, full_x)
    self_diag = jnp.diagonal(self_tiles, axis1=1, axis2=2).astype(jnp.float32).reshape(slab_rows)
    diag_shift = 1.0 + spectral_shift - self_diag / degree
    first = damping * residual / diag_shift
    first_after = operate(first) + spectral_shift * first
    r_one = residual - first_after
    weighted = (root_degree * r_one).reshape(vec_count, block_count, block_rows).sum(axis=2)
    rhs_part = jnp.zeros((vec_count, coarse_count), jnp.float32).at[:, my_coarse].add(weighted)
    coarse_rhs = lax.psum(rhs_part, "rows") * inv_scale[None, :]
    coarse_error = jax.scipy.linalg.cho_solve((coarse_factor, True), coarse_rhs.T).T
    coarse_gain = coarse_error * inv_scale[None, :]
    gain_here = coarse_gain[:, my_coarse]
    lifted = (root_degree.reshape(block_count, block_rows)[None] * gain_here[:, :, None]).reshape(
        vec_count, slab_rows
    )
    second = first + lifted
    after = operate(second) + spectral_shift * second
    corrected = second + damping * (residual - after) / diag_shift
    image_w = operate(corrected)
    full_w, full_image_w = (
        lax.all_gather(for_sending(corrected), "vec", axis=0, tiled=True).astype(corrected.dtype),
        lax.all_gather(for_sending(image_w), "vec", axis=0, tiled=True).astype(image_w.dtype),
    )
    basis = jnp.concatenate([full_x, full_w, full_p], axis=0)
    images = jnp.concatenate([full_image_x, full_image_w, full_image_p], axis=0)
    gram_b_part = highest(basis, basis.T)
    gram_a_part = highest(basis, images.T)
    gram_b, gram_a = lax.psum((gram_b_part, gram_a_part), "rows")
    factor = jnp.linalg.cholesky(gram_b)
    half_solved = jax.scipy.linalg.solve_triangular(factor, gram_a, lower=True)
    reduced = jax.scipy.linalg.solve_triangular(factor, half_solved.T, lower=True)
    projected = 0.5 * (reduced + reduced.T)
    return (residual, corrected, projected)


def solution(mesh):
    in_specs = (
        P("rows", None, None),
        P("rows", None, None, None),
        P(),
        P(),
        P("vec", "rows"),
        P("vec", "rows"),
    )
    out_specs = (P("vec", "rows"), P("vec", "rows"), P())
    return jax.shard_map(body, mesh=mesh, in_specs=in_specs, out_specs=out_specs, check_vma=False)
```

profile of v0, /device:TPU:1, one launch (start us, length us, event | category | flops | bytes accessed | tf_op | source)
XLA Modules:
  0.0 1844.7 jit_solution(11653626460511770603)
XLA Ops:
  7.2 12.7 copy.143
  21.7 2.7 gather_fusion
  26.3 8.7 collective-permute-start.1
  42.2 4.6 scatter_fusion.1
  46.8 2.6 copy.147
  50.6 9.1 all-gather
  65.0 9.8 all-gather.3
  82.0 10.1 all-gather.1
  92.5 495.3 %all-reduce.3 = (f32[16,16]{0,1:T(8,128)S(1)}, f32[16,16]{0,1:T(8,128)S(1)}) all-reduce(f32[16,16]{0,1:T(8,128)S(1)} %convolution_bitcast_fusion.6, f32[16,16]{0,1:T(8,128)} %fusion.121), channel_id=1, replica_groups=mesh['rows'=128,'vec'=4] {'rows'}, use_global_device_ids=true, to_apply=%region_5.7 | all-reduce | flops 512 | bytes 4096 | tf_op jit(solution)/shard_map/psum | solution.py:95
  593.3 7.6 collective-permute-start.3
  606.8 2.4 collective-permute-start.9
  609.2 3.2 collective-permute-start.8
  615.1 485.9 %all-reduce.2 = (f32[512]{0:T(512)S(1)}, f32[4,512]{1,0:T(4,128)S(1)}) all-reduce(f32[512]{0:T(512)S(1)} %copy-done.24, f32[4,512]{1,0:T(4,128)S(1)} %copy.162), channel_id=1, replica_groups=mesh['rows'=128,'vec'=4] {'rows'}, use_global_device_ids=true, to_apply=%region_8.10 | all-reduce | flops 2560 | bytes 20480 | tf_op jit(solution)/shard_map/psum | solution.py:77
  1107.8 2.6 copy.148
  1113.1 11.7 cholesky.144
  1126.1 9.8 custom-call.51
  1139.3 11.7 cholesky.277
  1153.8 9.8 custom-call.52
  1168.5 11.7 cholesky.298
  1181.0 9.8 custom-call.53
  1193.3 12.0 cholesky.315
  1213.4 14.5 while.1
  1227.9 40.1 %custom-call.54 = f32[4,128,128]{1,2,0:T(8,128)S(1)} custom-call(f32[4,128,128]{2,1,0:T(8,128)} %get-tuple-element.12), custom_call_target="InvertDiagBlocksLowerTriangular" | custom-call | tf_op jit(solution)/shard_map/jit(_cho_solve)/triangular_solve | solution.py:107
  1277.4 7.6 collective-permute-start.5
  1292.5 2.4 collective-permute-start.7
  1294.9 3.2 collective-permute-start.6
  1303.7 9.1 all-gather.2
  1312.7 9.1 all-gather.5
  1321.9 9.2 all-gather.4
  1333.9 492.9 %all-reduce.1 = (f32[48,48]{1,0:T(8,128)S(1)}, f32[48,48]{0,1:T(8,128)S(1)}) all-reduce(f32[48,48]{1,0:T(8,128)S(1)} %fusion.6, f32[48,48]{0,1:T(8,128)S(1)} %fusion.124), channel_id=1, replica_groups=mesh['rows'=128,'vec'=4] {'rows'}, use_global_device_ids=true, to_apply=%region_28.30 | all-reduce | flops 4608 | bytes 36864 | tf_op jit(solution)/shard_map/psum | solution.py:125
  1826.8 4.4 cholesky.327
  1832.6 3.7 custom-call.63
  (235 shorter events, 112.0 us)
Async XLA Ops:
  7.2 1098.2 %all-reduce.6.cloned.1.call-start = ((), (), s32[]{:S(2)}) async-start(), calls=%async_computation | async-start | bytes 2097152 | tf_op jit(solution)/shard_map/psum | solution.py:77
  7.2 17.2 copy-start.1
  19.9 6.3 copy-start.13
  19.9 17.1 copy-start
  26.3 51.3 %collective-permute-start.1 = (bf16[4,2048]{1,0:T(4,128)(2,1)S(1)}, bf16[4,2048]{1,0:T(4,128)(2,1)S(1)}, u32[]{:S(2)}, u32[]{:S(2)}) collective-permute-start(bf16[4,2048]{1,0:T(4,128)(2,1)S(1)} %divide_convert_fusion.4), channel_id=1, source_target_pairs={{4,0},{8,4},{12,8},{16,12},{20,16},{24,20},{28,24},{32,28},{36,32}... | collective-permute-start | bytes 49160 | tf_op jit(solution)/shard_map/ppermute | solution.py:18
  35.0 43.2 %collective-permute-start = (bf16[4,2048]{1,0:T(4,128)(2,1)S(1)}, bf16[4,2048]{1,0:T(4,128)(2,1)}, u32[]{:S(2)}, u32[]{:S(2)}) collective-permute-start(bf16[4,2048]{1,0:T(4,128)(2,1)S(1)} %divide_convert_fusion.4), channel_id=1, source_target_pairs={{0,4},{4,8},{8,12},{12,16},{16,20},{20,24},{24,28},{28,32},{32,36}... | collective-permute-start | bytes 49160 | tf_op jit(solution)/shard_map/ppermute | solution.py:15
  37.1 12.9 copy-start.25
  46.8 18.2 copy-start.7
  75.6 5.8 copy-start.21
  92.2 1010.3 %copy-start.5 = (f32[16,2048]{1,0:T(8,128)}, f32[16,2048]{1,0:T(8,128)S(1)}, u32[]{:S(2)}) copy-start(f32[16,2048]{1,0:T(8,128)S(1)} %reshape.342) | copy-start | bytes 393220
  92.2 514.5 %copy-start.8 = (f32[4,2048]{1,0:T(4,128)S(1)}, f32[4,2048]{1,0:T(4,128)}, u32[]{:S(2)}) copy-start(f32[4,2048]{1,0:T(4,128)} %param.15) | copy-start | bytes 98308
  593.2 509.3 %copy-start.10 = (f32[4,2048]{1,0:T(4,128)}, f32[4,2048]{1,0:T(4,128)S(1)}, u32[]{:S(2)}) copy-start(f32[4,2048]{1,0:T(4,128)S(1)} %get-tuple-element.70) | copy-start | bytes 98308
  593.2 21.8 %copy-start.24 = (f32[512]{0:T(512)S(1)}, f32[512]{0:T(512)}, u32[]{:S(2)}) copy-start(f32[512]{0:T(512)} %scatter_custom_fusion) | copy-start | bytes 6148
  593.3 11.1 collective-permute-start.3
  600.8 3.5 collective-permute-start.2
  602.8 500.5 %copy-start.14 = (s32[1024]{0:T(1024)S(1)}, s32[1024]{0:T(1024)}, u32[]{:S(2)}) copy-start(s32[1024]{0:T(1024)} %pad_clamp_fusion.2) | copy-start | bytes 12292
  602.8 501.1 %copy-start.22 = (pred[8,3]{1,0:T(8,128)(4,1)S(1)}, pred[8,3]{1,0:T(8,128)(4,1)}, u32[]{:S(2)}) copy-start(pred[8,3]{1,0:T(8,128)(4,1)} %copy-done.21) | copy-start | bytes 76
  606.8 496.4 %collective-permute-start.9 = (bf16[4,2048]{1,0:T(4,128)(2,1)S(1)}, bf16[4,2048]{1,0:T(4,128)(2,1)S(1)}, u32[]{:S(2)}, u32[]{:S(2)}) collective-permute-start(bf16[4,2048]{1,0:T(4,128)(2,1)S(1)} %get-tuple-element.67), channel_id=1, source_target_pairs={{4,0},{8,4},{12,8},{16,12},{20,16},{24,20},{28,24},{32,28},{36,32}... | collective-permute-start | bytes 49160 | tf_op jit(solution)/shard_map/ppermute | solution.py:18
  609.2 494.0 %collective-permute-start.8 = (bf16[4,2048]{1,0:T(4,128)(2,1)S(1)}, bf16[4,2048]{1,0:T(4,128)(2,1)S(1)}, u32[]{:S(2)}, u32[]{:S(2)}) collective-permute-start(bf16[4,2048]{1,0:T(4,128)(2,1)S(1)} %get-tuple-element.67), channel_id=1, source_target_pairs={{0,4},{4,8},{8,12},{12,16},{16,20},{20,24},{24,28},{28,32},{32,36}... | collective-permute-start | bytes 49160 | tf_op jit(solution)/shard_map/ppermute | solution.py:15
  1100.9 9.4 copy-start.18
  1164.3 49.0 %copy-start.26 = (s32[4]{0:T(128)S(1)}, s32[4]{0:T(128)}, u32[]{:S(2)}) copy-start(s32[4]{0:T(128)} %iota_multiply_fusion) | copy-start | bytes 52
  1166.9 101.2 %copy-start.20 = (f32[512,4]{0,1:T(4,128)S(1)}, f32[512,4]{0,1:T(4,128)}, u32[]{:S(2)}) copy-start(f32[512,4]{0,1:T(4,128)} %multiply_bitcast_fusion) | copy-start | bytes 24580
  1191.8 84.5 %copy-start.19 = (f32[512]{0:T(512)S(1)}, f32[512]{0:T(512)}, u32[]{:S(2)}) copy-start(f32[512]{0:T(512)} %copy-done.18) | copy-start | bytes 6148
  1205.4 72.0 %copy-start.11 = (f32[4,2048]{1,0:T(4,128)S(1)}, f32[4,2048]{1,0:T(4,128)}, u32[]{:S(2)}) copy-start(f32[4,2048]{1,0:T(4,128)} %copy-done.10) | copy-start | bytes 98308
  1277.4 11.9 copy-start.12
  1277.4 11.1 collective-permute-start.5
  1285.0 3.5 collective-permute-start.4
  1289.3 8.8 copy-start.2
  1291.0 40.1 %copy-start.3 = (f32[48,2048]{1,0:T(8,128)S(1)}, f32[48,2048]{1,0:T(8,128)}, u32[]{:S(2)}) copy-start(f32[48,2048]{1,0:T(8,128)} %constant_dynamic-update-slice_fusion.2) | copy-start | bytes 1179652
  1292.5 6.6 collective-permute-start.7
  1294.9 4.2 collective-permute-start.6
  1301.9 1.8 copy-start.17
  (6 other events, 6.4 us)
Sparse Core Ops, SparseCore 0:
  49.6 196.9 all-reduce.5
where the time goes:
time: 1870 us; the launch traced here: 1840 us
  blocking collectives  1530 us (82%)
  other arithmetic  162 us (9%)
  local copies, waits for them, and re-layouts  56.3 us (3%)
  starting transfers between devices  40.8 us (2%)
  matrix products  37.8 us (2%)
    psum x1, blocking collectives, body(): gram_x, cross = lax.psum((gram_part, cross_part), 'rows')  495 us
    psum x1, blocking collectives, body(): gram_b, gram_a = lax.psum((gram_b_part, gram_a_part), 'rows')  493 us
    psum x1, blocking collectives, body(): tile_sum, agg_degree = lax.psum((coarse_part, degree_part), 'rows')  486 us
    another operation x14, other arithmetic, body(): coarse_factor = jnp.linalg.cholesky(coarse_matrix)  80.2 us
    another operation x3, other arithmetic, body(): jax.scipy.linalg.cho_solve((coarse_factor, True), coarse_rhs.T)  43 us
  transfers between devices with their start and end apart: 11, of which 0 were waited for; matrix products, arithmetic and copies ran while one was open for 2% of the time, Pallas kernels for 0%

commit v1 on v0

v1 whole, which is shorter than its diff:
```python
import functools
import jax
import jax.numpy as jnp
from jax import lax
from jax.experimental import pallas as pl
from jax.experimental.pallas import tpu as pltpu
from jax.sharding import Mesh, PartitionSpec as P

spectral_shift = 0.25
damping = 0.6
LANE = 128
GROUPS = 4

F32 = jnp.float32
BF16 = jnp.bfloat16
EXACT = lax.Precision.HIGHEST


def nn(left, right, precision=None):
    return lax.dot_general(
        left, right, (((1,), (0,)), ((), ())), precision=precision, preferred_element_type=F32
    )


def nt(left, right, precision=None):
    return lax.dot_general(
        left, right, (((1,), (1,)), ((), ())), precision=precision, preferred_element_type=F32
    )


def tn(left, right, precision=None):
    return lax.dot_general(
        left, right, (((0,), (0,)), ((), ())), precision=precision, preferred_element_type=F32
    )


def iota(shape, dim):
    return lax.broadcasted_iota(jnp.int32, shape, dim)


def run(kernel, inputs, outputs, scratch=(), smem=0):
    in_specs = [
        pl.BlockSpec(memory_space=pltpu.SMEM if i < smem else pltpu.VMEM)
        for i in range(len(inputs))
    ]
    single = not isinstance(outputs, (list, tuple))
    shapes = [outputs] if single else list(outputs)
    specs = [pl.BlockSpec(memory_space=pltpu.VMEM) for _ in shapes]
    return pl.pallas_call(
        kernel,
        in_specs=in_specs,
        out_specs=specs[0] if single else specs,
        out_shape=shapes[0] if single else shapes,
        scratch_shapes=list(scratch),
    )(*inputs)


def arr(shape, dtype=F32):
    return jax.ShapeDtypeStruct(shape, dtype)


def safe(value):
    return jnp.where(value > 0.0, value, 1.0)


def prep_kernel(links_s, coarse_s, start_s, self_t, link_t, nodes, col, info):
    count, size = self_t.shape[0], self_t.shape[1]
    ones = jnp.ones((8, size), BF16)
    diagonal = iota((size, size), 0) == iota((size, size), 1)
    lane = iota((1, LANE), 1)
    for b in range(count):
        own = self_t[b]
        degree = nt(ones, own)[0:1]
        col[0, b : b + 1, :] = degree
        row = jnp.where(lane == 0, jnp.sum(degree, axis=1, keepdims=True), 0.0)
        ids = jnp.where(lane == 4, coarse_s[start_s[0] + b], 0)
        for s in range(3):
            tile = link_t[b, s]
            part = nt(ones, tile)[0:1]
            degree = degree + part
            row = jnp.where(lane == 1 + s, jnp.sum(part, axis=1, keepdims=True), row)
            ids = jnp.where(lane == 5 + s, coarse_s[links_s[b, s]], ids)
            col[1 + s, b : b + 1, :] = jnp.sum(tile.astype(F32), axis=0, keepdims=True)
        diag = jnp.sum(jnp.where(diagonal, own.astype(F32), 0.0), axis=0, keepdims=True)
        nodes[b : b + 1, :] = degree
        nodes[count + b : count + b + 1, :] = 1.0 + spectral_shift - diag / degree
        info[b : b + 1, :] = row + ids.astype(F32)


def apply_tiles(window_s, self_t, link_t, win, b, count):
    acc = nt(win[count + b], self_t[b])
    for s in range(3):
        acc = acc + nt(win[window_s[b, s]], link_t[b, s])
    return acc


def image_kernel(window_s, self_t, link_t, zc, zl, zh, nc, nl, nh, image, gram, win):
    count, size = self_t.shape[0], self_t.shape[1]
    half = zc.shape[0] // 2
    for part, (z, nodes) in enumerate(((zl, nl), (zc, nc), (zh, nh))):
        for b in range(count):
            root = jnp.sqrt(safe(nodes[b : b + 1, :]))
            win[part * count + b] = (z[:, b * size : (b + 1) * size] / root).astype(BF16)
    for b in range(count):
        acc = apply_tiles(window_s, self_t, link_t, win, b, count)
        span = slice(b * size, (b + 1) * size)
        image[:, span] = zc[:, span] - acc / jnp.sqrt(nc[b : b + 1, :])
    z = zc[...]
    img = image[...]
    basis = nt(z, z, EXACT)
    cross = nt(img, z, EXACT)
    mixed = 0.5 * (cross[:half, half:] + nt(z[:half], img[half:], EXACT))
    gram[:, 0:half] = basis[:half, :half]
    gram[:, half : 2 * half] = basis[:half, half:]
    gram[:, 2 * half : 3 * half] = basis[half:, half:]
    gram[:, 3 * half : 4 * half] = cross[:half, :half]
    gram[:, 4 * half : 5 * half] = mixed
    gram[:, 5 * half : 6 * half] = cross[half:, half:]
    gram[:, 6 * half :] = jnp.zeros((half, LANE - 6 * half), F32)


def restrict_kernel(
    window_s, zc, zl, zh, ic, il, ih, nc, nl, nh, col, gram, info, out, win, weighted, packed
):
    count, size = col.shape[1], col.shape[2]
    half = zc.shape[0] // 2
    width = 2 * half
    for part, (z, img, nodes) in enumerate(((zl, il, nl), (zc, ic, nc), (zh, ih, nh))):
        for b in range(count):
            span = slice(b * size, (b + 1) * size)
            root = jnp.sqrt(safe(nodes[b : b + 1, :]))
            shift = nodes[count + b : count + b + 1, :]
            shift = jnp.where(shift == 0.0, 1.0, shift)
            field = jnp.concatenate([z[:half, span], img[:half, span]], axis=0)
            smooth = damping * field / shift
            win[part * count + b] = smooth / root
            if part == 1:
                weighted[b * width : (b + 1) * width, :] = root * (
                    field - (1.0 + spectral_shift) * smooth
                )
    for b in range(count):
        acc = weighted[b * width : (b + 1) * width, :] + col[0, b : b + 1, :] * win[count + b]
        for s in range(3):
            acc = acc + col[1 + s, b : b + 1, :] * win[window_s[b, s]]
        weighted[b * width : (b + 1) * width, :] = acc
    sums = nt(jnp.ones((8, size), F32), weighted[...], EXACT)
    packed[...] = gram[...]
    for b in range(count):
        packed[b : b + 1, LANE - width :] = sums[0:1, b * width : (b + 1) * width]
        packed[count + b : count + b + 1, LANE - width :] = info[b : b + 1, 0:width]
    value = packed[...]
    for i in range(out.shape[0]):
        out[i] = value


def relay_kernel(got, out, packed):
    members, rows, _ = got.shape
    deep = members // GROUPS
    width = LANE // GROUPS
    total = got[0]
    for i in range(1, members):
        total = total + got[i]
    packed[0:rows, :] = total
    for i in range(members):
        g, j = i // deep, i % deep
        at = rows + j * rows
        packed[at : at + rows, g * width : (g + 1) * width] = got[i][:, LANE - width :]
    value = packed[...]
    for i in range(out.shape[0]):
        out[i] = value


def add_kernel(got, out):
    total = got[0]
    for i in range(1, got.shape[0]):
        total = total + got[i]
    for i in range(out.shape[0]):
        out[i] = total


def invert_dense(matrix):
    n = matrix.shape[0]
    rows = iota((n, 1), 0)
    lanes = iota((1, n), 1)
    for k in range(0, n, 2):
        r0, r1 = matrix[k : k + 1, :], matrix[k + 1 : k + 2, :]
        c0, c1 = matrix[:, k : k + 1], matrix[:, k + 1 : k + 2]
        a, b = r0[:, k : k + 1], r0[:, k + 1 : k + 2]
        c, d = r1[:, k : k + 1], r1[:, k + 1 : k + 2]
        scale = 1.0 / (a * d - b * c)
        first, second = lanes == k, lanes == k + 1
        r0 = jnp.where(first, 1.0, jnp.where(second, 0.0, r0))
        r1 = jnp.where(second, 1.0, jnp.where(first, 0.0, r1))
        n0 = (d * r0 - b * r1) * scale
        n1 = (a * r1 - c * r0) * scale
        unit = jnp.where(rows == lanes, 1.0, 0.0)
        rest = jnp.where(first | second, unit, matrix)
        matrix = rest - c0 * n0 - c1 * n1
        matrix = jnp.where(rows == k, n0, jnp.where(rows == k + 1, n1, matrix))
    return matrix


def split3(value):
    high = value.astype(BF16)
    rest = value - high.astype(F32)
    mid = rest.astype(BF16)
    low = (rest - mid.astype(F32)).astype(BF16)
    return high, mid, low


def coarse_kernel(coarse_s, start_s, got, coef, gain, gram, uw, info, mat, hot):
    members, depth, _ = got.shape
    rows = 16
    half = rows
    deep = (depth - rows) // rows
    width = LANE // GROUPS
    nc = mat.shape[0]
    count = coarse_s.shape[0]
    total = got[0, 0:rows]
    for y in range(1, members):
        total = total + got[y, 0:rows]
    gram[...] = total
    for y in range(members):
        for j in range(deep):
            at = (y * deep + j) * 8
            src = rows + j * rows
            uw[at : at + 8, :] = got[y, src : src + 8]
            info[at : at + 8, :] = got[y, src + 8 : src + 16]
    blocks = uw.shape[0]
    lanes = iota((blocks, nc), 1)
    agg = jnp.zeros((1, nc), F32)
    tiles = jnp.zeros((nc, nc), F32)
    for g in range(GROUPS):
        at = g * width
        values = [info[:, at + s : at + s + 1] for s in range(4)]
        ids = [info[:, at + 4 + s : at + 5 + s].astype(jnp.int32) for s in range(4)]
        here = lanes == ids[0]
        block_degree = values[0] + values[1] + values[2] + values[3]
        agg = agg + jnp.sum(jnp.where(here, block_degree, 0.0), axis=0, keepdims=True)
        spread = jnp.where(here, values[0], 0.0)
        for s in range(1, 4):
            spread = spread + jnp.where(lanes == ids[s], values[s], 0.0)
        member = jnp.where(here, 1.0, 0.0)
        hot[g] = member
        member = member.astype(BF16)
        for piece in split3(spread):
            tiles = tiles + tn(member, piece)
    same = iota((nc, nc), 0) == iota((nc, nc), 1)
    agg_col = jnp.sum(jnp.where(same, agg, 0.0), axis=1, keepdims=True)
    inv_row = 1.0 / jnp.sqrt(agg)
    inv_col = 1.0 / jnp.sqrt(agg_col)
    mat[...] = (jnp.where(same, (1.0 + spectral_shift) * agg, 0.0) - tiles) * inv_col * inv_row

    block = min(LANE, nc)

    def eliminate(step, _):
        at = pl.multiple_of(step * block, block)
        pivot = invert_dense(mat[pl.ds(at, block), pl.ds(at, block)])
        inside_lane = (iota((1, nc), 1) >= at) & (iota((1, nc), 1) < at + block)
        inside_row = (iota((nc, 1), 0) >= at) & (iota((nc, 1), 0) < at + block)
        shifted = iota((block, nc), 0) + at == iota((block, nc), 1)
        strip = jnp.where(inside_lane, jnp.where(shifted, 1.0, 0.0), mat[pl.ds(at, block), :])
        new_rows = nn(pivot, strip, EXACT)
        column = mat[:, pl.ds(at, block)]
        column = jnp.where(inside_row, 0.0, column)
        kept = jnp.where(inside_lane, 0.0, mat[...])
        mat[...] = kept - nn(column, new_rows, EXACT)
        mat[pl.ds(at, block), :] = new_rows
        return 0

    lax.fori_loop(0, nc // block, eliminate, 0)

    ritz = nn(total[:, 3 * half : 4 * half], invert_dense(total[:, 0:half]), EXACT)
    coef[...] = ritz
    unit = jnp.where(iota((half, half), 0) == iota((half, half), 1), 1.0, 0.0)
    combine = jnp.concatenate([-ritz, unit], axis=1)
    rhs = jnp.zeros((half, nc), F32)
    for g in range(GROUPS):
        block_rhs = nt(combine, uw[:, g * width : (g + 1) * width], EXACT)
        rhs = rhs + nn(block_rhs, hot[g], EXACT)
    error = nn(rhs * inv_row, mat[...], EXACT)
    lifted = error * inv_row
    wide = iota((1, nc), 1)
    picks = []
    for j in range(24):
        at = jnp.clip(start_s[0] - 8 + j, 0, count - 1)
        picks.append(jnp.where(wide == coarse_s[at], 1.0, 0.0))
    picks.append(jnp.zeros((8, nc), F32))
    gain[...] = nt(lifted, jnp.concatenate(picks, axis=0), EXACT)


def correct_kernel(
    window_s, self_t, link_t, zc, zl, zh, ic, il, ih, nc, nl, nh, coef, gain,
    residual, corrected, scaled, win, second,
):
    count, size = self_t.shape[0], self_t.shape[1]
    half = zc.shape[0] // 2
    ritz = coef[...]
    gains = gain[...]
    for part, (z, img, nodes) in enumerate(((zl, il, nl), (zc, ic, nc), (zh, ih, nh))):
        res = img[:half, :] - nn(ritz, z[:half, :], EXACT)
        if part == 1:
            residual[...] = res
        for b in range(count):
            span = slice(b * size, (b + 1) * size)
            root = jnp.sqrt(safe(nodes[b : b + 1, :]))
            shift = nodes[count + b : count + b + 1, :]
            shift = jnp.where(shift == 0.0, 1.0, shift)
            j = part * count + b
            field = damping * res[:, span] / shift + root * gains[:, j : j + 1]
            win[j] = (field / root).astype(BF16)
            if part == 1:
                second[:, span] = field
    for b in range(count):
        span = slice(b * size, (b + 1) * size)
        root = jnp.sqrt(nc[b : b + 1, :])
        shift = nc[count + b : count + b + 1, :]
        acc = apply_tiles(window_s, self_t, link_t, win, b, count)
        field = second[:, span]
        after = field - acc / root + spectral_shift * field
        field = field + damping * (residual[:, span] - after) / shift
        corrected[:, span] = field
        scaled[:, span] = (field / root).astype(BF16)


def search_kernel(window_s, self_t, link_t, w, sc, sl, sh, nc, z, img, out, win, image_w):
    count, size = self_t.shape[0], self_t.shape[1]
    half = w.shape[0]
    for part, s in enumerate((sl, sc, sh)):
        for b in range(count):
            win[part * count + b] = s[:, b * size : (b + 1) * size]
    for b in range(count):
        span = slice(b * size, (b + 1) * size)
        acc = apply_tiles(window_s, self_t, link_t, win, b, count)
        image_w[:, span] = w[:, span] - acc / jnp.sqrt(nc[b : b + 1, :])
    field = w[...]
    field_image = image_w[...]
    zz = z[...]
    value = jnp.concatenate(
        [
            nt(field, zz, EXACT),
            nt(field, field, EXACT),
            0.5 * (nt(field, img[...], EXACT) + nt(field_image, zz, EXACT)),
            nt(field, field_image, EXACT),
            jnp.zeros((half, LANE - 6 * half), F32),
        ],
        axis=1,
    )
    for i in range(out.shape[0]):
        out[i] = value


def project_kernel(got, gram, out):
    h = gram.shape[0]
    n = 3 * h
    new = got[0]
    for i in range(1, got.shape[0]):
        new = new + got[i]
    old = gram[...]
    zero = jnp.zeros((h, h), F32)
    unit = jnp.where(iota((n, n), 0) == iota((n, n), 1), 1.0, 0.0)

    def whole(xx, xp, pp, wx, ww, wp):
        upper = jnp.concatenate(
            [
                jnp.concatenate([0.5 * xx, zero, xp], axis=1),
                jnp.concatenate([wx, 0.5 * ww, wp], axis=1),
                jnp.concatenate([zero, zero, 0.5 * pp], axis=1),
            ],
            axis=0,
        )
        return upper + nt(unit, upper, EXACT)

    def piece(a, i):
        return a[:, i * h : (i + 1) * h]

    gram_b = whole(
        piece(old, 0), piece(old, 1), piece(old, 2), piece(new, 0), piece(new, 2), piece(new, 1)
    )
    gram_a = whole(
        piece(old, 3), piece(old, 4), piece(old, 5), piece(new, 3), piece(new, 5), piece(new, 4)
    )
    work = jnp.concatenate([gram_b, unit], axis=1)
    rows = iota((n, 1), 0)
    for k in range(n):
        pivot = work[k : k + 1, :]
        factor = work[:, k : k + 1] / pivot[:, k : k + 1]
        work = work - jnp.where(rows > k, factor, 0.0) * pivot
    diag = jnp.sum(jnp.where(unit > 0.0, work[:, :n], 0.0), axis=1, keepdims=True)
    inverse = work[:, n:] / jnp.sqrt(diag)
    out[...] = nt(nn(inverse, gram_a, EXACT), inverse, EXACT)


def body(self_tiles, link_tiles, links, coarse_row, vectors, directions):
    count, size = self_tiles.shape[0], self_tiles.shape[1]
    mine = vectors.shape[0]
    slab = count * size
    vec = lax.axis_size("vec")
    k = mine * vec
    row_axes = ("z", "y", "core")
    row_index = lax.axis_index(row_axes)
    row_count = lax.axis_size(row_axes)
    stage_one = ("z", "core")
    n_one = lax.axis_size(stage_one)
    n_two = lax.axis_size("y")
    forward = [(i, i + 1) for i in range(row_count - 1)]
    backward = [(i + 1, i) for i in range(row_count - 1)]

    def halo(a):
        return lax.ppermute(a, row_axes, forward), lax.ppermute(a, row_axes, backward)

    start = row_index * count
    start_s = start.reshape(1).astype(jnp.int32)
    links_s = lax.dynamic_slice_in_dim(links, start, count, 0)
    window_s = links_s - (start - count)

    nodes, col, info = run(
        prep_kernel,
        (links_s, coarse_row, start_s, self_tiles, link_tiles),
        (arr((2 * count, size)), arr((4, count, size)), arr((count, LANE))),
        smem=3,
    )
    both = jnp.broadcast_to(
        jnp.concatenate([vectors, directions], axis=0)[None], (vec, 2 * mine, slab)
    )
    both = lax.all_to_all(both, "vec", 0, 0)
    zc = jnp.swapaxes(both.reshape(vec, 2, mine, slab), 0, 1).reshape(2 * k, slab)
    nl, nh = halo(nodes)
    zl, zh = halo(zc)
    image, gram = run(
        image_kernel,
        (window_s, self_tiles, link_tiles, zc, zl, zh, nodes, nl, nh),
        (arr((2 * k, slab)), arr((k, LANE))),
        scratch=(pltpu.VMEM((3 * count, 2 * k, size), BF16),),
        smem=1,
    )
    il, ih = halo(image[:k])
    sent = run(
        restrict_kernel,
        (window_s, zc, zl, zh, image, il, ih, nodes, nl, nh, col, gram, info),
        arr((n_one, 2 * count, LANE)),
        scratch=(
            pltpu.VMEM((3 * count, 2 * k, size), F32),
            pltpu.VMEM((count * 2 * k, size), F32),
            pltpu.VMEM((2 * count, LANE), F32),
        ),
        smem=1,
    )
    got = lax.all_to_all(sent, stage_one, 0, 0)
    depth = 2 * count * (1 + n_one // GROUPS)
    sent = run(
        relay_kernel,
        (got,),
        arr((n_two, depth, LANE)),
        scratch=(pltpu.VMEM((depth, LANE), F32),),
    )
    got = lax.all_to_all(sent, "y", 0, 0)
    coarse_count = coarse_row.shape[0] // 2
    blocks = n_two * (n_one // GROUPS) * count
    coef, gain, gram = run(
        coarse_kernel,
        (coarse_row, start_s, got),
        (arr((k, k)), arr((k, 32)), arr((k, LANE))),
        scratch=(
            pltpu.VMEM((blocks, LANE), F32),
            pltpu.VMEM((blocks, LANE), F32),
            pltpu.VMEM((coarse_count, coarse_count), F32),
            pltpu.VMEM((GROUPS, blocks, coarse_count), F32),
        ),
        smem=2,
    )
    residual, corrected, scaled = run(
        correct_kernel,
        (
            window_s, self_tiles, link_tiles, zc, zl, zh, image, il, ih,
            nodes, nl, nh, coef, gain,
        ),
        (arr((k, slab)), arr((k, slab)), arr((k, slab), BF16)),
        scratch=(pltpu.VMEM((3 * count, k, size), BF16), pltpu.VMEM((k, slab), F32)),
        smem=1,
    )
    sl, sh = halo(scaled)
    sent = run(
        search_kernel,
        (window_s, self_tiles, link_tiles, corrected, scaled, sl, sh, nodes, zc, image),
        arr((n_one, k, LANE)),
        scratch=(pltpu.VMEM((3 * count, k, size), BF16), pltpu.VMEM((k, slab), F32)),
        smem=1,
    )
    got = lax.all_to_all(sent, stage_one, 0, 0)
    sent = run(add_kernel, (got,), arr((n_two, k, LANE)))
    got = lax.all_to_all(sent, "y", 0, 0)
    projected = run(project_kernel, (got, gram), arr((3 * k, 3 * k)))
    at = lax.axis_index("vec") * mine
    return (
        lax.dynamic_slice_in_dim(residual, at, mine, 0),
        lax.dynamic_slice_in_dim(corrected, at, mine, 0),
        projected,
    )


def row_split(rows):
    return (8, rows // 16, 2) if rows >= 64 else (2, rows // 4, 2)


def solution(mesh):
    z, y, core = row_split(mesh.shape["rows"])
    split = Mesh(
        mesh.devices.reshape(z, y, core, mesh.shape["vec"]), ("z", "y", "core", "vec")
    )
    rows = ("z", "y", "core")
    in_specs = (
        P(rows, None, None),
        P(rows, None, None, None),
        P(),
        P(),
        P("vec", rows),
        P("vec", rows),
    )
    out_specs = (P("vec", rows), P("vec", rows), P())
    return jax.shard_map(body, mesh=split, in_specs=in_specs, out_specs=out_specs, check_vma=False)
```

time: 1870 us -> 230 us (0.12); the launches traced: 1840 us -> 229 us
  blocking collectives: 1530 us -> 45.7 us
  other arithmetic: 162 us -> 1.39 us
  Pallas kernels: 0 us -> 106 us
  local copies, waits for them, and re-layouts: 56.3 us -> 8.27 us
  matrix products: 37.8 us -> 0 us
  waiting for transfers between devices: 0.04 us -> 24.4 us
    psum x3 -> x0, blocking collectives: 1470 us -> none  [the longest x1 495 us: body(): gram_x, cross = lax.psum((gram_part, cross_part), 'rows')]
    another operation x28 -> x0, other arithmetic: 137 us -> none  [the longest x14 80.2 us: body(): coarse_factor = jnp.linalg.cholesky(coarse_matrix)]
    pallas_call x0 -> x9, Pallas kernels: none -> 106 us  [run(): pl.pallas_call(kernel, in_specs=in_specs, out_specs=specs[0] if single el...]
    all_gather x6 -> x0, blocking collectives: 56.4 us -> none  [the longest x1 10.1 us: body(): lax.all_gather(image_x, 'vec', axis=0, tiled=True)]
    all_to_all x0 -> x2, blocking collectives: none -> 45.7 us  [the longest x1 27.8 us: body(): got = lax.all_to_all(sent, stage_one, 0, 0)]
    another operation x35 -> x0, local copies, waits for them, and re-layouts: 20.5 us -> none
    all_to_all x0 -> x3, waiting for transfers between devices: none -> 20.4 us  [the longest x1 8.89 us: body(): got = lax.all_to_all(sent, stage_one, 0, 0)]
    dot_general x15 -> x0, matrix products: 20.2 us -> none  [the longest x5 8.24 us: operate(): jnp.einsum('kbsj,bsij->kbi', remote, link_tiles, preferred_element_type=j...]
  transfers between devices with their start and end apart: 11 -> 11, of which waited for: 0 -> 8; matrix products, arithmetic and copies ran while one was open for 2% -> 1% of each run, Pallas kernels for 0% -> 2%
where the time goes in v1:
time: 230 us; the launch traced here: 229 us
  Pallas kernels  106 us (46%)
  blocking collectives  45.7 us (20%)
  starting transfers between devices  43.2 us (19%)
  waiting for transfers between devices  24.4 us (11%)
  local copies, waits for them, and re-layouts  8.27 us (4%)
    pallas_call x9, Pallas kernels, run(): pl.pallas_call(kernel, in_specs=in_specs, out_specs=specs[0] if single el...  106 us
    all_to_all x1, blocking collectives, body(): got = lax.all_to_all(sent, stage_one, 0, 0)  27.8 us
    all_to_all x1, blocking collectives, body(): got = lax.all_to_all(sent, 'y', 0, 0)  17.9 us
    ppermute x4, starting transfers between devices, halo(): lax.ppermute(a, row_axes, backward)  15.1 us
    ppermute x4, starting transfers between devices, halo(): lax.ppermute(a, row_axes, forward)  12.5 us
    all_to_all x1, waiting for transfers between devices, body(): got = lax.all_to_all(sent, stage_one, 0, 0)  8.89 us
    all_to_all x1, starting transfers between devices, body(): got = lax.all_to_all(sent, stage_one, 0, 0)  7.42 us
    all_to_all x1, waiting for transfers between devices, body(): got = lax.all_to_all(sent, 'y', 0, 0)  5.97 us
  transfers between devices with their start and end apart: 11, of which 8 were waited for; matrix products, arithmetic and copies ran while one was open for 1% of the time, Pallas kernels for 2%

profile of v1, /device:TPU:1, one launch (start us, length us, event | category | flops | bytes accessed | tf_op | source)
XLA Modules:
  0.0 229.3 jit_solution(5955002894308524961)
XLA Ops:
  0.6 0.8 pad_maximum_fusion
  1.4 0.7 broadcast_in_dim.2
  2.2 4.8 %all-to-all-start = ((f32[4,8,2048]{2,1,0:T(8,128)}), f32[4,8,2048]{2,1,0:T(8,128)S(1)}, u32[]{:S(2)}, u32[]{:S(2)}) async-start(f32[4,8,2048]{2,1,0:T(8,128)} %broadcast_in_dim.2), calls=%async_computation | async-start | bytes 524288 | tf_op jit(solution)/shard_map/all_to_all | solution.py:426
  7.0 5.5 %all-to-all-done = f32[4,8,2048]{2,1,0:T(8,128)S(1)} async-done(((f32[4,8,2048]{2,1,0:T(8,128)}), f32[4,8,2048]{2,1,0:T(8,128)S(1)}, u32[]{:S(2)}, u32[]{:S(2)}) %all-to-all-start) | async-done | bytes 262176 | tf_op jit(solution)/shard_map/all_to_all | solution.py:426
  13.0 8.4 %collective-permute-start.1 = (f32[32,2048]{1,0:T(8,128)S(1)}, f32[32,2048]{1,0:T(8,128)S(1)}, u32[]{:S(2)}, u32[]{:S(2)}) collective-permute-start(f32[32,2048]{1,0:T(8,128)S(1)} %reshape.17.zc.z), channel_id=1, source_target_pairs={{4,0},{8,4},{12,8},{16,12},{20,16},{24,20},{28,24},{32,28},{36,32}... | collective-permute-start | bytes 786440 | tf_op jit(solution)/shard_map/ppermute | solution.py:410
  21.4 1.9 collective-permute-start
  24.1 4.1 %shard_map.85 = (f32[16,256]{1,0:T(8,128)}, f32[4,8,256]{2,1,0:T(8,128)}, f32[8,128]{1,0:T(8,128)}) custom-call(s32[8,3]{1,0:T(8,128)} %copy.15.links_s, s32[1024]{0:T(1024)} %coarse_s.3, s32[1]{0:T(128)} %bitcast.2.start_s, bf16[8,256,256]{2,1,0:T(8,128)(2,1)} %self_t.7, bf16[8,3,256,256]{3,2,1,0:T(8,128)(2,1)} %link_t.7), custom_call_target="tpu_custom_call" | custom-call | tf_op jit(solution)/shard_map/pallas_call | solution.py:49
  28.2 2.4 %collective-permute-start.3 = (f32[16,256]{1,0:T(8,128)}, f32[16,256]{1,0:T(8,128)S(1)}, u32[]{:S(2)}, u32[]{:S(2)}) collective-permute-start(f32[16,256]{1,0:T(8,128)} %get-tuple-element.14.nc), channel_id=1, source_target_pairs={{4,0},{8,4},{12,8},{16,12},{20,16},{24,20},{28,24},{32,28},{36,32}... | collective-permute-start | bytes 49160 | tf_op jit(solution)/shard_map/ppermute | solution.py:410
  30.7 3.1 %collective-permute-start.2 = (f32[16,256]{1,0:T(8,128)}, f32[16,256]{1,0:T(8,128)S(1)}, u32[]{:S(2)}, u32[]{:S(2)}) collective-permute-start(f32[16,256]{1,0:T(8,128)} %get-tuple-element.14.nc), channel_id=1, source_target_pairs={{0,4},{4,8},{8,12},{12,16},{16,20},{20,24},{24,28},{28,32},{32,36}... | collective-permute-start | bytes 49160 | tf_op jit(solution)/shard_map/ppermute | solution.py:410
  36.3 5.0 %shard_map.86 = (f32[32,2048]{1,0:T(8,128)}, f32[16,128]{1,0:T(8,128)}) custom-call(s32[8,3]{1,0:T(8,128)} %broadcast_subtract_fusion.window_s, bf16[8,256,256]{2,1,0:T(8,128)(2,1)} %self_t.7, bf16[8,3,256,256]{3,2,1,0:T(8,128)(2,1)} %link_t.7, f32[32,2048]{1,0:T(8,128)} %copy-done.1, f32[32,2048]{1,0:T(8,128)} %copy-done.3, f32[32,2048]{1,0:T(8,128)} %copy-done.2, ...), custom_call_target="tpu_custom_call" | custom-call | tf_op jit(solution)/shard_map/pallas_call | solution.py:49
  41.2 0.9 slice.3
  42.1 1.9 collective-permute-start.5
  44.1 4.2 %collective-permute-start.4 = (f32[16,2048]{1,0:T(8,128)S(1)}, f32[16,2048]{1,0:T(8,128)S(1)}, u32[]{:S(2)}, u32[]{:S(2)}) collective-permute-start(f32[16,2048]{1,0:T(8,128)S(1)} %slice.3), channel_id=1, source_target_pairs={{0,4},{4,8},{8,12},{12,16},{16,20},{20,24},{24,28},{28,32},{32,36}... | collective-permute-start | bytes 393224 | tf_op jit(solution)/shard_map/ppermute | solution.py:410
  48.3 0.7 collective-permute-done.5.ih
  49.0 1.2 collective-permute-done.4.il
  50.8 2.6 %shard_map.87 = f32[16,16,128]{2,1,0:T(8,128)} custom-call(s32[8,3]{1,0:T(8,128)} %broadcast_subtract_fusion.window_s, f32[32,2048]{1,0:T(8,128)} %copy-done.1, f32[32,2048]{1,0:T(8,128)} %copy-done.3, f32[32,2048]{1,0:T(8,128)} %copy-done.2, f32[32,2048]{1,0:T(8,128)} %get-tuple-element.15.ic.img, f32[16,2048]{1,0:T(8,128)} %copy-done.5, ...), custom_call_target="tpu_custom_call" | custom-call | tf_op jit(solution)/shard_map/pallas_call | solution.py:49
  53.4 27.8 %all_to_all.25.got = f32[16,16,128]{2,1,0:T(8,128)} all-to-all(f32[16,16,128]{2,1,0:T(8,128)} %shard_map.87), channel_id=1, replica_groups=mesh['z'=8,'y'=8,'core'=2,'vec'=4] {'z','core'}, dimensions={0} | all-to-all | bytes 262144 | tf_op jit(solution)/shard_map/all_to_all | solution.py:449
  81.3 1.7 shard_map.88
  83.0 17.9 %all_to_all.26.got = f32[8,80,128]{2,1,0:T(8,128)} all-to-all(f32[8,80,128]{2,1,0:T(8,128)} %shard_map.88), channel_id=1, replica_groups=mesh['z'=8,'y'=8,'core'=2,'vec'=4] {'y'}, dimensions={0} | all-to-all | bytes 655360 | tf_op jit(solution)/shard_map/all_to_all | solution.py:457
  100.9 74.2 %shard_map.89 = (f32[16,16]{1,0:T(8,128)}, f32[16,32]{1,0:T(8,128)}, f32[16,128]{1,0:T(8,128)}) custom-call(s32[1024]{0:T(1024)} %coarse_s.3, s32[1]{0:T(128)} %bitcast.2.start_s, f32[8,80,128]{2,1,0:T(8,128)} %all_to_all.26.got), custom_call_target="tpu_custom_call" | custom-call | tf_op jit(solution)/shard_map/pallas_call | solution.py:49
  175.1 5.0 %shard_map.90 = (f32[16,2048]{1,0:T(8,128)}, f32[16,2048]{1,0:T(8,128)}, bf16[16,2048]{1,0:T(8,128)(2,1)}) custom-call(s32[8,3]{1,0:T(8,128)} %broadcast_subtract_fusion.window_s, bf16[8,256,256]{2,1,0:T(8,128)(2,1)} %self_t.7, bf16[8,3,256,256]{3,2,1,0:T(8,128)(2,1)} %link_t.7, f32[32,2048]{1,0:T(8,128)} %copy-done.1, f32[32,2048]{1,0:T(8,128)} %copy-done.3, ...), custom_call_target="tpu_custom_call" | custom-call | tf_op jit(solution)/shard_map/pallas_call | solution.py:49
  180.1 2.3 %collective-permute-start.7 = (bf16[16,2048]{1,0:T(8,128)(2,1)}, bf16[16,2048]{1,0:T(8,128)(2,1)S(1)}, u32[]{:S(2)}, u32[]{:S(2)}) collective-permute-start(bf16[16,2048]{1,0:T(8,128)(2,1)} %get-tuple-element.23.sc), channel_id=1, source_target_pairs={{4,0},{8,4},{12,8},{16,12},{20,16},{24,20},{28,24},{32,28},{36,32}... | collective-permute-start | bytes 196616 | tf_op jit(solution)/shard_map/ppermute | solution.py:410
  182.4 3.2 %collective-permute-start.6 = (bf16[16,2048]{1,0:T(8,128)(2,1)}, bf16[16,2048]{1,0:T(8,128)(2,1)S(1)}, u32[]{:S(2)}, u32[]{:S(2)}) collective-permute-start(bf16[16,2048]{1,0:T(8,128)(2,1)} %get-tuple-element.23.sc), channel_id=1, source_target_pairs={{0,4},{4,8},{8,12},{12,16},{16,20},{20,24},{24,28},{28,32},{32,36}... | collective-permute-start | bytes 196616 | tf_op jit(solution)/shard_map/ppermute | solution.py:410
  185.8 1.4 collective-permute-done.6.sl
  187.9 5.4 %shard_map.91 = f32[16,16,128]{2,1,0:T(8,128)} custom-call(s32[8,3]{1,0:T(8,128)} %broadcast_subtract_fusion.window_s, bf16[8,256,256]{2,1,0:T(8,128)(2,1)} %self_t.7, bf16[8,3,256,256]{3,2,1,0:T(8,128)(2,1)} %link_t.7, f32[16,2048]{1,0:T(8,128)} %get-tuple-element.22.w, bf16[16,2048]{1,0:T(8,128)(2,1)} %get-tuple-element.23.sc, ...), custom_call_target="tpu_custom_call" | custom-call | tf_op jit(solution)/shard_map/pallas_call | solution.py:49
  193.3 7.4 %all-to-all-start.3 = ((f32[16,16,128]{2,1,0:T(8,128)}), f32[16,16,128]{2,1,0:T(8,128)S(1)}, u32[]{:S(2)}, u32[]{:S(2)}) async-start(f32[16,16,128]{2,1,0:T(8,128)} %shard_map.91), calls=%async_computation.3 | async-start | bytes 262144 | tf_op jit(solution)/shard_map/all_to_all | solution.py:490
  200.7 8.9 %all-to-all-done.3.got = f32[16,16,128]{2,1,0:T(8,128)S(1)} async-done(((f32[16,16,128]{2,1,0:T(8,128)}), f32[16,16,128]{2,1,0:T(8,128)S(1)}, u32[]{:S(2)}, u32[]{:S(2)}) %all-to-all-start.3) | async-done | bytes 131104 | tf_op jit(solution)/shard_map/all_to_all | solution.py:490
  210.2 1.5 shard_map.92
  211.8 3.3 %all-to-all-start.4 = ((f32[8,16,128]{2,1,0:T(8,128)}), f32[8,16,128]{2,1,0:T(8,128)S(1)}, u32[]{:S(2)}, u32[]{:S(2)}) async-start(f32[8,16,128]{2,1,0:T(8,128)} %shard_map.92), calls=%async_computation.4 | async-start | bytes 131072 | tf_op jit(solution)/shard_map/all_to_all | solution.py:492
  215.1 1.5 constant_dynamic-slice_fusion
  216.7 6.0 %all-to-all-done.4.got = f32[8,16,128]{2,1,0:T(8,128)S(1)} async-done(((f32[8,16,128]{2,1,0:T(8,128)}), f32[8,16,128]{2,1,0:T(8,128)S(1)}, u32[]{:S(2)}, u32[]{:S(2)}) %all-to-all-start.4) | async-done | bytes 65568 | tf_op jit(solution)/shard_map/all_to_all | solution.py:492
  223.2 6.1 %shard_map.93 = f32[48,48]{1,0:T(8,128)} custom-call(f32[8,16,128]{2,1,0:T(8,128)} %copy-done.7, f32[16,128]{1,0:T(8,128)} %get-tuple-element.24.gram), custom_call_target="tpu_custom_call" | custom-call | tf_op jit(solution)/shard_map/pallas_call | solution.py:49
  (37 shorter events, 6.4 us)
Async XLA Ops:
  0.6 22.7 %copy-start = (s32[1024,3]{0,1:T(4,128)S(1)}, s32[1024,3]{0,1:T(4,128)}, u32[]{:S(2)}) copy-start(s32[1024,3]{0,1:T(4,128)} %param.8) | copy-start | bytes 36868
  2.2 10.4 %all-to-all-start = ((f32[4,8,2048]{2,1,0:T(8,128)}), f32[4,8,2048]{2,1,0:T(8,128)S(1)}, u32[]{:S(2)}, u32[]{:S(2)}) async-start(f32[4,8,2048]{2,1,0:T(8,128)} %broadcast_in_dim.2), calls=%async_computation | async-start | bytes 524288 | tf_op jit(solution)/shard_map/all_to_all | solution.py:426
  13.0 21.9 %copy-start.1 = (f32[32,2048]{1,0:T(8,128)}, f32[32,2048]{1,0:T(8,128)S(1)}, u32[]{:S(2)}) copy-start(f32[32,2048]{1,0:T(8,128)S(1)} %reshape.17.zc.z) | copy-start | bytes 786436
  13.0 21.9 %collective-permute-start.1 = (f32[32,2048]{1,0:T(8,128)S(1)}, f32[32,2048]{1,0:T(8,128)S(1)}, u32[]{:S(2)}, u32[]{:S(2)}) collective-permute-start(f32[32,2048]{1,0:T(8,128)S(1)} %reshape.17.zc.z), channel_id=1, source_target_pairs={{4,0},{8,4},{12,8},{16,12},{20,16},{24,20},{28,24},{32,28},{36,32}... | collective-permute-start | bytes 786440 | tf_op jit(solution)/shard_map/ppermute | solution.py:410
  21.4 13.4 %collective-permute-start = (f32[32,2048]{1,0:T(8,128)S(1)}, f32[32,2048]{1,0:T(8,128)S(1)}, u32[]{:S(2)}, u32[]{:S(2)}) collective-permute-start(f32[32,2048]{1,0:T(8,128)S(1)} %reshape.17.zc.z), channel_id=1, source_target_pairs={{0,4},{4,8},{8,12},{12,16},{16,20},{20,24},{24,28},{28,32},{32,36}... | collective-permute-start | bytes 786440 | tf_op jit(solution)/shard_map/ppermute | solution.py:410
  24.1 9.7 %copy-start.12 = (s32[8,3]{1,0:T(8,128)S(1)}, s32[8,3]{1,0:T(8,128)}, u32[]{:S(2)}) copy-start(s32[8,3]{1,0:T(8,128)} %copy.15.links_s) | copy-start | bytes 292
  28.2 6.2 %collective-permute-start.3 = (f32[16,256]{1,0:T(8,128)}, f32[16,256]{1,0:T(8,128)S(1)}, u32[]{:S(2)}, u32[]{:S(2)}) collective-permute-start(f32[16,256]{1,0:T(8,128)} %get-tuple-element.14.nc), channel_id=1, source_target_pairs={{4,0},{8,4},{12,8},{16,12},{20,16},{24,20},{28,24},{32,28},{36,32}... | collective-permute-start | bytes 49160 | tf_op jit(solution)/shard_map/ppermute | solution.py:410
  30.7 4.2 %collective-permute-start.2 = (f32[16,256]{1,0:T(8,128)}, f32[16,256]{1,0:T(8,128)S(1)}, u32[]{:S(2)}, u32[]{:S(2)}) collective-permute-start(f32[16,256]{1,0:T(8,128)} %get-tuple-element.14.nc), channel_id=1, source_target_pairs={{0,4},{4,8},{8,12},{12,16},{16,20},{20,24},{24,28},{28,32},{32,36}... | collective-permute-start | bytes 49160 | tf_op jit(solution)/shard_map/ppermute | solution.py:410
  34.4 0.6 copy-start.8
  34.9 0.6 copy-start.9
  34.9 0.7 copy-start.2
  35.6 0.7 copy-start.3
  42.1 6.8 %collective-permute-start.5 = (f32[16,2048]{1,0:T(8,128)S(1)}, f32[16,2048]{1,0:T(8,128)S(1)}, u32[]{:S(2)}, u32[]{:S(2)}) collective-permute-start(f32[16,2048]{1,0:T(8,128)S(1)} %slice.3), channel_id=1, source_target_pairs={{4,0},{8,4},{12,8},{16,12},{20,16},{24,20},{28,24},{32,28},{36,32}... | collective-permute-start | bytes 393224 | tf_op jit(solution)/shard_map/ppermute | solution.py:410
  44.1 6.1 %collective-permute-start.4 = (f32[16,2048]{1,0:T(8,128)S(1)}, f32[16,2048]{1,0:T(8,128)S(1)}, u32[]{:S(2)}, u32[]{:S(2)}) collective-permute-start(f32[16,2048]{1,0:T(8,128)S(1)} %slice.3), channel_id=1, source_target_pairs={{0,4},{4,8},{8,12},{12,16},{16,20},{20,24},{24,28},{28,32},{32,36}... | collective-permute-start | bytes 393224 | tf_op jit(solution)/shard_map/ppermute | solution.py:410
  49.0 1.2 copy-start.4
  50.2 0.6 copy-start.5
  180.1 5.8 %collective-permute-start.7 = (bf16[16,2048]{1,0:T(8,128)(2,1)}, bf16[16,2048]{1,0:T(8,128)(2,1)S(1)}, u32[]{:S(2)}, u32[]{:S(2)}) collective-permute-start(bf16[16,2048]{1,0:T(8,128)(2,1)} %get-tuple-element.23.sc), channel_id=1, source_target_pairs={{4,0},{8,4},{12,8},{16,12},{20,16},{24,20},{28,24},{32,28},{36,32}... | collective-permute-start | bytes 196616 | tf_op jit(solution)/shard_map/ppermute | solution.py:410
  182.4 4.9 %collective-permute-start.6 = (bf16[16,2048]{1,0:T(8,128)(2,1)}, bf16[16,2048]{1,0:T(8,128)(2,1)S(1)}, u32[]{:S(2)}, u32[]{:S(2)}) collective-permute-start(bf16[16,2048]{1,0:T(8,128)(2,1)} %get-tuple-element.23.sc), channel_id=1, source_target_pairs={{0,4},{4,8},{8,12},{12,16},{16,20},{20,24},{24,28},{28,32},{32,36}... | collective-permute-start | bytes 196616 | tf_op jit(solution)/shard_map/ppermute | solution.py:410
  185.8 1.4 copy-start.10
  187.2 0.6 copy-start.11
  193.3 16.3 %all-to-all-start.3 = ((f32[16,16,128]{2,1,0:T(8,128)}), f32[16,16,128]{2,1,0:T(8,128)S(1)}, u32[]{:S(2)}, u32[]{:S(2)}) async-start(f32[16,16,128]{2,1,0:T(8,128)} %shard_map.91), calls=%async_computation.3 | async-start | bytes 262144 | tf_op jit(solution)/shard_map/all_to_all | solution.py:490
  209.6 0.6 copy-start.6
  211.8 10.8 %all-to-all-start.4 = ((f32[8,16,128]{2,1,0:T(8,128)}), f32[8,16,128]{2,1,0:T(8,128)S(1)}, u32[]{:S(2)}, u32[]{:S(2)}) async-start(f32[8,16,128]{2,1,0:T(8,128)} %shard_map.92), calls=%async_computation.4 | async-start | bytes 131072 | tf_op jit(solution)/shard_map/all_to_all | solution.py:492
  222.6 0.6 copy-start.7

commit v2 on v1

--- a/solution.py
+++ b/solution.py
@@ -1,4 +1,3 @@
-import functools
 import jax
 import jax.numpy as jnp
 from jax import lax
@@ -38,7 +37,7 @@
     return lax.broadcasted_iota(jnp.int32, shape, dim)
 
 
-def run(kernel, inputs, outputs, scratch=(), smem=0):
+def run(kernel, inputs, outputs, scratch=(), smem=0, work=0):
     in_specs = [
         pl.BlockSpec(memory_space=pltpu.SMEM if i < smem else pltpu.VMEM)
         for i in range(len(inputs))
@@ -52,6 +51,9 @@
         out_specs=specs[0] if single else specs,
         out_shape=shapes[0] if single else shapes,
         scratch_shapes=list(scratch),
+        cost_estimate=pl.CostEstimate(
+            flops=work, bytes_accessed=sum(a.size * a.dtype.itemsize for a in inputs), transcendentals=0
+        ),
     )(*inputs)
 
 
@@ -82,9 +84,20 @@
             ids = jnp.where(lane == 5 + s, coarse_s[links_s[b, s]], ids)
             col[1 + s, b : b + 1, :] = jnp.sum(tile.astype(F32), axis=0, keepdims=True)
         diag = jnp.sum(jnp.where(diagonal, own.astype(F32), 0.0), axis=0, keepdims=True)
-        nodes[b : b + 1, :] = degree
-        nodes[count + b : count + b + 1, :] = 1.0 + spectral_shift - diag / degree
+        span = slice(b * size, (b + 1) * size)
+        nodes[0:1, span] = degree
+        nodes[1:2, span] = 1.0 + spectral_shift - diag / degree
         info[b : b + 1, :] = row + ids.astype(F32)
+    nodes[2:8, :] = jnp.zeros((6, nodes.shape[1]), F32)
+
+
+def pack_kernel(both, nodes, out):
+    members, twice, _ = both.shape
+    mine = twice // 2
+    for v in range(members):
+        out[v * mine : (v + 1) * mine, :] = both[v, :mine]
+        out[(members + v) * mine : (members + v + 1) * mine, :] = both[v, mine:]
+    out[members * twice :, :] = nodes[...]
 
 
 def apply_tiles(window_s, self_t, link_t, win, b, count):
@@ -94,45 +107,54 @@
     return acc
 
 
-def image_kernel(window_s, self_t, link_t, zc, zl, zh, nc, nl, nh, image, gram, win):
+def image_kernel(window_s, self_t, link_t, fc, fl, fh, image_x, image_p, gram, win):
     count, size = self_t.shape[0], self_t.shape[1]
-    half = zc.shape[0] // 2
-    for part, (z, nodes) in enumerate(((zl, nl), (zc, nc), (zh, nh))):
+    half = image_x.shape[0]
+    both = 2 * half
+    for part, f in enumerate((fl, fc, fh)):
         for b in range(count):
-            root = jnp.sqrt(safe(nodes[b : b + 1, :]))
-            win[part * count + b] = (z[:, b * size : (b + 1) * size] / root).astype(BF16)
+            span = slice(b * size, (b + 1) * size)
+            root = jnp.sqrt(safe(f[both : both + 1, span]))
+            win[part * count + b] = (f[:both, span] / root).astype(BF16)
     for b in range(count):
         acc = apply_tiles(window_s, self_t, link_t, win, b, count)
         span = slice(b * size, (b + 1) * size)
-        image[:, span] = zc[:, span] - acc / jnp.sqrt(nc[b : b + 1, :])
-    z = zc[...]
-    img = image[...]
+        value = fc[:both, span] - acc / jnp.sqrt(fc[both : both + 1, span])
+        image_x[:, span] = value[:half]
+        image_p[:, span] = value[half:]
+    z = fc[:both, :]
+    ix = image_x[...]
+    ip = image_p[...]
     basis = nt(z, z, EXACT)
-    cross = nt(img, z, EXACT)
-    mixed = 0.5 * (cross[:half, half:] + nt(z[:half], img[half:], EXACT))
+    cross = nt(ix, z, EXACT)
+    other = nt(ip, z, EXACT)
+    mixed = 0.5 * (cross[:, half:] + nt(z[:half], ip, EXACT))
     gram[:, 0:half] = basis[:half, :half]
     gram[:, half : 2 * half] = basis[:half, half:]
     gram[:, 2 * half : 3 * half] = basis[half:, half:]
-    gram[:, 3 * half : 4 * half] = cross[:half, :half]
+    gram[:, 3 * half : 4 * half] = cross[:, :half]
     gram[:, 4 * half : 5 * half] = mixed
-    gram[:, 5 * half : 6 * half] = cross[half:, half:]
+    gram[:, 5 * half : 6 * half] = other[:, half:]
     gram[:, 6 * half :] = jnp.zeros((half, LANE - 6 * half), F32)
 
 
+def node_scales(f, both, span):
+    shift = f[both + 1 : both + 2, span]
+    return jnp.sqrt(safe(f[both : both + 1, span])), jnp.where(shift == 0.0, 1.0, shift)
+
+
 def restrict_kernel(
-    window_s, zc, zl, zh, ic, il, ih, nc, nl, nh, col, gram, info, out, win, weighted, packed
+    window_s, fc, fl, fh, ic, il, ih, col, gram, info, out, win, weighted, packed
 ):
     count, size = col.shape[1], col.shape[2]
-    half = zc.shape[0] // 2
+    half = ic.shape[0]
     width = 2 * half
-    for part, (z, img, nodes) in enumerate(((zl, il, nl), (zc, ic, nc), (zh, ih, nh))):
+    for part, (f, img) in enumerate(((fl, il), (fc, ic), (fh, ih))):
         for b in range(count):
             span = slice(b * size, (b + 1) * size)
-            root = jnp.sqrt(safe(nodes[b : b + 1, :]))
-            shift = nodes[count + b : count + b + 1, :]
-            shift = jnp.where(shift == 0.0, 1.0, shift)
-            field = jnp.concatenate([z[:half, span], img[:half, span]], axis=0)
-            smooth = damping * field / shift
+            root, shift = node_scales(f, width, span)
+            field = jnp.concatenate([f[:half, span], img[:, span]], axis=0)
+            smooth = field * (damping / shift)
             win[part * count + b] = smooth / root
             if part == 1:
                 weighted[b * width : (b + 1) * width, :] = root * (
@@ -178,26 +200,150 @@
         out[i] = total
 
 
-def invert_dense(matrix):
+def sum4(xs, ys):
+    return (xs[0] * ys[0] + xs[1] * ys[1]) + (xs[2] * ys[2] + xs[3] * ys[3])
+
+
+def inverse4(e):
+    def g(i, j):
+        return e[min(i, j), max(i, j)]
+
+    def minor(r0, r1, c0, c1):
+        return g(r0, c0) * g(r1, c1) - g(r0, c1) * g(r1, c0)
+
+    s0, s1, s2 = minor(0, 1, 0, 1), minor(0, 1, 0, 2), minor(0, 1, 0, 3)
+    s3, s4, s5 = minor(0, 1, 1, 2), minor(0, 1, 1, 3), minor(0, 1, 2, 3)
+    c5, c4, c3 = minor(2, 3, 2, 3), minor(2, 3, 1, 3), minor(2, 3, 1, 2)
+    c2, c1, c0 = minor(2, 3, 0, 3), minor(2, 3, 0, 2), minor(2, 3, 0, 1)
+    r = 1.0 / (((s0 * c5 - s1 * c4) + (s2 * c3 + s3 * c2)) + (s5 * c0 - s4 * c1))
+    q = {
+        (0, 0): (g(1, 1) * c5 - g(1, 2) * c4 + g(1, 3) * c3) * r,
+        (0, 1): (g(0, 2) * c4 - g(0, 1) * c5 - g(0, 3) * c3) * r,
+        (0, 2): (g(3, 1) * s5 - g(3, 2) * s4 + g(3, 3) * s3) * r,
+        (0, 3): (g(2, 2) * s4 - g(2, 1) * s5 - g(2, 3) * s3) * r,
+        (1, 1): (g(0, 0) * c5 - g(0, 2) * c2 + g(0, 3) * c1) * r,
+        (1, 2): (g(3, 2) * s2 - g(3, 0) * s5 - g(3, 3) * s1) * r,
+        (1, 3): (g(2, 0) * s5 - g(2, 2) * s2 + g(2, 3) * s1) * r,
+        (2, 2): (g(3, 0) * s4 - g(3, 1) * s2 + g(3, 3) * s0) * r,
+        (2, 3): (g(2, 1) * s2 - g(2, 0) * s4 - g(2, 3) * s0) * r,
+        (3, 3): (g(2, 0) * s3 - g(2, 1) * s1 + g(2, 2) * s0) * r,
+    }
+    return [[q[min(i, j), max(i, j)] for j in range(4)] for i in range(4)]
+
+
+def inverse8(e):
+    q = inverse4(e)
+    side = [[e[i, 4 + j] for i in range(4)] for j in range(4)]
+    w = [[sum4(q[i], side[j]) for j in range(4)] for i in range(4)]
+    wt = [[w[i][j] for i in range(4)] for j in range(4)]
+    schur = {
+        (i, j): e[4 + i, 4 + j] - sum4(side[i], wt[j]) for i in range(4) for j in range(i, 4)
+    }
+    x = inverse4(schur)
+    u = [[-sum4(w[i], x[j]) for j in range(4)] for i in range(4)]
+    full = [[None] * 8 for _ in range(8)]
+    for i in range(4):
+        for j in range(4):
+            full[4 + i][4 + j] = x[i][j]
+            full[i][4 + j] = u[i][j]
+            full[4 + j][i] = u[i][j]
+            if j >= i:
+                full[i][j] = q[i][j] - sum4(u[i], w[j])
+                full[j][i] = full[i][j]
+    return full
+
+
+def inverse2(e):
+    r = 1.0 / (e[0, 0] * e[1, 1] - e[0, 1] * e[0, 1])
+    off = -e[0, 1] * r
+    return [[e[1, 1] * r, off], [off, e[0, 0] * r]]
+
+
+def spread_block(tile, k, width, shape):
+    s = k % 8
+    cols = [jnp.broadcast_to(tile[:, k + j : k + j + 1], shape) for j in range(width)]
+    entries = {
+        (i, j): jnp.broadcast_to(cols[j][s + i : s + i + 1, :], shape)
+        for i in range(width)
+        for j in range(i, width)
+    }
+    rows = [jnp.broadcast_to(tile[s + i : s + i + 1, :], shape) for i in range(width)]
+    return cols, entries, rows
+
+
+def invert_dense(matrix, width, block_inverse):
     n = matrix.shape[0]
-    rows = iota((n, 1), 0)
-    lanes = iota((1, n), 1)
-    for k in range(0, n, 2):
-        r0, r1 = matrix[k : k + 1, :], matrix[k + 1 : k + 2, :]
-        c0, c1 = matrix[:, k : k + 1], matrix[:, k + 1 : k + 2]
-        a, b = r0[:, k : k + 1], r0[:, k + 1 : k + 2]
-        c, d = r1[:, k : k + 1], r1[:, k + 1 : k + 2]
-        scale = 1.0 / (a * d - b * c)
-        first, second = lanes == k, lanes == k + 1
-        r0 = jnp.where(first, 1.0, jnp.where(second, 0.0, r0))
-        r1 = jnp.where(second, 1.0, jnp.where(first, 0.0, r1))
-        n0 = (d * r0 - b * r1) * scale
-        n1 = (a * r1 - c * r0) * scale
-        unit = jnp.where(rows == lanes, 1.0, 0.0)
-        rest = jnp.where(first | second, unit, matrix)
-        matrix = rest - c0 * n0 - c1 * n1
-        matrix = jnp.where(rows == k, n0, jnp.where(rows == k + 1, n1, matrix))
-    return matrix
+    shape = (8, n)
+    tiles = [matrix[8 * i : 8 * i + 8, :] for i in range(n // 8)]
+    lane, sub = iota(shape, 1), iota(shape, 0)
+    for k in range(0, n, width):
+        at, s = k // 8, k % 8
+        cols, entries, rows = spread_block(tiles[at], k, width, shape)
+        inside = (lane >= k) & (lane < k + width)
+        rows = [
+            jnp.where(inside, jnp.where(lane == k + i, 1.0, 0.0), rows[i]) for i in range(width)
+        ]
+        q = block_inverse(entries)
+        new = []
+        for i in range(width):
+            value = q[i][0] * rows[0]
+            for j in range(1, width):
+                value = value + q[i][j] * rows[j]
+            new.append(value)
+        for i in range(n // 8):
+            old = tiles[i]
+            value = jnp.where(inside, 0.0, old)
+            if i != at or width < 8:
+                for j in range(width):
+                    c = cols[j] if i == at else jnp.broadcast_to(old[:, k + j : k + j + 1], shape)
+                    value = value - c * new[j]
+            if i == at:
+                for j in range(width):
+                    value = jnp.where(sub == s + j, new[j], value)
+            tiles[i] = value
+    return jnp.concatenate(tiles, axis=0)
+
+
+def inverse_factor(matrix, unit):
+    n = matrix.shape[0]
+    shape = (8, 2 * n)
+    work = jnp.concatenate([matrix, unit], axis=1)
+    tiles = [work[8 * i : 8 * i + 8, :] for i in range(n // 8)]
+    sub = iota(shape, 0)
+    for k in range(0, n, 4):
+        at, s = k // 8, k % 8
+        cols, e, rows = spread_block(tiles[at], k, 4, shape)
+        low, inv, new = {}, [], []
+        for i in range(4):
+            value, row = e[i, i], rows[i]
+            for m in range(i):
+                value = value - low[i, m] * low[i, m]
+                row = row - low[i, m] * new[m]
+            inv.append(1.0 / jnp.sqrt(value))
+            new.append(row * inv[i])
+            for j in range(i + 1, 4):
+                value = e[i, j]
+                for m in range(i):
+                    value = value - low[i, m] * low[j, m]
+                low[j, i] = value * inv[i]
+        back = [None] * 4
+        for i in (3, 2, 1, 0):
+            value = new[i]
+            for m in range(i + 1, 4):
+                value = value - low[m, i] * back[m]
+            back[i] = value * inv[i]
+        for i in range(at, n // 8):
+            old = tiles[i]
+            value = old
+            for j in range(4):
+                c = cols[j] if i == at else jnp.broadcast_to(old[:, k + j : k + j + 1], shape)
+                value = value - c * back[j]
+            if i == at:
+                value = jnp.where(sub >= s + 4, value, old)
+                for j in range(4):
+                    value = jnp.where(sub == s + j, new[j], value)
+            tiles[i] = value
+    return jnp.concatenate(tiles, axis=0)[:, n:]
 
 
 def split3(value):
@@ -208,7 +354,7 @@
     return high, mid, low
 
 
-def coarse_kernel(coarse_s, start_s, got, coef, gain, gram, uw, info, mat, hot):
+def coarse_kernel(coarse_s, start_s, got, coef, gain, gram, uw, info, mat, hot, upper, pivots):
     members, depth, _ = got.shape
     rows = 16
     half = rows
@@ -251,34 +397,49 @@
     inv_col = 1.0 / jnp.sqrt(agg_col)
     mat[...] = (jnp.where(same, (1.0 + spectral_shift) * agg, 0.0) - tiles) * inv_col * inv_row
 
-    block = min(LANE, nc)
-
-    def eliminate(step, _):
-        at = pl.multiple_of(step * block, block)
-        pivot = invert_dense(mat[pl.ds(at, block), pl.ds(at, block)])
-        inside_lane = (iota((1, nc), 1) >= at) & (iota((1, nc), 1) < at + block)
-        inside_row = (iota((nc, 1), 0) >= at) & (iota((nc, 1), 0) < at + block)
-        shifted = iota((block, nc), 0) + at == iota((block, nc), 1)
-        strip = jnp.where(inside_lane, jnp.where(shifted, 1.0, 0.0), mat[pl.ds(at, block), :])
-        new_rows = nn(pivot, strip, EXACT)
-        column = mat[:, pl.ds(at, block)]
-        column = jnp.where(inside_row, 0.0, column)
-        kept = jnp.where(inside_lane, 0.0, mat[...])
-        mat[...] = kept - nn(column, new_rows, EXACT)
-        mat[pl.ds(at, block), :] = new_rows
-        return 0
-
-    lax.fori_loop(0, nc // block, eliminate, 0)
-
-    ritz = nn(total[:, 3 * half : 4 * half], invert_dense(total[:, 0:half]), EXACT)
+    grams = total[:, 0:half]
+    square = iota((half, half), 0) == iota((half, half), 1)
+    diag_row = jnp.sum(jnp.where(square, grams, 0.0), axis=0, keepdims=True)
+    diag_col = jnp.sum(jnp.where(square, grams, 0.0), axis=1, keepdims=True)
+    unit_row, unit_col = 1.0 / jnp.sqrt(diag_row), 1.0 / jnp.sqrt(diag_col)
+    inverse = invert_dense(grams * unit_row * unit_col, 2, inverse2) * unit_row * unit_col
+    ritz = nn(total[:, 3 * half : 4 * half], inverse, EXACT)
     coef[...] = ritz
-    unit = jnp.where(iota((half, half), 0) == iota((half, half), 1), 1.0, 0.0)
-    combine = jnp.concatenate([-ritz, unit], axis=1)
+    combine = jnp.concatenate([-ritz, jnp.where(square, 1.0, 0.0)], axis=1)
     rhs = jnp.zeros((half, nc), F32)
     for g in range(GROUPS):
         block_rhs = nt(combine, uw[:, g * width : (g + 1) * width], EXACT)
         rhs = rhs + nn(block_rhs, hot[g], EXACT)
-    error = nn(rhs * inv_row, mat[...], EXACT)
+    rhs = rhs * inv_row
+
+    block = min(LANE, nc)
+    steps = nc // block
+
+    def eliminate(step, _):
+        at = pl.multiple_of(step * block, block)
+        pivot = invert_dense(mat[pl.ds(at, block), pl.ds(at, block)], 8, inverse8)
+        pivots[pl.ds(at, block), :] = pivot
+        for j in range(steps - 1):
+
+            @pl.when(step == j)
+            def _():
+                lo, hi = j * block, (j + 1) * block
+                strip = nn(pivot, mat[lo:hi, hi:], EXACT)
+                upper[lo:hi, hi:] = strip
+                mat[hi:, hi:] = mat[hi:, hi:] - nn(mat[hi:, lo:hi], strip, EXACT)
+
+        return 0
+
+    lax.fori_loop(0, steps, eliminate, 0)
+    for j in range(steps - 1):
+        lo, hi = j * block, (j + 1) * block
+        rest = rhs[:, hi:] - nn(rhs[:, lo:hi], upper[lo:hi, hi:], EXACT)
+        rhs = jnp.concatenate([rhs[:, :hi], rest], axis=1)
+    error = nn(rhs[:, nc - block :], pivots[nc - block :, :], EXACT)
+    for j in reversed(range(steps - 1)):
+        lo, hi = j * block, (j + 1) * block
+        head = nn(rhs[:, lo:hi], pivots[lo:hi, :], EXACT) - nt(error, upper[lo:hi, hi:], EXACT)
+        error = jnp.concatenate([head, error], axis=1)
     lifted = error * inv_row
     wide = iota((1, nc), 1)
     picks = []
@@ -290,22 +451,21 @@
 
 
 def correct_kernel(
-    window_s, self_t, link_t, zc, zl, zh, ic, il, ih, nc, nl, nh, coef, gain,
+    window_s, self_t, link_t, fc, fl, fh, ic, il, ih, coef, gain,
     residual, corrected, scaled, win, second,
 ):
     count, size = self_t.shape[0], self_t.shape[1]
-    half = zc.shape[0] // 2
+    half = ic.shape[0]
+    both = 2 * half
     ritz = coef[...]
     gains = gain[...]
-    for part, (z, img, nodes) in enumerate(((zl, il, nl), (zc, ic, nc), (zh, ih, nh))):
-        res = img[:half, :] - nn(ritz, z[:half, :], EXACT)
+    for part, (f, img) in enumerate(((fl, il), (fc, ic), (fh, ih))):
+        res = img[...] - nn(ritz, f[:half, :], EXACT)
         if part == 1:
             residual[...] = res
         for b in range(count):
             span = slice(b * size, (b + 1) * size)
-            root = jnp.sqrt(safe(nodes[b : b + 1, :]))
-            shift = nodes[count + b : count + b + 1, :]
-            shift = jnp.where(shift == 0.0, 1.0, shift)
+            root, shift = node_scales(f, both, span)
             j = part * count + b
             field = damping * res[:, span] / shift + root * gains[:, j : j + 1]
             win[j] = (field / root).astype(BF16)
@@ -313,8 +473,7 @@
                 second[:, span] = field
     for b in range(count):
         span = slice(b * size, (b + 1) * size)
-        root = jnp.sqrt(nc[b : b + 1, :])
-        shift = nc[count + b : count + b + 1, :]
+        root, shift = node_scales(fc, both, span)
         acc = apply_tiles(window_s, self_t, link_t, win, b, count)
         field = second[:, span]
         after = field - acc / root + spectral_shift * field
@@ -323,7 +482,7 @@
         scaled[:, span] = (field / root).astype(BF16)
 
 
-def search_kernel(window_s, self_t, link_t, w, sc, sl, sh, nc, z, img, out, win, image_w):
+def search_kernel(window_s, self_t, link_t, w, sc, sl, sh, fc, ix, ip, out, win, image_w):
     count, size = self_t.shape[0], self_t.shape[1]
     half = w.shape[0]
     for part, s in enumerate((sl, sc, sh)):
@@ -332,15 +491,16 @@
     for b in range(count):
         span = slice(b * size, (b + 1) * size)
         acc = apply_tiles(window_s, self_t, link_t, win, b, count)
-        image_w[:, span] = w[:, span] - acc / jnp.sqrt(nc[b : b + 1, :])
+        image_w[:, span] = w[:, span] - acc / jnp.sqrt(fc[2 * half : 2 * half + 1, span])
     field = w[...]
     field_image = image_w[...]
-    zz = z[...]
+    zz = fc[: 2 * half, :]
+    images = jnp.concatenate([ix[...], ip[...]], axis=0)
     value = jnp.concatenate(
         [
             nt(field, zz, EXACT),
             nt(field, field, EXACT),
-            0.5 * (nt(field, img[...], EXACT) + nt(field_image, zz, EXACT)),
+            0.5 * (nt(field, images, EXACT) + nt(field_image, zz, EXACT)),
             nt(field, field_image, EXACT),
             jnp.zeros((half, LANE - 6 * half), F32),
         ],
@@ -380,14 +540,7 @@
     gram_a = whole(
         piece(old, 3), piece(old, 4), piece(old, 5), piece(new, 3), piece(new, 5), piece(new, 4)
     )
-    work = jnp.concatenate([gram_b, unit], axis=1)
-    rows = iota((n, 1), 0)
-    for k in range(n):
-        pivot = work[k : k + 1, :]
-        factor = work[:, k : k + 1] / pivot[:, k : k + 1]
-        work = work - jnp.where(rows > k, factor, 0.0) * pivot
-    diag = jnp.sum(jnp.where(unit > 0.0, work[:, :n], 0.0), axis=1, keepdims=True)
-    inverse = work[:, n:] / jnp.sqrt(diag)
+    inverse = inverse_factor(gram_b, unit)
     out[...] = nt(nn(inverse, gram_a, EXACT), inverse, EXACT)
 
 
@@ -414,30 +567,30 @@
     links_s = lax.dynamic_slice_in_dim(links, start, count, 0)
     window_s = links_s - (start - count)
 
+    both = jnp.broadcast_to(
+        jnp.concatenate([vectors, directions], axis=0)[None], (vec, 2 * mine, slab)
+    )
+    both = lax.all_to_all(both, "vec", 0, 0)
     nodes, col, info = run(
         prep_kernel,
         (links_s, coarse_row, start_s, self_tiles, link_tiles),
-        (arr((2 * count, size)), arr((4, count, size)), arr((count, LANE))),
+        (arr((8, slab)), arr((4, count, size)), arr((count, LANE))),
         smem=3,
-    )
-    both = jnp.broadcast_to(
-        jnp.concatenate([vectors, directions], axis=0)[None], (vec, 2 * mine, slab)
-    )
-    both = lax.all_to_all(both, "vec", 0, 0)
-    zc = jnp.swapaxes(both.reshape(vec, 2, mine, slab), 0, 1).reshape(2 * k, slab)
-    nl, nh = halo(nodes)
-    zl, zh = halo(zc)
-    image, gram = run(
+        work=1 << 30,
+    )
+    fc = run(pack_kernel, (both, nodes), arr((2 * k + 8, slab)))
+    fl, fh = halo(fc)
+    ic, ip, gram = run(
         image_kernel,
-        (window_s, self_tiles, link_tiles, zc, zl, zh, nodes, nl, nh),
-        (arr((2 * k, slab)), arr((k, LANE))),
+        (window_s, self_tiles, link_tiles, fc, fl, fh),
+        (arr((k, slab)), arr((k, slab)), arr((k, LANE))),
         scratch=(pltpu.VMEM((3 * count, 2 * k, size), BF16),),
         smem=1,
     )
-    il, ih = halo(image[:k])
+    il, ih = halo(ic)
     sent = run(
         restrict_kernel,
-        (window_s, zc, zl, zh, image, il, ih, nodes, nl, nh, col, gram, info),
+        (window_s, fc, fl, fh, ic, il, ih, col, gram, info),
         arr((n_one, 2 * count, LANE)),
         scratch=(
             pltpu.VMEM((3 * count, 2 * k, size), F32),
@@ -466,15 +619,14 @@
             pltpu.VMEM((blocks, LANE), F32),
             pltpu.VMEM((coarse_count, coarse_count), F32),
             pltpu.VMEM((GROUPS, blocks, coarse_count), F32),
+            pltpu.VMEM((coarse_count, coarse_count), F32),
+            pltpu.VMEM((coarse_count, min(LANE, coarse_count)), F32),
         ),
         smem=2,
     )
     residual, corrected, scaled = run(
         correct_kernel,
-        (
-            window_s, self_tiles, link_tiles, zc, zl, zh, image, il, ih,
-            nodes, nl, nh, coef, gain,
-        ),
+        (window_s, self_tiles, link_tiles, fc, fl, fh, ic, il, ih, coef, gain),
         (arr((k, slab)), arr((k, slab)), arr((k, slab), BF16)),
         scratch=(pltpu.VMEM((3 * count, k, size), BF16), pltpu.VMEM((k, slab), F32)),
         smem=1,
@@ -482,7 +634,7 @@
     sl, sh = halo(scaled)
     sent = run(
         search_kernel,
-        (window_s, self_tiles, link_tiles, corrected, scaled, sl, sh, nodes, zc, image),
+        (window_s, self_tiles, link_tiles, corrected, scaled, sl, sh, fc, ic, ip),
         arr((n_one, k, LANE)),
         scratch=(pltpu.VMEM((3 * count, k, size), BF16), pltpu.VMEM((k, slab), F32)),
         smem=1,

time: 230 us -> 175 us (0.76)
  Pallas kernels: 106 us -> 62 us
  starting transfers between devices: 43.2 us -> 37.7 us
  blocking collectives: 45.7 us -> 42.3 us
    pallas_call x9 -> x10, Pallas kernels: 106 us -> 62 us  [run(): pl.pallas_call(kernel, in_specs=in_specs, out_specs=specs[0] if single el...]
    all_to_all x1, waiting for transfers between devices: 5.53 us -> 0.67 us  [body(): both = lax.all_to_all(both, 'vec', 0, 0)]
    all_to_all x1, blocking collectives: 27.8 us -> 24.4 us  [body(): got = lax.all_to_all(sent, stage_one, 0, 0)]
    ppermute x4 -> x3, waiting for transfers between devices: 3.07 us -> 6.42 us  [halo(): lax.ppermute(a, row_axes, forward)]
    ppermute x4 -> x3, starting transfers between devices: 12.5 us -> 9.44 us  [halo(): lax.ppermute(a, row_axes, forward)]
    ppermute x4 -> x3, starting transfers between devices: 15.1 us -> 12.6 us  [halo(): lax.ppermute(a, row_axes, backward)]
    unnamed x27 -> x23, local copies, waits for them, and re-layouts: 4.61 us -> 4.64 us
  transfers between devices with their start and end apart: 11 -> 9, of which waited for: 8 -> 8; matrix products, arithmetic and copies ran while one was open for 1% -> 2% of each run, Pallas kernels for 2% -> 2%
where the time goes in v2:
time: 175 us; the launch traced here: 174 us
  Pallas kernels  62 us (35%)
  blocking collectives  42.3 us (24%)
  starting transfers between devices  37.7 us (22%)
  waiting for transfers between devices  23.1 us (13%)
  local copies, waits for them, and re-layouts  6.94 us (4%)
    pallas_call x10, Pallas kernels, run(): pl.pallas_call(kernel, in_specs=in_specs, out_specs=specs[0] if single el...  62 us
    all_to_all x1, blocking collectives, body(): got = lax.all_to_all(sent, stage_one, 0, 0)  24.4 us
    all_to_all x1, blocking collectives, body(): got = lax.all_to_all(sent, 'y', 0, 0)  17.9 us
    ppermute x3, starting transfers between devices, halo(): lax.ppermute(a, row_axes, backward)  12.6 us
    ppermute x3, starting transfers between devices, halo(): lax.ppermute(a, row_axes, forward)  9.44 us
    all_to_all x1, waiting for transfers between devices, body(): got = lax.all_to_all(sent, stage_one, 0, 0)  8.89 us
    all_to_all x1, starting transfers between devices, body(): got = lax.all_to_all(sent, stage_one, 0, 0)  7.42 us
    ppermute x3, waiting for transfers between devices, halo(): lax.ppermute(a, row_axes, forward)  6.42 us
  transfers between devices with their start and end apart: 9, of which 8 were waited for; matrix products, arithmetic and copies ran while one was open for 2% of the time, Pallas kernels for 2%

profile of v2, /device:TPU:1, one launch (start us, length us, event | category | flops | bytes accessed | tf_op | source)
XLA Modules:
  0.0 174.1 jit_solution(10715692012114205839)
XLA Ops:
  0.6 0.8 pad_maximum_fusion
  1.4 0.7 broadcast_in_dim.2
  2.2 4.8 %all-to-all-start = ((f32[4,8,2048]{2,1,0:T(8,128)}), f32[4,8,2048]{2,1,0:T(8,128)S(1)}, u32[]{:S(2)}, u32[]{:S(2)}) async-start(f32[4,8,2048]{2,1,0:T(8,128)} %broadcast_in_dim.2), calls=%async_computation | async-start | bytes 524288 | tf_op jit(solution)/shard_map/all_to_all | solution.py:573
  7.7 4.1 %shard_map.85 = (f32[8,2048]{1,0:T(8,128)}, f32[4,8,256]{2,1,0:T(8,128)}, f32[8,128]{1,0:T(8,128)}) custom-call(s32[8,3]{1,0:T(8,128)} %copy.10.links_s, s32[1024]{0:T(1024)} %coarse_s.3, s32[1]{0:T(128)} %bitcast.start_s, bf16[8,256,256]{2,1,0:T(8,128)(2,1)} %self_t.7, bf16[8,3,256,256]{3,2,1,0:T(8,128)(2,1)} %link_t.7), custom_call_target="tpu_custom_call" | custom-call | flops 1073741824 | bytes 4198500 | tf_op jit(solution)/shard_map/pallas_call | solution.py:48
  12.5 0.7 copy-done.3
  13.2 1.7 shard_map.86.fc
  15.0 8.4 %collective-permute-start.1 = (f32[40,2048]{1,0:T(8,128)}, f32[40,2048]{1,0:T(8,128)S(1)}, u32[]{:S(2)}, u32[]{:S(2)}) collective-permute-start(f32[40,2048]{1,0:T(8,128)} %shard_map.86.fc), channel_id=1, source_target_pairs={{4,0},{8,4},{12,8},{16,12},{20,16},{24,20},{28,24},{32,28},{36,32}... | collective-permute-start | bytes 983048 | tf_op jit(solution)/shard_map/ppermute | solution.py:563
  23.4 1.9 %collective-permute-start = (f32[40,2048]{1,0:T(8,128)}, f32[40,2048]{1,0:T(8,128)S(1)}, u32[]{:S(2)}, u32[]{:S(2)}) collective-permute-start(f32[40,2048]{1,0:T(8,128)} %shard_map.86.fc), channel_id=1, source_target_pairs={{0,4},{4,8},{8,12},{12,16},{16,20},{20,24},{24,28},{28,32},{32,36}... | collective-permute-start | bytes 983048 | tf_op jit(solution)/shard_map/ppermute | solution.py:563
  25.9 3.7 %collective-permute-done.fl = f32[40,2048]{1,0:T(8,128)S(1)} collective-permute-done((f32[40,2048]{1,0:T(8,128)}, f32[40,2048]{1,0:T(8,128)S(1)}, u32[]{:S(2)}, u32[]{:S(2)}) %collective-permute-start) | collective-permute-done | bytes 327712 | tf_op jit(solution)/shard_map/ppermute | solution.py:563
  29.7 0.7 copy-done.2
  30.4 5.3 %shard_map.87 = (f32[16,2048]{1,0:T(8,128)}, f32[16,2048]{1,0:T(8,128)}, f32[16,128]{1,0:T(8,128)}) custom-call(s32[8,3]{1,0:T(8,128)} %broadcast_subtract_fusion.window_s, bf16[8,256,256]{2,1,0:T(8,128)(2,1)} %self_t.7, bf16[8,3,256,256]{3,2,1,0:T(8,128)(2,1)} %link_t.7, f32[40,2048]{1,0:T(8,128)} %shard_map.86.fc, f32[40,2048]{1,0:T(8,128)} %copy-done.2, ...), custom_call_target="tpu_custom_call" | custom-call | bytes 5177440 | tf_op jit(solution)/shard_map/pallas_call | solution.py:48
  35.7 1.9 %collective-permute-start.3 = (f32[16,2048]{1,0:T(8,128)}, f32[16,2048]{1,0:T(8,128)S(1)}, u32[]{:S(2)}, u32[]{:S(2)}) collective-permute-start(f32[16,2048]{1,0:T(8,128)} %get-tuple-element.16.ic.ix), channel_id=1, source_target_pairs={{4,0},{8,4},{12,8},{16,12},{20,16},{24,20},{28,24},{32,28},{36,32}... | collective-permute-start | bytes 393224 | tf_op jit(solution)/shard_map/ppermute | solution.py:563
  37.6 4.3 %collective-permute-start.2 = (f32[16,2048]{1,0:T(8,128)}, f32[16,2048]{1,0:T(8,128)S(1)}, u32[]{:S(2)}, u32[]{:S(2)}) collective-permute-start(f32[16,2048]{1,0:T(8,128)} %get-tuple-element.16.ic.ix), channel_id=1, source_target_pairs={{0,4},{4,8},{8,12},{12,16},{16,20},{20,24},{24,28},{28,32},{32,36}... | collective-permute-start | bytes 393224 | tf_op jit(solution)/shard_map/ppermute | solution.py:563
  41.9 0.9 collective-permute-done.3.ih
  42.8 1.3 collective-permute-done.2.il
  44.8 2.6 %shard_map.88 = f32[16,16,128]{2,1,0:T(8,128)} custom-call(s32[8,3]{1,0:T(8,128)} %broadcast_subtract_fusion.window_s, f32[40,2048]{1,0:T(8,128)} %shard_map.86.fc, f32[40,2048]{1,0:T(8,128)} %copy-done.2, f32[40,2048]{1,0:T(8,128)} %copy-done.1, f32[16,2048]{1,0:T(8,128)} %get-tuple-element.16.ic.ix, f32[16,2048]{1,0:T(8,128)} %copy-done.5, ...), custom_call_target="tpu_custom_call" | custom-call | bytes 1421408 | tf_op jit(solution)/shard_map/pallas_call | solution.py:48
  47.4 24.4 %all_to_all.25.got = f32[16,16,128]{2,1,0:T(8,128)} all-to-all(f32[16,16,128]{2,1,0:T(8,128)} %shard_map.88), channel_id=1, replica_groups=mesh['z'=8,'y'=8,'core'=2,'vec'=4] {'z','core'}, dimensions={0} | all-to-all | bytes 262144 | tf_op jit(solution)/shard_map/all_to_all | solution.py:602
  71.8 1.8 %shard_map.89 = f32[8,80,128]{2,1,0:T(8,128)} custom-call(f32[16,16,128]{2,1,0:T(8,128)} %all_to_all.25.got), custom_call_target="tpu_custom_call" | custom-call | bytes 131072 | tf_op jit(solution)/shard_map/pallas_call | solution.py:48
  73.5 17.9 %all_to_all.26.got = f32[8,80,128]{2,1,0:T(8,128)} all-to-all(f32[8,80,128]{2,1,0:T(8,128)} %shard_map.89), channel_id=1, replica_groups=mesh['z'=8,'y'=8,'core'=2,'vec'=4] {'y'}, dimensions={0} | all-to-all | bytes 655360 | tf_op jit(solution)/shard_map/all_to_all | solution.py:610
  91.4 29.7 %shard_map.90 = (f32[16,16]{1,0:T(8,128)}, f32[16,32]{1,0:T(8,128)}, f32[16,128]{1,0:T(8,128)}) custom-call(s32[1024]{0:T(1024)} %coarse_s.3, s32[1]{0:T(128)} %bitcast.start_s, f32[8,80,128]{2,1,0:T(8,128)} %all_to_all.26.got), custom_call_target="tpu_custom_call" | custom-call | bytes 331780 | tf_op jit(solution)/shard_map/pallas_call | solution.py:48
  121.1 5.0 %shard_map.91 = (f32[16,2048]{1,0:T(8,128)}, f32[16,2048]{1,0:T(8,128)}, bf16[16,2048]{1,0:T(8,128)(2,1)}) custom-call(s32[8,3]{1,0:T(8,128)} %broadcast_subtract_fusion.window_s, bf16[8,256,256]{2,1,0:T(8,128)(2,1)} %self_t.7, bf16[8,3,256,256]{3,2,1,0:T(8,128)(2,1)} %link_t.7, f32[40,2048]{1,0:T(8,128)} %shard_map.86.fc, f32[40,2048]{1,0:T(8,128)} %copy-done.2, ...), custom_call_target="tpu_custom_call" | custom-call | bytes 5573728 | tf_op jit(solution)/shard_map/pallas_call | solution.py:48
  126.1 2.3 %collective-permute-start.5 = (bf16[16,2048]{1,0:T(8,128)(2,1)}, bf16[16,2048]{1,0:T(8,128)(2,1)S(1)}, u32[]{:S(2)}, u32[]{:S(2)}) collective-permute-start(bf16[16,2048]{1,0:T(8,128)(2,1)} %get-tuple-element.24.sc), channel_id=1, source_target_pairs={{4,0},{8,4},{12,8},{16,12},{20,16},{24,20},{28,24},{32,28},{36,32}... | collective-permute-start | bytes 196616 | tf_op jit(solution)/shard_map/ppermute | solution.py:563
  128.4 3.2 %collective-permute-start.4 = (bf16[16,2048]{1,0:T(8,128)(2,1)}, bf16[16,2048]{1,0:T(8,128)(2,1)S(1)}, u32[]{:S(2)}, u32[]{:S(2)}) collective-permute-start(bf16[16,2048]{1,0:T(8,128)(2,1)} %get-tuple-element.24.sc), channel_id=1, source_target_pairs={{0,4},{4,8},{8,12},{12,16},{16,20},{20,24},{24,28},{28,32},{32,36}... | collective-permute-start | bytes 196616 | tf_op jit(solution)/shard_map/ppermute | solution.py:563
  131.9 1.4 collective-permute-done.4.sl
  133.9 5.4 %shard_map.92 = f32[16,16,128]{2,1,0:T(8,128)} custom-call(s32[8,3]{1,0:T(8,128)} %broadcast_subtract_fusion.window_s, bf16[8,256,256]{2,1,0:T(8,128)(2,1)} %self_t.7, bf16[8,3,256,256]{3,2,1,0:T(8,128)(2,1)} %link_t.7, f32[16,2048]{1,0:T(8,128)} %get-tuple-element.23.w, bf16[16,2048]{1,0:T(8,128)(2,1)} %get-tuple-element.24.sc, bf16[16,2048]{1,0:T(8,128)(2,1)} %copy-done.9, ...), custom_call_target="tpu_custom_call" | custom-call | bytes 5111904 | tf_op jit(solution)/shard_map/pallas_call | solution.py:48
  139.3 7.4 %all-to-all-start.3 = ((f32[16,16,128]{2,1,0:T(8,128)}), f32[16,16,128]{2,1,0:T(8,128)S(1)}, u32[]{:S(2)}, u32[]{:S(2)}) async-start(f32[16,16,128]{2,1,0:T(8,128)} %shard_map.92), calls=%async_computation.3 | async-start | bytes 262144 | tf_op jit(solution)/shard_map/all_to_all | solution.py:642
  146.7 8.9 %all-to-all-done.3.got = f32[16,16,128]{2,1,0:T(8,128)S(1)} async-done(((f32[16,16,128]{2,1,0:T(8,128)}), f32[16,16,128]{2,1,0:T(8,128)S(1)}, u32[]{:S(2)}, u32[]{:S(2)}) %all-to-all-start.3) | async-done | bytes 131104 | tf_op jit(solution)/shard_map/all_to_all | solution.py:642
  156.2 1.5 shard_map.93
  157.8 3.3 %all-to-all-start.4 = ((f32[8,16,128]{2,1,0:T(8,128)}), f32[8,16,128]{2,1,0:T(8,128)S(1)}, u32[]{:S(2)}, u32[]{:S(2)}) async-start(f32[8,16,128]{2,1,0:T(8,128)} %shard_map.93), calls=%async_computation.4 | async-start | bytes 131072 | tf_op jit(solution)/shard_map/all_to_all | solution.py:644
  161.1 1.5 constant_dynamic-slice_fusion
  162.7 6.0 %all-to-all-done.4.got = f32[8,16,128]{2,1,0:T(8,128)S(1)} async-done(((f32[8,16,128]{2,1,0:T(8,128)}), f32[8,16,128]{2,1,0:T(8,128)S(1)}, u32[]{:S(2)}, u32[]{:S(2)}) %all-to-all-start.4) | async-done | bytes 65568 | tf_op jit(solution)/shard_map/all_to_all | solution.py:644
  169.2 4.9 %shard_map.94 = f32[48,48]{1,0:T(8,128)} custom-call(f32[8,16,128]{2,1,0:T(8,128)} %copy-done.7, f32[16,128]{1,0:T(8,128)} %get-tuple-element.26.gram), custom_call_target="tpu_custom_call" | custom-call | bytes 73728 | tf_op jit(solution)/shard_map/pallas_call | solution.py:48
  (26 shorter events, 4.8 us)
Async XLA Ops:
  0.6 6.4 %copy-start = (s32[1024,3]{0,1:T(4,128)S(1)}, s32[1024,3]{0,1:T(4,128)}, u32[]{:S(2)}) copy-start(s32[1024,3]{0,1:T(4,128)} %param.8) | copy-start | bytes 36868
  2.2 10.4 %all-to-all-start = ((f32[4,8,2048]{2,1,0:T(8,128)}), f32[4,8,2048]{2,1,0:T(8,128)S(1)}, u32[]{:S(2)}, u32[]{:S(2)}) async-start(f32[4,8,2048]{2,1,0:T(8,128)} %broadcast_in_dim.2), calls=%async_computation | async-start | bytes 524288 | tf_op jit(solution)/shard_map/all_to_all | solution.py:573
  7.7 17.6 %copy-start.10 = (s32[8,3]{1,0:T(8,128)S(1)}, s32[8,3]{1,0:T(8,128)}, u32[]{:S(2)}) copy-start(s32[8,3]{1,0:T(8,128)} %copy.10.links_s) | copy-start | bytes 292
  12.5 0.7 copy-start.3
  15.0 11.0 %collective-permute-start.1 = (f32[40,2048]{1,0:T(8,128)}, f32[40,2048]{1,0:T(8,128)S(1)}, u32[]{:S(2)}, u32[]{:S(2)}) collective-permute-start(f32[40,2048]{1,0:T(8,128)} %shard_map.86.fc), channel_id=1, source_target_pairs={{4,0},{8,4},{12,8},{16,12},{20,16},{24,20},{28,24},{32,28},{36,32}... | collective-permute-start | bytes 983048 | tf_op jit(solution)/shard_map/ppermute | solution.py:563
  23.4 6.2 %collective-permute-start = (f32[40,2048]{1,0:T(8,128)}, f32[40,2048]{1,0:T(8,128)S(1)}, u32[]{:S(2)}, u32[]{:S(2)}) collective-permute-start(f32[40,2048]{1,0:T(8,128)} %shard_map.86.fc), channel_id=1, source_target_pairs={{0,4},{4,8},{8,12},{12,16},{16,20},{20,24},{24,28},{28,32},{32,36}... | collective-permute-start | bytes 983048 | tf_op jit(solution)/shard_map/ppermute | solution.py:563
  25.9 3.7 %copy-start.1 = (f32[40,2048]{1,0:T(8,128)}, f32[40,2048]{1,0:T(8,128)S(1)}, u32[]{:S(2)}) copy-start(f32[40,2048]{1,0:T(8,128)S(1)} %collective-permute-done.1.fh) | copy-start | bytes 983044
  29.6 0.7 copy-start.2
  35.7 7.1 %collective-permute-start.3 = (f32[16,2048]{1,0:T(8,128)}, f32[16,2048]{1,0:T(8,128)S(1)}, u32[]{:S(2)}, u32[]{:S(2)}) collective-permute-start(f32[16,2048]{1,0:T(8,128)} %get-tuple-element.16.ic.ix), channel_id=1, source_target_pairs={{4,0},{8,4},{12,8},{16,12},{20,16},{24,20},{28,24},{32,28},{36,32}... | collective-permute-start | bytes 393224 | tf_op jit(solution)/shard_map/ppermute | solution.py:563
  37.6 6.5 %collective-permute-start.2 = (f32[16,2048]{1,0:T(8,128)}, f32[16,2048]{1,0:T(8,128)S(1)}, u32[]{:S(2)}, u32[]{:S(2)}) collective-permute-start(f32[16,2048]{1,0:T(8,128)} %get-tuple-element.16.ic.ix), channel_id=1, source_target_pairs={{0,4},{4,8},{8,12},{12,16},{16,20},{20,24},{24,28},{28,32},{32,36}... | collective-permute-start | bytes 393224 | tf_op jit(solution)/shard_map/ppermute | solution.py:563
  42.8 1.3 copy-start.4
  44.1 0.6 copy-start.5
  126.1 5.8 %collective-permute-start.5 = (bf16[16,2048]{1,0:T(8,128)(2,1)}, bf16[16,2048]{1,0:T(8,128)(2,1)S(1)}, u32[]{:S(2)}, u32[]{:S(2)}) collective-permute-start(bf16[16,2048]{1,0:T(8,128)(2,1)} %get-tuple-element.24.sc), channel_id=1, source_target_pairs={{4,0},{8,4},{12,8},{16,12},{20,16},{24,20},{28,24},{32,28},{36,32}... | collective-permute-start | bytes 196616 | tf_op jit(solution)/shard_map/ppermute | solution.py:563
  128.4 4.9 %collective-permute-start.4 = (bf16[16,2048]{1,0:T(8,128)(2,1)}, bf16[16,2048]{1,0:T(8,128)(2,1)S(1)}, u32[]{:S(2)}, u32[]{:S(2)}) collective-permute-start(bf16[16,2048]{1,0:T(8,128)(2,1)} %get-tuple-element.24.sc), channel_id=1, source_target_pairs={{0,4},{4,8},{8,12},{12,16},{16,20},{20,24},{24,28},{28,32},{32,36}... | collective-permute-start | bytes 196616 | tf_op jit(solution)/shard_map/ppermute | solution.py:563
  131.9 1.4 copy-start.8
  133.3 0.6 copy-start.9
  139.3 16.3 %all-to-all-start.3 = ((f32[16,16,128]{2,1,0:T(8,128)}), f32[16,16,128]{2,1,0:T(8,128)S(1)}, u32[]{:S(2)}, u32[]{:S(2)}) async-start(f32[16,16,128]{2,1,0:T(8,128)} %shard_map.92), calls=%async_computation.3 | async-start | bytes 262144 | tf_op jit(solution)/shard_map/all_to_all | solution.py:642
  155.6 0.6 copy-start.6
  157.8 10.8 %all-to-all-start.4 = ((f32[8,16,128]{2,1,0:T(8,128)}), f32[8,16,128]{2,1,0:T(8,128)S(1)}, u32[]{:S(2)}, u32[]{:S(2)}) async-start(f32[8,16,128]{2,1,0:T(8,128)} %shard_map.93), calls=%async_computation.4 | async-start | bytes 131072 | tf_op jit(solution)/shard_map/all_to_all | solution.py:644
  168.6 0.6 copy-start.7

commit v3 on v2

--- a/solution.py
+++ b/solution.py
@@ -51,6 +51,7 @@
         out_specs=specs[0] if single else specs,
         out_shape=shapes[0] if single else shapes,
         scratch_shapes=list(scratch),
+        compiler_params=pltpu.CompilerParams(vmem_limit_bytes=16 << 20),
         cost_estimate=pl.CostEstimate(
             flops=work, bytes_accessed=sum(a.size * a.dtype.itemsize for a in inputs), transcendentals=0
         ),
@@ -451,8 +452,8 @@
 
 
 def correct_kernel(
-    window_s, self_t, link_t, fc, fl, fh, ic, il, ih, coef, gain,
-    residual, corrected, scaled, win, second,
+    window_s, start_s, self_t, link_t, fc, fl, fh, ic, il, ih, coef, gain,
+    my_residual, my_corrected, corrected, scaled, win, second, residual,
 ):
     count, size = self_t.shape[0], self_t.shape[1]
     half = ic.shape[0]
@@ -480,6 +481,11 @@
         field = field + damping * (residual[:, span] - after) / shift
         corrected[:, span] = field
         scaled[:, span] = (field / root).astype(BF16)
+    mine = my_residual.shape[0]
+    pick = iota((mine, half), 1) == iota((mine, half), 0) + start_s[1] * mine
+    pick = jnp.where(pick, 1.0, 0.0)
+    my_residual[...] = nn(pick, residual[...], EXACT)
+    my_corrected[...] = nn(pick, corrected[...], EXACT)
 
 
 def search_kernel(window_s, self_t, link_t, w, sc, sl, sh, fc, ix, ip, out, win, image_w):
@@ -563,7 +569,7 @@
         return lax.ppermute(a, row_axes, forward), lax.ppermute(a, row_axes, backward)
 
     start = row_index * count
-    start_s = start.reshape(1).astype(jnp.int32)
+    start_s = jnp.stack([start, lax.axis_index("vec")]).astype(jnp.int32)
     links_s = lax.dynamic_slice_in_dim(links, start, count, 0)
     window_s = links_s - (start - count)
 
@@ -624,12 +630,16 @@
         ),
         smem=2,
     )
-    residual, corrected, scaled = run(
+    residual, my_corrected, corrected, scaled = run(
         correct_kernel,
-        (window_s, self_tiles, link_tiles, fc, fl, fh, ic, il, ih, coef, gain),
-        (arr((k, slab)), arr((k, slab)), arr((k, slab), BF16)),
-        scratch=(pltpu.VMEM((3 * count, k, size), BF16), pltpu.VMEM((k, slab), F32)),
-        smem=1,
+        (window_s, start_s, self_tiles, link_tiles, fc, fl, fh, ic, il, ih, coef, gain),
+        (arr((mine, slab)), arr((mine, slab)), arr((k, slab)), arr((k, slab), BF16)),
+        scratch=(
+            pltpu.VMEM((3 * count, k, size), BF16),
+            pltpu.VMEM((k, slab), F32),
+            pltpu.VMEM((k, slab), F32),
+        ),
+        smem=2,
     )
     sl, sh = halo(scaled)
     sent = run(
@@ -643,12 +653,7 @@
     sent = run(add_kernel, (got,), arr((n_two, k, LANE)))
     got = lax.all_to_all(sent, "y", 0, 0)
     projected = run(project_kernel, (got, gram), arr((3 * k, 3 * k)))
-    at = lax.axis_index("vec") * mine
-    return (
-        lax.dynamic_slice_in_dim(residual, at, mine, 0),
-        lax.dynamic_slice_in_dim(corrected, at, mine, 0),
-        projected,
-    )
+    return residual, my_corrected, projected
 
 
 def row_split(rows):

time: 175 us -> 159 us (0.909)
  blocking collectives: 42.3 us -> 67.7 us
  waiting for transfers between devices: 23.1 us -> 6.51 us
  Pallas kernels: 62 us -> 46.6 us
  starting transfers between devices: 37.7 us -> 26.1 us
  local copies, waits for them, and re-layouts: 6.94 us -> 9.4 us
    all_to_all x1 -> x2, blocking collectives: 24.4 us -> 41.5 us  [body(): got = lax.all_to_all(sent, stage_one, 0, 0)]
    pallas_call x10, Pallas kernels: 62 us -> 46.6 us  [run(): pl.pallas_call(kernel, in_specs=in_specs, out_specs=specs[0] if single el...]
    all_to_all x2 -> x0, waiting for transfers between devices: 14.9 us -> none  [the longest x1 8.89 us: body(): got = lax.all_to_all(sent, stage_one, 0, 0)]
    all_to_all x2 -> x0, starting transfers between devices: 10.8 us -> none  [the longest x1 7.42 us: body(): got = lax.all_to_all(sent, stage_one, 0, 0)]
    all_to_all x1 -> x2, blocking collectives: 17.9 us -> 26.1 us  [body(): got = lax.all_to_all(sent, 'y', 0, 0)]
    unnamed x23 -> x35, local copies, waits for them, and re-layouts: 4.64 us -> 8.6 us
  transfers between devices with their start and end apart: 9 -> 7, of which waited for: 8 -> 4; matrix products, arithmetic and copies ran while one was open for 2% -> 1% of each run, Pallas kernels for 2% -> 1%
where the time goes in v3:
time: 159 us
  blocking collectives  67.7 us (43%)
  Pallas kernels  46.6 us (29%)
  starting transfers between devices  26.1 us (16%)
  local copies, waits for them, and re-layouts  9.4 us (6%)
  waiting for transfers between devices  6.51 us (4%)
    pallas_call x10, Pallas kernels, run(): pl.pallas_call(kernel, in_specs=in_specs, out_specs=specs[0] if single el...  46.6 us
    all_to_all x2, blocking collectives, body(): got = lax.all_to_all(sent, stage_one, 0, 0)  41.5 us
    all_to_all x2, blocking collectives, body(): got = lax.all_to_all(sent, 'y', 0, 0)  26.1 us
    ppermute x3, starting transfers between devices, halo(): lax.ppermute(a, row_axes, backward)  11.6 us
    ppermute x3, starting transfers between devices, halo(): lax.ppermute(a, row_axes, forward)  9.62 us
    unnamed x35, local copies, waits for them, and re-layouts  8.6 us
    ppermute x3, waiting for transfers between devices, halo(): lax.ppermute(a, row_axes, forward)  5.79 us
    all_to_all x1, starting transfers between devices, body(): both = lax.all_to_all(both, 'vec', 0, 0)  4.83 us
  transfers between devices with their start and end apart: 7, of which 4 were waited for; matrix products, arithmetic and copies ran while one was open for 1% of the time, Pallas kernels for 1%

profile of v3, /device:TPU:1, one launch (start us, length us, event | category | flops | bytes accessed | tf_op | source)
XLA Modules:
  0.0 158.6 jit_solution(2504256831866319856)
XLA Ops:
  0.6 0.8 pad_maximum_fusion
  1.4 0.7 broadcast_in_dim.2
  2.2 4.8 %all-to-all-start = ((f32[4,8,2048]{2,1,0:T(8,128)}), f32[4,8,2048]{2,1,0:T(8,128)S(1)}, u32[]{:S(2)}, u32[]{:S(2)}) async-start(f32[4,8,2048]{2,1,0:T(8,128)} %broadcast_in_dim.2), calls=%async_computation | async-start | bytes 524288 | tf_op jit(solution)/shard_map/all_to_all | solution.py:579
  7.2 1.9 %copy-done.1 = bf16[8,3,256,256]{3,2,1,0:T(8,128)(2,1)S(1)} copy-done((bf16[8,3,256,256]{3,2,1,0:T(8,128)(2,1)S(1)}, bf16[8,3,256,256]{3,2,1,0:T(8,128)(2,1)}, u32[]{:S(2)}) %copy-start.1) | copy-done | bytes 3145752
  9.1 1.2 copy-done.3
  10.4 0.7 copy-done.11
  11.1 2.0 %shard_map.85 = (f32[8,2048]{1,0:T(8,128)S(1)}, f32[4,8,256]{2,1,0:T(8,128)S(1)}, f32[8,128]{1,0:T(8,128)S(1)}) custom-call(s32[8,3]{1,0:T(8,128)S(1)} %copy.10.links_s, s32[1024]{0:T(1024)S(1)} %copy-done.11, s32[2]{0:T(128)S(1)} %pad_add_fusion.start_s, bf16[8,256,256]{2,1,0:T(8,128)(2,1)S(1)} %copy-done.3, bf16[8,3,256,256]{3,2,1,0:T(8,128)(2,1)S(1)} %copy-done.1), custom_call_target="tpu_custom_call" | custom-call | flops 1073741824 | bytes 4198504 | tf_op jit(solution)/shard_map/pallas_call | solution.py:48
  13.0 0.6 copy-done.9
  14.8 0.7 copy-done.6
  15.5 0.9 copy-done.7
  16.6 7.4 %collective-permute-start.1 = (f32[40,2048]{1,0:T(8,128)S(1)}, f32[40,2048]{1,0:T(8,128)}, u32[]{:S(2)}, u32[]{:S(2)}) collective-permute-start(f32[40,2048]{1,0:T(8,128)S(1)} %shard_map.86.fc), channel_id=1, source_target_pairs={{4,0},{8,4},{12,8},{16,12},{20,16},{24,20},{28,24},{32,28},{36,32}... | collective-permute-start | bytes 983048 | tf_op jit(solution)/shard_map/ppermute | solution.py:569
  23.9 1.9 %collective-permute-start = (f32[40,2048]{1,0:T(8,128)S(1)}, f32[40,2048]{1,0:T(8,128)}, u32[]{:S(2)}, u32[]{:S(2)}) collective-permute-start(f32[40,2048]{1,0:T(8,128)S(1)} %shard_map.86.fc), channel_id=1, source_target_pairs={{0,4},{4,8},{8,12},{12,16},{16,20},{20,24},{24,28},{28,32},{32,36}... | collective-permute-start | bytes 983048 | tf_op jit(solution)/shard_map/ppermute | solution.py:569
  25.9 0.7 broadcast_subtract_fusion.window_s
  26.6 3.3 %collective-permute-done.fl = f32[40,2048]{1,0:T(8,128)} collective-permute-done((f32[40,2048]{1,0:T(8,128)S(1)}, f32[40,2048]{1,0:T(8,128)}, u32[]{:S(2)}, u32[]{:S(2)}) %collective-permute-start) | collective-permute-done | bytes 327712 | tf_op jit(solution)/shard_map/ppermute | solution.py:569
  29.8 1.2 copy-done.4
  31.1 3.4 %shard_map.87 = (f32[16,2048]{1,0:T(8,128)S(1)}, f32[16,2048]{1,0:T(8,128)S(1)}, f32[16,128]{1,0:T(8,128)S(1)}) custom-call(s32[8,3]{1,0:T(8,128)S(1)} %broadcast_subtract_fusion.window_s, bf16[8,256,256]{2,1,0:T(8,128)(2,1)S(1)} %copy-done.4, bf16[8,3,256,256]{3,2,1,0:T(8,128)(2,1)S(1)} %copy-done.2, f32[40,2048]{1,0:T(8,128)S(1)} %shard_map.86.fc, ...), custom_call_target="tpu_custom_call" | custom-call | bytes 5177440 | tf_op jit(solution)/shard_map/pallas_call | solution.py:48
  34.4 1.9 %collective-permute-start.3 = (f32[16,2048]{1,0:T(8,128)S(1)}, f32[16,2048]{1,0:T(8,128)S(1)}, u32[]{:S(2)}, u32[]{:S(2)}) collective-permute-start(f32[16,2048]{1,0:T(8,128)S(1)} %get-tuple-element.17.ic.ix), channel_id=1, source_target_pairs={{4,0},{8,4},{12,8},{16,12},{20,16},{24,20},{28,24},{32,28},{36,32}... | collective-permute-start | bytes 393224 | tf_op jit(solution)/shard_map/ppermute | solution.py:569
  36.4 4.5 %collective-permute-start.2 = (f32[16,2048]{1,0:T(8,128)S(1)}, f32[16,2048]{1,0:T(8,128)S(1)}, u32[]{:S(2)}, u32[]{:S(2)}) collective-permute-start(f32[16,2048]{1,0:T(8,128)S(1)} %get-tuple-element.17.ic.ix), channel_id=1, source_target_pairs={{0,4},{4,8},{8,12},{12,16},{16,20},{20,24},{24,28},{28,32},{32,36}... | collective-permute-start | bytes 393224 | tf_op jit(solution)/shard_map/ppermute | solution.py:569
  40.9 0.7 collective-permute-done.3.ih
  41.6 1.2 collective-permute-done.2.il
  42.8 1.7 %shard_map.88 = f32[16,16,128]{2,1,0:T(8,128)S(1)} custom-call(s32[8,3]{1,0:T(8,128)S(1)} %broadcast_subtract_fusion.window_s, f32[40,2048]{1,0:T(8,128)S(1)} %shard_map.86.fc, f32[40,2048]{1,0:T(8,128)} %collective-permute-done.fl, f32[40,2048]{1,0:T(8,128)} %collective-permute-done.1.fh, f32[16,2048]{1,0:T(8,128)S(1)} %get-tuple-element.17.ic.ix, ...), custom_call_target="tpu_custom_call" | custom-call | bytes 1421408 | tf_op jit(solution)/shard_map/pallas_call | solution.py:48
  44.5 25.3 %all_to_all.25.got = f32[16,16,128]{2,1,0:T(8,128)S(1)} all-to-all(f32[16,16,128]{2,1,0:T(8,128)S(1)} %shard_map.88), channel_id=1, replica_groups=mesh['z'=8,'y'=8,'core'=2,'vec'=4] {'z','core'}, dimensions={0} | all-to-all | bytes 262144 | tf_op jit(solution)/shard_map/all_to_all | solution.py:608
  69.9 16.2 %all_to_all.26.got = f32[8,80,128]{2,1,0:T(8,128)S(1)} all-to-all(f32[8,80,128]{2,1,0:T(8,128)S(1)} %shard_map.89), channel_id=1, replica_groups=mesh['z'=8,'y'=8,'core'=2,'vec'=4] {'y'}, dimensions={0} | all-to-all | bytes 655360 | tf_op jit(solution)/shard_map/all_to_all | solution.py:616
  86.1 28.7 %shard_map.90 = (f32[16,16]{1,0:T(8,128)S(1)}, f32[16,32]{1,0:T(8,128)S(1)}, f32[16,128]{1,0:T(8,128)S(1)}) custom-call(s32[1024]{0:T(1024)S(1)} %copy-done.12, s32[2]{0:T(128)S(1)} %copy-done.14, f32[8,80,128]{2,1,0:T(8,128)S(1)} %all_to_all.26.got), custom_call_target="tpu_custom_call" | custom-call | bytes 331784 | tf_op jit(solution)/shard_map/pallas_call | solution.py:48
  114.8 3.7 %shard_map.91 = (f32[4,2048]{1,0:T(4,128)}, f32[4,2048]{1,0:T(4,128)}, f32[16,2048]{1,0:T(8,128)S(1)}, bf16[16,2048]{1,0:T(8,128)(2,1)S(1)}) custom-call(s32[8,3]{1,0:T(8,128)S(1)} %broadcast_subtract_fusion.window_s, s32[2]{0:T(128)S(1)} %copy-done.14, bf16[8,256,256]{2,1,0:T(8,128)(2,1)S(1)} %copy-done.5, bf16[8,3,256,256]{3,2,1,0:T(8,128)(2,1)S(1)} %copy-done.2, ...), custom_call_target="tpu_custom_call" | custom-call | bytes 5573736 | tf_op jit(solution)/shard_map/pallas_call | solution.py:48
  118.5 2.3 %collective-permute-start.5 = (bf16[16,2048]{1,0:T(8,128)(2,1)S(1)}, bf16[16,2048]{1,0:T(8,128)(2,1)S(1)}, u32[]{:S(2)}, u32[]{:S(2)}) collective-permute-start(bf16[16,2048]{1,0:T(8,128)(2,1)S(1)} %get-tuple-element.26.sc), channel_id=1, source_target_pairs={{4,0},{8,4},{12,8},{16,12},{20,16},{24,20},{28,24},{32,28},{36,32}... | collective-permute-start | bytes 196616 | tf_op jit(solution)/shard_map/ppermute | solution.py:569
  120.9 3.2 %collective-permute-start.4 = (bf16[16,2048]{1,0:T(8,128)(2,1)S(1)}, bf16[16,2048]{1,0:T(8,128)(2,1)S(1)}, u32[]{:S(2)}, u32[]{:S(2)}) collective-permute-start(bf16[16,2048]{1,0:T(8,128)(2,1)S(1)} %get-tuple-element.26.sc), channel_id=1, source_target_pairs={{0,4},{4,8},{8,12},{12,16},{16,20},{20,24},{24,28},{28,32},{32,36}... | collective-permute-start | bytes 196616 | tf_op jit(solution)/shard_map/ppermute | solution.py:569
  124.1 1.3 collective-permute-done.4.sl
  125.4 2.9 %shard_map.92 = f32[16,16,128]{2,1,0:T(8,128)S(1)} custom-call(s32[8,3]{1,0:T(8,128)S(1)} %broadcast_subtract_fusion.window_s, bf16[8,256,256]{2,1,0:T(8,128)(2,1)S(1)} %copy-done.5, bf16[8,3,256,256]{3,2,1,0:T(8,128)(2,1)S(1)} %copy-done.2, f32[16,2048]{1,0:T(8,128)S(1)} %get-tuple-element.25.w, bf16[16,2048]{1,0:T(8,128)(2,1)S(1)} %get-tuple-element.26.sc, ...), custom_call_target="tpu_custom_call" | custom-call | bytes 5111904 | tf_op jit(solution)/shard_map/pallas_call | solution.py:48
  128.3 16.2 %all_to_all.27.got = f32[16,16,128]{2,1,0:T(8,128)S(1)} all-to-all(f32[16,16,128]{2,1,0:T(8,128)S(1)} %shard_map.92), channel_id=1, replica_groups=mesh['z'=8,'y'=8,'core'=2,'vec'=4] {'z','core'}, dimensions={0} | all-to-all | bytes 262144 | tf_op jit(solution)/shard_map/all_to_all | solution.py:652
  144.6 9.9 %all_to_all.28.got = f32[8,16,128]{2,1,0:T(8,128)S(1)} all-to-all(f32[8,16,128]{2,1,0:T(8,128)S(1)} %shard_map.93), channel_id=1, replica_groups=mesh['z'=8,'y'=8,'core'=2,'vec'=4] {'y'}, dimensions={0} | all-to-all | bytes 131072 | tf_op jit(solution)/shard_map/all_to_all | solution.py:654
  154.6 4.1 %shard_map.94 = f32[48,48]{1,0:T(8,128)} custom-call(f32[8,16,128]{2,1,0:T(8,128)S(1)} %all_to_all.28.got, f32[16,128]{1,0:T(8,128)S(1)} %get-tuple-element.28.gram), custom_call_target="tpu_custom_call" | custom-call | bytes 73728 | tf_op jit(solution)/shard_map/pallas_call | solution.py:48
  (36 shorter events, 1.6 us)
Async XLA Ops:
  0.6 6.4 %copy-start = (s32[1024,3]{0,1:T(4,128)S(1)}, s32[1024,3]{0,1:T(4,128)}, u32[]{:S(2)}) copy-start(s32[1024,3]{0,1:T(4,128)} %param.8) | copy-start | bytes 36868
  2.2 12.6 %all-to-all-start = ((f32[4,8,2048]{2,1,0:T(8,128)}), f32[4,8,2048]{2,1,0:T(8,128)S(1)}, u32[]{:S(2)}, u32[]{:S(2)}) async-start(f32[4,8,2048]{2,1,0:T(8,128)} %broadcast_in_dim.2), calls=%async_computation | async-start | bytes 524288 | tf_op jit(solution)/shard_map/all_to_all | solution.py:579
  7.2 7.6 %copy-start.8 = (s32[8,3]{1,0:T(8,128)}, s32[8,3]{1,0:T(8,128)S(1)}, u32[]{:S(2)}) copy-start(s32[8,3]{1,0:T(8,128)S(1)} %copy.10.links_s) | copy-start | bytes 292
  7.2 1.9 %copy-start.1 = (bf16[8,3,256,256]{3,2,1,0:T(8,128)(2,1)S(1)}, bf16[8,3,256,256]{3,2,1,0:T(8,128)(2,1)}, u32[]{:S(2)}) copy-start(bf16[8,3,256,256]{3,2,1,0:T(8,128)(2,1)} %link_t.7) | copy-start | bytes 9437188
  9.1 1.2 copy-start.3
  10.4 0.7 copy-start.11
  11.1 18.8 %copy-start.2 = (bf16[8,3,256,256]{3,2,1,0:T(8,128)(2,1)S(1)}, bf16[8,3,256,256]{3,2,1,0:T(8,128)(2,1)}, u32[]{:S(2)}) copy-start(bf16[8,3,256,256]{3,2,1,0:T(8,128)(2,1)} %link_t.7) | copy-start | bytes 9437188
  13.0 0.6 copy-start.9
  13.6 0.6 copy-start.13
  14.2 0.6 copy-start.15
  14.8 0.7 copy-start.6
  15.5 0.9 copy-start.7
  16.5 26.3 %copy-start.16 = (f32[8,128]{1,0:T(8,128)S(1)}, f32[8,128]{1,0:T(8,128)}, u32[]{:S(2)}) copy-start(f32[8,128]{1,0:T(8,128)} %copy-done.15) | copy-start | bytes 12292
  16.6 10.0 %collective-permute-start.1 = (f32[40,2048]{1,0:T(8,128)S(1)}, f32[40,2048]{1,0:T(8,128)}, u32[]{:S(2)}, u32[]{:S(2)}) collective-permute-start(f32[40,2048]{1,0:T(8,128)S(1)} %shard_map.86.fc), channel_id=1, source_target_pairs={{4,0},{8,4},{12,8},{16,12},{20,16},{24,20},{28,24},{32,28},{36,32}... | collective-permute-start | bytes 983048 | tf_op jit(solution)/shard_map/ppermute | solution.py:569
  23.9 5.9 %collective-permute-start = (f32[40,2048]{1,0:T(8,128)S(1)}, f32[40,2048]{1,0:T(8,128)}, u32[]{:S(2)}, u32[]{:S(2)}) collective-permute-start(f32[40,2048]{1,0:T(8,128)S(1)} %shard_map.86.fc), channel_id=1, source_target_pairs={{0,4},{4,8},{8,12},{12,16},{16,20},{20,24},{24,28},{28,32},{32,36}... | collective-permute-start | bytes 983048 | tf_op jit(solution)/shard_map/ppermute | solution.py:569
  25.8 60.3 %copy-start.12 = (s32[1024]{0:T(1024)S(1)}, s32[1024]{0:T(1024)}, u32[]{:S(2)}) copy-start(s32[1024]{0:T(1024)} %coarse_s.3) | copy-start | bytes 12292
  25.9 60.2 %copy-start.14 = (s32[2]{0:T(128)S(1)}, s32[2]{0:T(128)}, u32[]{:S(2)}) copy-start(s32[2]{0:T(128)} %copy-done.13) | copy-start | bytes 28
  29.8 1.2 copy-start.4
  31.1 11.8 %copy-start.10 = (f32[4,8,256]{2,1,0:T(8,128)S(1)}, f32[4,8,256]{2,1,0:T(8,128)}, u32[]{:S(2)}) copy-start(f32[4,8,256]{2,1,0:T(8,128)} %copy-done.9) | copy-start | bytes 98308
  31.1 83.7 %copy-start.5 = (bf16[8,256,256]{2,1,0:T(8,128)(2,1)S(1)}, bf16[8,256,256]{2,1,0:T(8,128)(2,1)}, u32[]{:S(2)}) copy-start(bf16[8,256,256]{2,1,0:T(8,128)(2,1)} %self_t.7) | copy-start | bytes 3145732
  34.4 7.2 %collective-permute-start.3 = (f32[16,2048]{1,0:T(8,128)S(1)}, f32[16,2048]{1,0:T(8,128)S(1)}, u32[]{:S(2)}, u32[]{:S(2)}) collective-permute-start(f32[16,2048]{1,0:T(8,128)S(1)} %get-tuple-element.17.ic.ix), channel_id=1, source_target_pairs={{4,0},{8,4},{12,8},{16,12},{20,16},{24,20},{28,24},{32,28},{36,32}... | collective-permute-start | bytes 393224 | tf_op jit(solution)/shard_map/ppermute | solution.py:569
  36.4 6.4 %collective-permute-start.2 = (f32[16,2048]{1,0:T(8,128)S(1)}, f32[16,2048]{1,0:T(8,128)S(1)}, u32[]{:S(2)}, u32[]{:S(2)}) collective-permute-start(f32[16,2048]{1,0:T(8,128)S(1)} %get-tuple-element.17.ic.ix), channel_id=1, source_target_pairs={{0,4},{4,8},{8,12},{12,16},{16,20},{20,24},{24,28},{28,32},{32,36}... | collective-permute-start | bytes 393224 | tf_op jit(solution)/shard_map/ppermute | solution.py:569
  118.5 5.6 %collective-permute-start.5 = (bf16[16,2048]{1,0:T(8,128)(2,1)S(1)}, bf16[16,2048]{1,0:T(8,128)(2,1)S(1)}, u32[]{:S(2)}, u32[]{:S(2)}) collective-permute-start(bf16[16,2048]{1,0:T(8,128)(2,1)S(1)} %get-tuple-element.26.sc), channel_id=1, source_target_pairs={{4,0},{8,4},{12,8},{16,12},{20,16},{24,20},{28,24},{32,28},{36,32}... | collective-permute-start | bytes 196616 | tf_op jit(solution)/shard_map/ppermute | solution.py:569
  120.9 4.5 %collective-permute-start.4 = (bf16[16,2048]{1,0:T(8,128)(2,1)S(1)}, bf16[16,2048]{1,0:T(8,128)(2,1)S(1)}, u32[]{:S(2)}, u32[]{:S(2)}) collective-permute-start(bf16[16,2048]{1,0:T(8,128)(2,1)S(1)} %get-tuple-element.26.sc), channel_id=1, source_target_pairs={{0,4},{4,8},{8,12},{12,16},{16,20},{20,24},{24,28},{28,32},{32,36}... | collective-permute-start | bytes 196616 | tf_op jit(solution)/shard_map/ppermute | solution.py:569

commit v4 on v3

v4 whole, which is shorter than its diff:
```python
import functools
import jax
import jax.numpy as jnp
from jax import lax
from jax.experimental import pallas as pl
from jax.experimental.pallas import tpu as pltpu
from jax.sharding import Mesh, PartitionSpec as P

spectral_shift = 0.25
damping = 0.6
LANE = 128
GROUPS = 4

F32 = jnp.float32
BF16 = jnp.bfloat16
EXACT = lax.Precision.HIGHEST


def nn(left, right, precision=None):
    return lax.dot_general(
        left, right, (((1,), (0,)), ((), ())), precision=precision, preferred_element_type=F32
    )


def nt(left, right, precision=None):
    return lax.dot_general(
        left, right, (((1,), (1,)), ((), ())), precision=precision, preferred_element_type=F32
    )


def tn(left, right, precision=None):
    return lax.dot_general(
        left, right, (((0,), (0,)), ((), ())), precision=precision, preferred_element_type=F32
    )


def iota(shape, dim):
    return lax.broadcasted_iota(jnp.int32, shape, dim)


def run(kernel, inputs, outputs, scratch=(), smem=0):
    in_specs = [
        pl.BlockSpec(memory_space=pltpu.SMEM if i < smem else pltpu.VMEM)
        for i in range(len(inputs))
    ]
    single = not isinstance(outputs, (list, tuple))
    shapes = [outputs] if single else list(outputs)
    specs = [pl.BlockSpec(memory_space=pltpu.VMEM) for _ in shapes]
    return pl.pallas_call(
        kernel,
        in_specs=in_specs,
        out_specs=specs[0] if single else specs,
        out_shape=shapes[0] if single else shapes,
        scratch_shapes=list(scratch),
        compiler_params=pltpu.CompilerParams(vmem_limit_bytes=16 << 20),
    )(*inputs)


def arr(shape, dtype=F32):
    return jax.ShapeDtypeStruct(shape, dtype)


def safe(value):
    return jnp.where(value > 0.0, value, 1.0)


def stack_kernel(vectors, directions, out):
    mine = vectors.shape[0]
    for v in range(out.shape[0]):
        out[v, :mine] = vectors[...]
        out[v, mine:] = directions[...]


def prep_kernel(links_s, coarse_s, start_s, self_t, link_t, both, fields, col, info):
    count, size = self_t.shape[0], self_t.shape[1]
    members, twice, _ = both.shape
    mine = twice // 2
    base = members * twice
    for v in range(members):
        fields[v * mine : (v + 1) * mine, :] = both[v, :mine]
        fields[(members + v) * mine : (members + v + 1) * mine, :] = both[v, mine:]
    ones = jnp.ones((8, size), BF16)
    diagonal = iota((size, size), 0) == iota((size, size), 1)
    lane = iota((1, LANE), 1)
    for b in range(count):
        own = self_t[b]
        degree = nt(ones, own)[0:1]
        col[0, b : b + 1, :] = degree
        row = jnp.where(lane == 0, jnp.sum(degree, axis=1, keepdims=True), 0.0)
        ids = jnp.where(lane == 4, coarse_s[start_s[0] + b], 0)
        for s in range(3):
            tile = link_t[b, s]
            part = nt(ones, tile)[0:1]
            degree = degree + part
            row = jnp.where(lane == 1 + s, jnp.sum(part, axis=1, keepdims=True), row)
            ids = jnp.where(lane == 5 + s, coarse_s[links_s[s, start_s[0] + b]], ids)
            col[1 + s, b : b + 1, :] = jnp.sum(tile.astype(F32), axis=0, keepdims=True)
        diag = jnp.sum(jnp.where(diagonal, own.astype(F32), 0.0), axis=0, keepdims=True)
        span = slice(b * size, (b + 1) * size)
        fields[base : base + 1, span] = degree
        fields[base + 1 : base + 2, span] = 1.0 + spectral_shift - diag / degree
        info[b : b + 1, :] = row + ids.astype(F32)
    fields[base + 2 : base + 8, :] = jnp.zeros((6, fields.shape[1]), F32)


def linked(links_s, start_s, b, s, count):
    return links_s[s, start_s[0] + b] - start_s[0] + count


def apply_tiles(links_s, start_s, self_t, link_t, win, b, count):
    acc = nt(win[count + b], self_t[b])
    for s in range(3):
        acc = acc + nt(win[linked(links_s, start_s, b, s, count)], link_t[b, s])
    return acc


def image_kernel(links_s, start_s, self_t, link_t, fc, fl, fh, image_x, image_p, gram, win):
    count, size = self_t.shape[0], self_t.shape[1]
    half = image_x.shape[0]
    both = 2 * half
    for part, f in enumerate((fl, fc, fh)):
        for b in range(count):
            span = slice(b * size, (b + 1) * size)
            root = jnp.sqrt(safe(f[both : both + 1, span]))
            win[part * count + b] = (f[:both, span] / root).astype(BF16)
    for b in range(count):
        acc = apply_tiles(links_s, start_s, self_t, link_t, win, b, count)
        span = slice(b * size, (b + 1) * size)
        value = fc[:both, span] - acc / jnp.sqrt(fc[both : both + 1, span])
        image_x[:, span] = value[:half]
        image_p[:, span] = value[half:]
    z = fc[:both, :]
    ix = image_x[...]
    ip = image_p[...]
    basis = nt(z, z, EXACT)
    cross = nt(ix, z, EXACT)
    other = nt(ip, z, EXACT)
    mixed = 0.5 * (cross[:, half:] + nt(z[:half], ip, EXACT))
    gram[:, 0:half] = basis[:half, :half]
    gram[:, half : 2 * half] = basis[:half, half:]
    gram[:, 2 * half : 3 * half] = basis[half:, half:]
    gram[:, 3 * half : 4 * half] = cross[:, :half]
    gram[:, 4 * half : 5 * half] = mixed
    gram[:, 5 * half : 6 * half] = other[:, half:]
    gram[:, 6 * half :] = jnp.zeros((half, LANE - 6 * half), F32)


def node_scales(f, both, span):
    shift = f[both + 1 : both + 2, span]
    return jnp.sqrt(safe(f[both : both + 1, span])), jnp.where(shift == 0.0, 1.0, shift)


def restrict_kernel(
    links_s, start_s, fc, fl, fh, ic, il, ih, col, gram, info, out, win, weighted, packed
):
    count, size = col.shape[1], col.shape[2]
    half = ic.shape[0]
    width = 2 * half
    for part, (f, img) in enumerate(((fl, il), (fc, ic), (fh, ih))):
        for b in range(count):
            span = slice(b * size, (b + 1) * size)
            root, shift = node_scales(f, width, span)
            field = jnp.concatenate([f[:half, span], img[:, span]], axis=0)
            smooth = field * (damping / shift)
            win[part * count + b] = smooth / root
            if part == 1:
                weighted[b * width : (b + 1) * width, :] = root * (
                    field - (1.0 + spectral_shift) * smooth
                )
    for b in range(count):
        acc = weighted[b * width : (b + 1) * width, :] + col[0, b : b + 1, :] * win[count + b]
        for s in range(3):
            acc = acc + col[1 + s, b : b + 1, :] * win[linked(links_s, start_s, b, s, count)]
        weighted[b * width : (b + 1) * width, :] = acc
    sums = nt(jnp.ones((8, size), F32), weighted[...], EXACT)
    packed[...] = gram[...]
    for b in range(count):
        packed[b : b + 1, LANE - width :] = sums[0:1, b * width : (b + 1) * width]
        packed[count + b : count + b + 1, LANE - width :] = info[b : b + 1, 0:width]
    value = packed[...]
    for i in range(out.shape[0]):
        out[i] = value


def relay_kernel(got, out, packed):
    members, rows, _ = got.shape
    half = rows // 2
    deep = members // GROUPS
    width = LANE // GROUPS
    total = got[0]
    for i in range(1, members):
        total = total + got[i]
    packed[0:rows, :] = total
    tail = rows + deep * half
    if members * 8 < LANE:
        packed[tail : tail + half, :] = jnp.zeros((half, LANE), F32)
    for i in range(members):
        g, j = i // deep, i % deep
        at = rows + j * half
        mine = got[i]
        packed[at : at + half, g * width : (g + 1) * width] = mine[:half, LANE - width :]
        packed[tail : tail + half, i * 8 : (i + 1) * 8] = mine[half:, LANE - width : LANE - width + 8]
    value = packed[...]
    for i in range(out.shape[0]):
        out[i] = value


def add_kernel(got, out):
    total = got[0]
    for i in range(1, got.shape[0]):
        total = total + got[i]
    for i in range(out.shape[0]):
        out[i] = total


def lane_copy(tile, at):
    return jnp.broadcast_to(tile[:, at : at + 1], tile.shape)


def row_copy(tile, at):
    return jnp.broadcast_to(tile[at : at + 1, :], tile.shape)


def solve_tile(cols, tile, more, sub):
    fields = list(cols) + [tile] + list(more)
    final = tile
    for p in range(0, 8, 2):
        q = p + 1
        vp, vq = fields[p], fields[q]
        a, c = row_copy(vp, p), row_copy(vp, q)
        b, d = row_copy(vq, p), row_copy(vq, q)
        det = a * d - b * c
        r = 1.0 / det
        ar, br, cr, dr = a * r, b * r, c * r, d * r
        f0, f1 = vp * dr - vq * cr, vq * ar - vp * br
        f0 = jnp.where(sub == p, 1.0 - dr, jnp.where(sub == q, cr, f0))
        f1 = jnp.where(sub == p, br, jnp.where(sub == q, 1.0 - ar, f1))
        x0, x1 = row_copy(fields[8], p), row_copy(fields[8], q)
        root = 1.0 / jnp.sqrt(a)
        final = jnp.where(sub == p, x0 * root, final)
        final = jnp.where(sub == q, (x1 * a - c * x0) * (root / jnp.sqrt(det)), final)
        for m in range(q + 1, len(fields)):
            x = fields[m]
            fields[m] = x - (f0 * row_copy(x, p) + f1 * row_copy(x, q))
    return fields[8], final, fields[9:]


def sum8(terms):
    a, b, c, d, e, f, g, h = terms
    return ((a + b) + (c + d)) + ((e + f) + (g + h))


def invert_dense(matrix, whole):
    n = matrix.shape[0]
    shape = (8, n)
    tiles = [matrix[8 * i : 8 * i + 8, :] for i in range(n // 8)]
    lane, sub = iota(shape, 1), iota(shape, 0)
    cols = [lane_copy(tiles[0], j) for j in range(8)]
    for at in range(n // 8):
        k = 8 * at
        last = at + 1 == n // 8
        inside = (lane >= k) & (lane < k + 8)
        start = jnp.where(inside, jnp.where(lane == sub + k, 1.0, 0.0), tiles[at])
        ahead = [] if last else [lane_copy(tiles[at], k + 8 + j) for j in range(8)]
        new, final, ahead = solve_tile(cols, start, ahead, sub)
        rows = [row_copy(new, j) for j in range(8)]
        for i in range(0 if whole else at + 1, n // 8):
            if i != at:
                old = tiles[i]
                parts = [lane_copy(old, k + j) for j in range(8)]
                if i == at + 1:
                    cols = [
                        lane_copy(old, k + 8 + j)
                        - sum8([parts[m] * row_copy(ahead[j], m) for m in range(8)])
                        for j in range(8)
                    ]
                tiles[i] = jnp.where(inside, 0.0, old) - sum8(
                    [parts[j] * rows[j] for j in range(8)]
                )
        tiles[at] = new if whole else jnp.where(lane <= sub + k, final, 0.0)
    return jnp.concatenate(tiles, axis=0)


def unit_scales(matrix):
    square = iota(matrix.shape, 0) == iota(matrix.shape, 1)
    diag = jnp.where(square, matrix, 0.0)
    row = 1.0 / jnp.sqrt(jnp.sum(diag, axis=0, keepdims=True))
    return row, 1.0 / jnp.sqrt(jnp.sum(diag, axis=1, keepdims=True))


def split3(value):
    high = value.astype(BF16)
    rest = value - high.astype(F32)
    mid = rest.astype(BF16)
    low = (rest - mid.astype(F32)).astype(BF16)
    return high, mid, low


def coarse_kernel(coarse_s, start_s, got, coef, gain, gram, uw, info, mat, hot, upper, pivots):
    members, depth, _ = got.shape
    rows = 16
    half = rows
    deep = (depth - rows) // 8 - 1
    width = LANE // GROUPS
    nc = mat.shape[0]
    count = coarse_s.shape[0]
    total = got[0, 0:rows]
    for y in range(1, members):
        total = total + got[y, 0:rows]
    gram[...] = total
    for y in range(members):
        for j in range(deep):
            at = (y * deep + j) * 8
            src = rows + j * 8
            uw[at : at + 8, :] = got[y, src : src + 8]
            for g in range(GROUPS):
                i = (g * deep + j) * 8
                info[at : at + 8, g * width : g * width + 8] = got[y, depth - 8 :, i : i + 8]
    blocks = uw.shape[0]
    lanes = iota((blocks, nc), 1)
    agg = jnp.zeros((1, nc), F32)
    tiles = jnp.zeros((nc, nc), F32)
    for g in range(GROUPS):
        at = g * width
        values = [info[:, at + s : at + s + 1] for s in range(4)]
        ids = [info[:, at + 4 + s : at + 5 + s].astype(jnp.int32) for s in range(4)]
        here = lanes == ids[0]
        block_degree = values[0] + values[1] + values[2] + values[3]
        agg = agg + jnp.sum(jnp.where(here, block_degree, 0.0), axis=0, keepdims=True)
        spread = jnp.where(here, values[0], 0.0)
        for s in range(1, 4):
            spread = spread + jnp.where(lanes == ids[s], values[s], 0.0)
        member = jnp.where(here, 1.0, 0.0)
        hot[g] = member
        member = member.astype(BF16)
        for piece in split3(spread):
            tiles = tiles + tn(member, piece)
    same = iota((nc, nc), 0) == iota((nc, nc), 1)
    agg_col = jnp.sum(jnp.where(same, agg, 0.0), axis=1, keepdims=True)
    inv_row = 1.0 / jnp.sqrt(agg)
    inv_col = 1.0 / jnp.sqrt(agg_col)
    mat[...] = (jnp.where(same, (1.0 + spectral_shift) * agg, 0.0) - tiles) * inv_col * inv_row

    grams = total[:, 0:half]
    square = iota((half, half), 0) == iota((half, half), 1)
    unit_row, unit_col = unit_scales(grams)
    inverse = invert_dense(grams * unit_row * unit_col, True) * unit_row * unit_col
    ritz = nn(total[:, 3 * half : 4 * half], inverse, EXACT)
    coef[...] = ritz
    combine = jnp.concatenate([-ritz, jnp.where(square, 1.0, 0.0)], axis=1)
    rhs = jnp.zeros((half, nc), F32)
    for g in range(GROUPS):
        block_rhs = nt(combine, uw[:, g * width : (g + 1) * width], EXACT)
        rhs = rhs + nn(block_rhs, hot[g], EXACT)
    rhs = rhs * inv_row

    block = min(LANE, nc)
    steps = nc // block

    def eliminate(step, _):
        at = pl.multiple_of(step * block, block)
        pivot = invert_dense(mat[pl.ds(at, block), pl.ds(at, block)], False)
        pivots[pl.ds(at, block), :] = pivot
        for j in range(steps - 1):

            @pl.when(step == j)
            def _():
                lo, hi = j * block, (j + 1) * block
                strip = nn(pivot, mat[lo:hi, hi:], EXACT)
                upper[lo:hi, hi:] = strip
                mat[hi:, hi:] = mat[hi:, hi:] - tn(strip, strip, EXACT)

        return 0

    lax.fori_loop(0, steps, eliminate, 0)
    halves = []
    for j in range(steps):
        lo, hi = j * block, (j + 1) * block
        head = nt(rhs[:, :block], pivots[lo:hi, :], EXACT)
        halves.append(head)
        if hi < nc:
            rhs = rhs[:, block:] - nn(head, upper[lo:hi, hi:], EXACT)
    error = nn(halves[-1], pivots[nc - block :, :], EXACT)
    for j in reversed(range(steps - 1)):
        lo, hi = j * block, (j + 1) * block
        head = halves[j] - nt(error, upper[lo:hi, hi:], EXACT)
        error = jnp.concatenate([nn(head, pivots[lo:hi, :], EXACT), error], axis=1)
    lifted = error * inv_row
    wide = iota((1, nc), 1)
    picks = []
    for j in range(24):
        at = jnp.clip(start_s[0] - 8 + j, 0, count - 1)
        picks.append(jnp.where(wide == coarse_s[at], 1.0, 0.0))
    picks.append(jnp.zeros((8, nc), F32))
    gain[...] = nt(lifted, jnp.concatenate(picks, axis=0), EXACT)


def correct_kernel(
    links_s, start_s, self_t, link_t, fc, fl, fh, ic, il, ih, coef, gain,
    my_residual, my_corrected, corrected, scaled, win, second, residual,
):
    count, size = self_t.shape[0], self_t.shape[1]
    half = ic.shape[0]
    both = 2 * half
    ritz = coef[...]
    gains = gain[...]
    for part, (f, img) in enumerate(((fl, il), (fc, ic), (fh, ih))):
        res = img[...] - nn(ritz, f[:half, :], EXACT)
        if part == 1:
            residual[...] = res
        for b in range(count):
            span = slice(b * size, (b + 1) * size)
            root, shift = node_scales(f, both, span)
            j = part * count + b
            field = damping * res[:, span] / shift + root * gains[:, j : j + 1]
            win[j] = (field / root).astype(BF16)
            if part == 1:
                second[:, span] = field
    for b in range(count):
        span = slice(b * size, (b + 1) * size)
        root, shift = node_scales(fc, both, span)
        acc = apply_tiles(links_s, start_s, self_t, link_t, win, b, count)
        field = second[:, span]
        after = field - acc / root + spectral_shift * field
        field = field + damping * (residual[:, span] - after) / shift
        corrected[:, span] = field
        scaled[:, span] = (field / root).astype(BF16)
    mine = my_residual.shape[0]
    pick = iota((mine, half), 1) == iota((mine, half), 0) + start_s[1] * mine
    pick = jnp.where(pick, 1.0, 0.0)
    my_residual[...] = nn(pick, residual[...], EXACT)
    my_corrected[...] = nn(pick, corrected[...], EXACT)


def search_kernel(links_s, start_s, self_t, link_t, w, sc, sl, sh, fc, ix, ip, out, win, image_w):
    count, size = self_t.shape[0], self_t.shape[1]
    half = w.shape[0]
    for part, s in enumerate((sl, sc, sh)):
        for b in range(count):
            win[part * count + b] = s[:, b * size : (b + 1) * size]
    for b in range(count):
        span = slice(b * size, (b + 1) * size)
        acc = apply_tiles(links_s, start_s, self_t, link_t, win, b, count)
        image_w[:, span] = w[:, span] - acc / jnp.sqrt(fc[2 * half : 2 * half + 1, span])
    field = w[...]
    field_image = image_w[...]
    zz = fc[: 2 * half, :]
    images = jnp.concatenate([ix[...], ip[...]], axis=0)
    value = jnp.concatenate(
        [
            nt(field, zz, EXACT),
            nt(field, field, EXACT),
            0.5 * (nt(field, images, EXACT) + nt(field_image, zz, EXACT)),
            nt(field, field_image, EXACT),
            jnp.zeros((half, LANE - 6 * half), F32),
        ],
        axis=1,
    )
    for i in range(out.shape[0]):
        out[i] = value


def project_kernel(got, gram, out):
    h = gram.shape[0]
    n = 3 * h
    new = got[0]
    for i in range(1, got.shape[0]):
        new = new + got[i]
    old = gram[...]
    zero = jnp.zeros((h, h), F32)
    unit = jnp.where(iota((n, n), 0) == iota((n, n), 1), 1.0, 0.0)

    def whole(xx, xp, pp, wx, ww, wp):
        upper = jnp.concatenate(
            [
                jnp.concatenate([0.5 * xx, zero, xp], axis=1),
                jnp.concatenate([wx, 0.5 * ww, wp], axis=1),
                jnp.concatenate([zero, zero, 0.5 * pp], axis=1),
            ],
            axis=0,
        )
        return upper + nt(unit, upper, EXACT)

    def piece(a, i):
        return a[:, i * h : (i + 1) * h]

    gram_b = whole(
        piece(old, 0), piece(old, 1), piece(old, 2), piece(new, 0), piece(new, 2), piece(new, 1)
    )
    gram_a = whole(
        piece(old, 3), piece(old, 4), piece(old, 5), piece(new, 3), piece(new, 5), piece(new, 4)
    )
    unit_row, unit_col = unit_scales(gram_b)
    inverse = invert_dense(gram_b * unit_row * unit_col, False) * unit_row
    out[...] = nt(nn(inverse, gram_a, EXACT), inverse, EXACT)


def body(self_tiles, link_tiles, links, coarse_row, vectors, directions):
    count, size = self_tiles.shape[0], self_tiles.shape[1]
    mine = vectors.shape[0]
    slab = count * size
    vec = lax.axis_size("vec")
    k = mine * vec
    row_axes = ("z", "y", "core")
    row_index = lax.axis_index(row_axes)
    row_count = lax.axis_size(row_axes)
    stage_one = ("z", "core")
    n_one = lax.axis_size(stage_one)
    n_two = lax.axis_size("y")
    forward = [(i, i + 1) for i in range(row_count - 1)]
    backward = [(i + 1, i) for i in range(row_count - 1)]

    def halo(a):
        return lax.ppermute(a, row_axes, forward), lax.ppermute(a, row_axes, backward)

    start_s = jnp.stack([row_index * count, lax.axis_index("vec")]).astype(jnp.int32)
    links_s = links.T
    both = run(stack_kernel, (vectors, directions), arr((vec, 2 * mine, slab)))
    both, start_s = lax.optimization_barrier((both, start_s))
    both = lax.all_to_all(both, "vec", 0, 0)
    fc, col, info = run(
        prep_kernel,
        (links_s, coarse_row, start_s, self_tiles, link_tiles, both),
        (arr((2 * k + 8, slab)), arr((4, count, size)), arr((count, LANE))),
        smem=3,
    )
    fl, fh = halo(fc)
    ic, ip, gram = run(
        image_kernel,
        (links_s, start_s, self_tiles, link_tiles, fc, fl, fh),
        (arr((k, slab)), arr((k, slab)), arr((k, LANE))),
        scratch=(pltpu.VMEM((3 * count, 2 * k, size), BF16),),
        smem=2,
    )
    il, ih = halo(ic)
    sent = run(
        restrict_kernel,
        (links_s, start_s, fc, fl, fh, ic, il, ih, col, gram, info),
        arr((n_one, 2 * count, LANE)),
        scratch=(
            pltpu.VMEM((3 * count, 2 * k, size), F32),
            pltpu.VMEM((count * 2 * k, size), F32),
            pltpu.VMEM((2 * count, LANE), F32),
        ),
        smem=2,
    )
    got = lax.all_to_all(sent, stage_one, 0, 0)
    depth = count * (3 + n_one // GROUPS)
    sent = run(
        relay_kernel,
        (got,),
        arr((n_two, depth, LANE)),
        scratch=(pltpu.VMEM((depth, LANE), F32),),
    )
    got = lax.all_to_all(sent, "y", 0, 0)
    coarse_count = coarse_row.shape[0] // 2
    blocks = n_two * (n_one // GROUPS) * count
    coef, gain, gram = run(
        coarse_kernel,
        (coarse_row, start_s, got),
        (arr((k, k)), arr((k, 32)), arr((k, LANE))),
        scratch=(
            pltpu.VMEM((blocks, LANE), F32),
            pltpu.VMEM((blocks, LANE), F32),
            pltpu.VMEM((coarse_count, coarse_count), F32),
            pltpu.VMEM((GROUPS, blocks, coarse_count), F32),
            pltpu.VMEM((coarse_count, coarse_count), F32),
            pltpu.VMEM((coarse_count, min(LANE, coarse_count)), F32),
        ),
        smem=2,
    )
    residual, my_corrected, corrected, scaled = run(
        correct_kernel,
        (links_s, start_s, self_tiles, link_tiles, fc, fl, fh, ic, il, ih, coef, gain),
        (arr((mine, slab)), arr((mine, slab)), arr((k, slab)), arr((k, slab), BF16)),
        scratch=(
            pltpu.VMEM((3 * count, k, size), BF16),
            pltpu.VMEM((k, slab), F32),
            pltpu.VMEM((k, slab), F32),
        ),
        smem=2,
    )
    sl, sh = halo(scaled)
    sent = run(
        search_kernel,
        (links_s, start_s, self_tiles, link_tiles, corrected, scaled, sl, sh, fc, ic, ip),
        arr((n_one, k, LANE)),
        scratch=(pltpu.VMEM((3 * count, k, size), BF16), pltpu.VMEM((k, slab), F32)),
        smem=2,
    )
    got = lax.all_to_all(sent, stage_one, 0, 0)
    sent = run(add_kernel, (got,), arr((n_two, k, LANE)))
    got = lax.all_to_all(sent, "y", 0, 0)
    projected = run(project_kernel, (got, gram), arr((3 * k, 3 * k)))
    return residual, my_corrected, projected


def row_split(rows):
    return (8, rows // 16, 2) if rows >= 64 else (2, rows // 4, 2)


def solution(mesh):
    z, y, core = row_split(mesh.shape["rows"])
    split = Mesh(
        mesh.devices.reshape(z, y, core, mesh.shape["vec"]), ("z", "y", "core", "vec")
    )
    rows = ("z", "y", "core")
    in_specs = (
        P(rows, None, None),
        P(rows, None, None, None),
        P(),
        P(),
        P("vec", rows),
        P("vec", rows),
    )
    out_specs = (P("vec", rows), P("vec", rows), P())
    return jax.shard_map(body, mesh=split, in_specs=in_specs, out_specs=out_specs, check_vma=False)
```

time: 159 us -> 152 us (0.956)
  blocking collectives: 67.7 us -> 74.8 us
  Pallas kernels: 46.6 us -> 41.2 us
  starting transfers between devices: 26.1 us -> 21.8 us
  local copies, waits for them, and re-layouts: 9.4 us -> 6.05 us
    all_to_all x0 -> x1, blocking collectives: none -> 10.2 us  [body(): both = lax.all_to_all(both, 'vec', 0, 0)]
    pallas_call x10, Pallas kernels: 46.6 us -> 41.2 us  [run(): pl.pallas_call(kernel, in_specs=in_specs, out_specs=specs[0] if single el...]
    all_to_all x1 -> x0, starting transfers between devices: 4.83 us -> none  [body(): both = lax.all_to_all(both, 'vec', 0, 0)]
    unnamed x35 -> x20, local copies, waits for them, and re-layouts: 8.6 us -> 6.05 us
    all_to_all x2, blocking collectives: 26.1 us -> 24.1 us  [body(): got = lax.all_to_all(sent, 'y', 0, 0)]
  transfers between devices with their start and end apart: 7 -> 6, of which waited for: 4 -> 5; matrix products, arithmetic and copies ran while one was open for 1% -> 0% of each run, Pallas kernels for 1% -> 0%
where the time goes in v4:
time: 152 us
  blocking collectives  74.8 us (49%)
  Pallas kernels  41.2 us (27%)
  starting transfers between devices  21.8 us (14%)
  waiting for transfers between devices  7 us (5%)
  local copies, waits for them, and re-layouts  6.05 us (4%)
    pallas_call x10, Pallas kernels, run(): pl.pallas_call(kernel, in_specs=in_specs, out_specs=specs[0] if single el...  41.2 us
    all_to_all x2, blocking collectives, body(): got = lax.all_to_all(sent, stage_one, 0, 0)  40.5 us
    all_to_all x2, blocking collectives, body(): got = lax.all_to_all(sent, 'y', 0, 0)  24.1 us
    ppermute x3, starting transfers between devices, halo(): lax.ppermute(a, row_axes, backward)  12.1 us
    all_to_all x1, blocking collectives, body(): both = lax.all_to_all(both, 'vec', 0, 0)  10.2 us
    ppermute x3, starting transfers between devices, halo(): lax.ppermute(a, row_axes, forward)  9.75 us
    unnamed x20, local copies, waits for them, and re-layouts  6.05 us
    ppermute x3, waiting for transfers between devices, halo(): lax.ppermute(a, row_axes, forward)  5.93 us
  transfers between devices with their start and end apart: 6, of which 5 were waited for; matrix products, arithmetic and copies ran while one was open for 0% of the time, Pallas kernels for 0%

profile of v4, /device:TPU:1, one launch (start us, length us, event | category | flops | bytes accessed | tf_op | source)
XLA Modules:
  0.0 151.7 jit_solution(10171526850502816365)
XLA Ops:
  0.6 0.1 pad_add_fusion.start_s
  0.7 0.8 copy-done.6
  1.5 0.8 copy-done.7
  2.3 10.2 %all_to_all.25.both = f32[4,8,2048]{2,1,0:T(8,128)S(1)} all-to-all(f32[4,8,2048]{2,1,0:T(8,128)S(1)} %shard_map.85), channel_id=1, replica_groups=mesh['z'=8,'y'=8,'core'=2,'vec'=4] {'vec'}, dimensions={0} | all-to-all | bytes 524288 | tf_op jit(solution)/shard_map/all_to_all | solution.py:520
  12.4 1.9 %copy-done = bf16[8,3,256,256]{3,2,1,0:T(8,128)(2,1)S(1)} copy-done((bf16[8,3,256,256]{3,2,1,0:T(8,128)(2,1)S(1)}, bf16[8,3,256,256]{3,2,1,0:T(8,128)(2,1)}, u32[]{:S(2)}) %copy-start) | copy-done | bytes 3145752
  14.3 1.2 copy-done.2
  15.6 0.7 copy-done.4
  16.3 0.7 copy-done.8
  17.0 2.2 %shard_map.86 = (f32[40,2048]{1,0:T(8,128)S(1)}, f32[4,8,256]{2,1,0:T(8,128)S(1)}, f32[8,128]{1,0:T(8,128)S(1)}) custom-call(s32[3,1024]{1,0:T(4,128)S(1)} %bitcast.3, s32[1024]{0:T(1024)S(1)} %copy-done.8, s32[2]{0:T(128)S(1)} %pad_add_fusion.start_s, bf16[8,256,256]{2,1,0:T(8,128)(2,1)S(1)} %copy-done.2, bf16[8,3,256,256]{3,2,1,0:T(8,128)(2,1)S(1)} %copy-done, ...), custom_call_target="tpu_custom_call" | custom-call | tf_op jit(solution)/shard_map/pallas_call | solution.py:49
  19.2 0.0 copy-start.5
  19.2 7.8 %collective-permute-start.1 = (f32[40,2048]{1,0:T(8,128)S(1)}, f32[40,2048]{1,0:T(8,128)S(1)}, u32[]{:S(2)}, u32[]{:S(2)}) collective-permute-start(f32[40,2048]{1,0:T(8,128)S(1)} %get-tuple-element.20.fc), channel_id=1, source_target_pairs={{4,0},{8,4},{12,8},{16,12},{20,16},{24,20},{28,24},{32,28},{36,32}... | collective-permute-start | bytes 983048 | tf_op jit(solution)/shard_map/ppermute | solution.py:514
  27.0 1.9 %collective-permute-start = (f32[40,2048]{1,0:T(8,128)S(1)}, f32[40,2048]{1,0:T(8,128)S(1)}, u32[]{:S(2)}, u32[]{:S(2)}) collective-permute-start(f32[40,2048]{1,0:T(8,128)S(1)} %get-tuple-element.20.fc), channel_id=1, source_target_pairs={{0,4},{4,8},{8,12},{12,16},{16,20},{20,24},{24,28},{28,32},{32,36}... | collective-permute-start | bytes 983048 | tf_op jit(solution)/shard_map/ppermute | solution.py:514
  28.9 0.4 collective-permute-done.1.fh
  29.3 3.6 %collective-permute-done.fl = f32[40,2048]{1,0:T(8,128)S(1)} collective-permute-done((f32[40,2048]{1,0:T(8,128)S(1)}, f32[40,2048]{1,0:T(8,128)S(1)}, u32[]{:S(2)}, u32[]{:S(2)}) %collective-permute-start) | collective-permute-done | bytes 327712 | tf_op jit(solution)/shard_map/ppermute | solution.py:514
  32.9 3.0 %shard_map.87 = (f32[16,2048]{1,0:T(8,128)S(1)}, f32[16,2048]{1,0:T(8,128)S(1)}, f32[16,128]{1,0:T(8,128)S(1)}) custom-call(s32[3,1024]{1,0:T(4,128)S(1)} %bitcast.4, s32[2]{0:T(128)S(1)} %pad_add_fusion.start_s, bf16[8,256,256]{2,1,0:T(8,128)(2,1)S(1)} %copy-done.2, bf16[8,3,256,256]{3,2,1,0:T(8,128)(2,1)S(1)} %copy-done.1, ...), custom_call_target="tpu_custom_call" | custom-call | tf_op jit(solution)/shard_map/pallas_call | solution.py:49
  35.9 1.9 %collective-permute-start.3 = (f32[16,2048]{1,0:T(8,128)S(1)}, f32[16,2048]{1,0:T(8,128)S(1)}, u32[]{:S(2)}, u32[]{:S(2)}) collective-permute-start(f32[16,2048]{1,0:T(8,128)S(1)} %get-tuple-element.21.ic.ix), channel_id=1, source_target_pairs={{4,0},{8,4},{12,8},{16,12},{20,16},{24,20},{28,24},{32,28},{36,32}... | collective-permute-start | bytes 393224 | tf_op jit(solution)/shard_map/ppermute | solution.py:514
  37.9 4.4 %collective-permute-start.2 = (f32[16,2048]{1,0:T(8,128)S(1)}, f32[16,2048]{1,0:T(8,128)S(1)}, u32[]{:S(2)}, u32[]{:S(2)}) collective-permute-start(f32[16,2048]{1,0:T(8,128)S(1)} %get-tuple-element.21.ic.ix), channel_id=1, source_target_pairs={{0,4},{4,8},{8,12},{12,16},{16,20},{20,24},{24,28},{28,32},{32,36}... | collective-permute-start | bytes 393224 | tf_op jit(solution)/shard_map/ppermute | solution.py:514
  42.3 0.7 collective-permute-done.3.ih
  43.0 1.2 collective-permute-done.2.il
  44.2 1.4 shard_map.88
  45.6 25.0 %all_to_all.26.got = f32[16,16,128]{2,1,0:T(8,128)S(1)} all-to-all(f32[16,16,128]{2,1,0:T(8,128)S(1)} %shard_map.88), channel_id=1, replica_groups=mesh['z'=8,'y'=8,'core'=2,'vec'=4] {'z','core'}, dimensions={0} | all-to-all | bytes 262144 | tf_op jit(solution)/shard_map/all_to_all | solution.py:547
  70.6 0.1 shard_map.89
  70.8 14.1 %all_to_all.27.got = f32[8,56,128]{2,1,0:T(8,128)S(1)} all-to-all(f32[8,56,128]{2,1,0:T(8,128)S(1)} %shard_map.89), channel_id=1, replica_groups=mesh['z'=8,'y'=8,'core'=2,'vec'=4] {'y'}, dimensions={0} | all-to-all | bytes 458752 | tf_op jit(solution)/shard_map/all_to_all | solution.py:555
  84.9 25.3 %shard_map.90 = (f32[16,16]{1,0:T(8,128)S(1)}, f32[16,32]{1,0:T(8,128)S(1)}, f32[16,128]{1,0:T(8,128)S(1)}) custom-call(s32[1024]{0:T(1024)S(1)} %copy-done.9, s32[2]{0:T(128)S(1)} %pad_add_fusion.start_s, f32[8,56,128]{2,1,0:T(8,128)S(1)} %all_to_all.27.got), custom_call_target="tpu_custom_call" | custom-call | tf_op jit(solution)/shard_map/pallas_call | solution.py:49
  110.2 3.4 %shard_map.91 = (f32[4,2048]{1,0:T(4,128)}, f32[4,2048]{1,0:T(4,128)}, f32[16,2048]{1,0:T(8,128)S(1)}, bf16[16,2048]{1,0:T(8,128)(2,1)S(1)}) custom-call(s32[3,1024]{1,0:T(4,128)S(1)} %bitcast.6, s32[2]{0:T(128)S(1)} %pad_add_fusion.start_s, bf16[8,256,256]{2,1,0:T(8,128)(2,1)S(1)} %copy-done.3, bf16[8,3,256,256]{3,2,1,0:T(8,128)(2,1)S(1)} %copy-done.1, ...), custom_call_target="tpu_custom_call" | custom-call | tf_op jit(solution)/shard_map/pallas_call | solution.py:49
  113.7 2.3 %collective-permute-start.5 = (bf16[16,2048]{1,0:T(8,128)(2,1)S(1)}, bf16[16,2048]{1,0:T(8,128)(2,1)S(1)}, u32[]{:S(2)}, u32[]{:S(2)}) collective-permute-start(bf16[16,2048]{1,0:T(8,128)(2,1)S(1)} %get-tuple-element.30.sc), channel_id=1, source_target_pairs={{4,0},{8,4},{12,8},{16,12},{20,16},{24,20},{28,24},{32,28},{36,32}... | collective-permute-start | bytes 196616 | tf_op jit(solution)/shard_map/ppermute | solution.py:514
  116.0 3.4 %collective-permute-start.4 = (bf16[16,2048]{1,0:T(8,128)(2,1)S(1)}, bf16[16,2048]{1,0:T(8,128)(2,1)S(1)}, u32[]{:S(2)}, u32[]{:S(2)}) collective-permute-start(bf16[16,2048]{1,0:T(8,128)(2,1)S(1)} %get-tuple-element.30.sc), channel_id=1, source_target_pairs={{0,4},{4,8},{8,12},{12,16},{16,20},{20,24},{24,28},{28,32},{32,36}... | collective-permute-start | bytes 196616 | tf_op jit(solution)/shard_map/ppermute | solution.py:514
  119.5 1.1 collective-permute-done.4.sl
  120.5 3.2 %shard_map.92 = f32[16,16,128]{2,1,0:T(8,128)S(1)} custom-call(s32[3,1024]{1,0:T(4,128)S(1)} %bitcast.7, s32[2]{0:T(128)S(1)} %pad_add_fusion.start_s, bf16[8,256,256]{2,1,0:T(8,128)(2,1)S(1)} %copy-done.3, bf16[8,3,256,256]{3,2,1,0:T(8,128)(2,1)S(1)} %copy-done.1, f32[16,2048]{1,0:T(8,128)S(1)} %get-tuple-element.29.w, ...), custom_call_target="tpu_custom_call" | custom-call | tf_op jit(solution)/shard_map/pallas_call | solution.py:49
  123.7 15.5 %all_to_all.28.got = f32[16,16,128]{2,1,0:T(8,128)S(1)} all-to-all(f32[16,16,128]{2,1,0:T(8,128)S(1)} %shard_map.92), channel_id=1, replica_groups=mesh['z'=8,'y'=8,'core'=2,'vec'=4] {'z','core'}, dimensions={0} | all-to-all | bytes 262144 | tf_op jit(solution)/shard_map/all_to_all | solution.py:591
  139.3 9.9 %all_to_all.29.got = f32[8,16,128]{2,1,0:T(8,128)S(1)} all-to-all(f32[8,16,128]{2,1,0:T(8,128)S(1)} %shard_map.93), channel_id=1, replica_groups=mesh['z'=8,'y'=8,'core'=2,'vec'=4] {'y'}, dimensions={0} | all-to-all | bytes 131072 | tf_op jit(solution)/shard_map/all_to_all | solution.py:593
  149.2 2.4 %shard_map.94 = f32[48,48]{1,0:T(8,128)} custom-call(f32[8,16,128]{2,1,0:T(8,128)S(1)} %all_to_all.29.got, f32[16,128]{1,0:T(8,128)S(1)} %get-tuple-element.32.gram), custom_call_target="tpu_custom_call" | custom-call | tf_op jit(solution)/shard_map/pallas_call | solution.py:49
  (16 shorter events, 0.1 us)
Async XLA Ops:
  0.7 0.8 copy-start.6
  1.5 0.8 copy-start.7
  12.4 1.9 %copy-start = (bf16[8,3,256,256]{3,2,1,0:T(8,128)(2,1)S(1)}, bf16[8,3,256,256]{3,2,1,0:T(8,128)(2,1)}, u32[]{:S(2)}) copy-start(bf16[8,3,256,256]{3,2,1,0:T(8,128)(2,1)} %link_t.7) | copy-start | bytes 9437188
  14.3 1.2 copy-start.2
  15.5 0.7 copy-start.4
  16.3 0.7 copy-start.8
  17.0 16.0 %copy-start.1 = (bf16[8,3,256,256]{3,2,1,0:T(8,128)(2,1)S(1)}, bf16[8,3,256,256]{3,2,1,0:T(8,128)(2,1)}, u32[]{:S(2)}) copy-start(bf16[8,3,256,256]{3,2,1,0:T(8,128)(2,1)} %link_t.7) | copy-start | bytes 9437188
  19.2 65.7 %copy-start.9 = (s32[1024]{0:T(1024)S(1)}, s32[1024]{0:T(1024)}, u32[]{:S(2)}) copy-start(s32[1024]{0:T(1024)} %coarse_s.3) | copy-start | bytes 12292
  19.2 91.0 %copy-start.3 = (bf16[8,256,256]{2,1,0:T(8,128)(2,1)S(1)}, bf16[8,256,256]{2,1,0:T(8,128)(2,1)}, u32[]{:S(2)}) copy-start(bf16[8,256,256]{2,1,0:T(8,128)(2,1)} %self_t.7) | copy-start | bytes 3145732
  19.2 91.0 %copy-start.5 = (s32[1024,3]{0,1:T(4,128)S(1)}, s32[1024,3]{0,1:T(4,128)}, u32[]{:S(2)}) copy-start(s32[1024,3]{0,1:T(4,128)} %param.8) | copy-start | bytes 36868
  19.2 10.1 %collective-permute-start.1 = (f32[40,2048]{1,0:T(8,128)S(1)}, f32[40,2048]{1,0:T(8,128)S(1)}, u32[]{:S(2)}, u32[]{:S(2)}) collective-permute-start(f32[40,2048]{1,0:T(8,128)S(1)} %get-tuple-element.20.fc), channel_id=1, source_target_pairs={{4,0},{8,4},{12,8},{16,12},{20,16},{24,20},{28,24},{32,28},{36,32}... | collective-permute-start | bytes 983048 | tf_op jit(solution)/shard_map/ppermute | solution.py:514
  27.0 5.9 %collective-permute-start = (f32[40,2048]{1,0:T(8,128)S(1)}, f32[40,2048]{1,0:T(8,128)S(1)}, u32[]{:S(2)}, u32[]{:S(2)}) collective-permute-start(f32[40,2048]{1,0:T(8,128)S(1)} %get-tuple-element.20.fc), channel_id=1, source_target_pairs={{0,4},{4,8},{8,12},{12,16},{16,20},{20,24},{24,28},{28,32},{32,36}... | collective-permute-start | bytes 983048 | tf_op jit(solution)/shard_map/ppermute | solution.py:514
  35.9 7.1 %collective-permute-start.3 = (f32[16,2048]{1,0:T(8,128)S(1)}, f32[16,2048]{1,0:T(8,128)S(1)}, u32[]{:S(2)}, u32[]{:S(2)}) collective-permute-start(f32[16,2048]{1,0:T(8,128)S(1)} %get-tuple-element.21.ic.ix), channel_id=1, source_target_pairs={{4,0},{8,4},{12,8},{16,12},{20,16},{24,20},{28,24},{32,28},{36,32}... | collective-permute-start | bytes 393224 | tf_op jit(solution)/shard_map/ppermute | solution.py:514
  37.9 6.3 %collective-permute-start.2 = (f32[16,2048]{1,0:T(8,128)S(1)}, f32[16,2048]{1,0:T(8,128)S(1)}, u32[]{:S(2)}, u32[]{:S(2)}) collective-permute-start(f32[16,2048]{1,0:T(8,128)S(1)} %get-tuple-element.21.ic.ix), channel_id=1, source_target_pairs={{0,4},{4,8},{8,12},{12,16},{16,20},{20,24},{24,28},{28,32},{32,36}... | collective-permute-start | bytes 393224 | tf_op jit(solution)/shard_map/ppermute | solution.py:514
  113.7 5.8 %collective-permute-start.5 = (bf16[16,2048]{1,0:T(8,128)(2,1)S(1)}, bf16[16,2048]{1,0:T(8,128)(2,1)S(1)}, u32[]{:S(2)}, u32[]{:S(2)}) collective-permute-start(bf16[16,2048]{1,0:T(8,128)(2,1)S(1)} %get-tuple-element.30.sc), channel_id=1, source_target_pairs={{4,0},{8,4},{12,8},{16,12},{20,16},{24,20},{28,24},{32,28},{36,32}... | collective-permute-start | bytes 196616 | tf_op jit(solution)/shard_map/ppermute | solution.py:514
  116.0 4.5 %collective-permute-start.4 = (bf16[16,2048]{1,0:T(8,128)(2,1)S(1)}, bf16[16,2048]{1,0:T(8,128)(2,1)S(1)}, u32[]{:S(2)}, u32[]{:S(2)}) collective-permute-start(bf16[16,2048]{1,0:T(8,128)(2,1)S(1)} %get-tuple-element.30.sc), channel_id=1, source_target_pairs={{0,4},{4,8},{8,12},{12,16},{16,20},{20,24},{24,28},{28,32},{32,36}... | collective-permute-start | bytes 196616 | tf_op jit(solution)/shard_map/ppermute | solution.py:514

commit v5 on v4

--- a/solution.py
+++ b/solution.py
@@ -38,9 +38,11 @@
     return lax.broadcasted_iota(jnp.int32, shape, dim)
 
 
-def run(kernel, inputs, outputs, scratch=(), smem=0):
+def run(kernel, inputs, outputs, scratch=(), smem=0, hbm=()):
     in_specs = [
-        pl.BlockSpec(memory_space=pltpu.SMEM if i < smem else pltpu.VMEM)
+        pl.BlockSpec(
+            memory_space=pltpu.SMEM if i < smem else pltpu.HBM if i in hbm else pltpu.VMEM
+        )
         for i in range(len(inputs))
     ]
     single = not isinstance(outputs, (list, tuple))
@@ -71,18 +73,22 @@
         out[v, mine:] = directions[...]
 
 
-def prep_kernel(links_s, coarse_s, start_s, self_t, link_t, both, fields, col, info):
+def prep_kernel(
+    links_s, coarse_s, start_s, self_far, link_far, nodes, col, info, link_t, self_t, arrived
+):
     count, size = self_t.shape[0], self_t.shape[1]
-    members, twice, _ = both.shape
-    mine = twice // 2
-    base = members * twice
-    for v in range(members):
-        fields[v * mine : (v + 1) * mine, :] = both[v, :mine]
-        fields[(members + v) * mine : (members + v + 1) * mine, :] = both[v, mine:]
+    copies = []
+    for b in range(count):
+        copies.append(pltpu.make_async_copy(self_far.at[b], self_t.at[b], arrived.at[b]))
+        copies.append(pltpu.make_async_copy(link_far.at[b], link_t.at[b], arrived.at[count + b]))
+    for copy in copies:
+        copy.start()
     ones = jnp.ones((8, size), BF16)
     diagonal = iota((size, size), 0) == iota((size, size), 1)
     lane = iota((1, LANE), 1)
     for b in range(count):
+        copies[2 * b].wait()
+        copies[2 * b + 1].wait()
         own = self_t[b]
         degree = nt(ones, own)[0:1]
         col[0, b : b + 1, :] = degree
@@ -97,10 +103,19 @@
             col[1 + s, b : b + 1, :] = jnp.sum(tile.astype(F32), axis=0, keepdims=True)
         diag = jnp.sum(jnp.where(diagonal, own.astype(F32), 0.0), axis=0, keepdims=True)
         span = slice(b * size, (b + 1) * size)
-        fields[base : base + 1, span] = degree
-        fields[base + 1 : base + 2, span] = 1.0 + spectral_shift - diag / degree
+        nodes[0:1, span] = degree
+        nodes[1:2, span] = 1.0 + spectral_shift - diag / degree
         info[b : b + 1, :] = row + ids.astype(F32)
-    fields[base + 2 : base + 8, :] = jnp.zeros((6, fields.shape[1]), F32)
+    nodes[2:8, :] = jnp.zeros((6, nodes.shape[1]), F32)
+
+
+def pack_kernel(both, nodes, out):
+    members, twice, _ = both.shape
+    mine = twice // 2
+    for v in range(members):
+        out[v * mine : (v + 1) * mine, :] = both[v, :mine]
+        out[(members + v) * mine : (members + v + 1) * mine, :] = both[v, mine:]
+    out[members * twice :, :] = nodes[...]
 
 
 def linked(links_s, start_s, b, s, count):
@@ -114,8 +129,12 @@
     return acc
 
 
-def image_kernel(links_s, start_s, self_t, link_t, fc, fl, fh, image_x, image_p, gram, win):
+def image_kernel(
+    links_s, start_s, self_far, link_t, fc, fl, fh, image_x, image_p, gram, win, self_t, arrived
+):
     count, size = self_t.shape[0], self_t.shape[1]
+    copy = pltpu.make_async_copy(self_far, self_t, arrived)
+    copy.start()
     half = image_x.shape[0]
     both = 2 * half
     for part, f in enumerate((fl, fc, fh)):
@@ -123,6 +142,7 @@
             span = slice(b * size, (b + 1) * size)
             root = jnp.sqrt(safe(f[both : both + 1, span]))
             win[part * count + b] = (f[:both, span] / root).astype(BF16)
+    copy.wait()
     for b in range(count):
         acc = apply_tiles(links_s, start_s, self_t, link_t, win, b, count)
         span = slice(b * size, (b + 1) * size)
@@ -330,11 +350,10 @@
         spread = jnp.where(here, values[0], 0.0)
         for s in range(1, 4):
             spread = spread + jnp.where(lanes == ids[s], values[s], 0.0)
-        member = jnp.where(here, 1.0, 0.0)
+        member = jnp.where(here, 1.0, 0.0).astype(BF16)
         hot[g] = member
-        member = member.astype(BF16)
-        for piece in split3(spread):
-            tiles = tiles + tn(member, piece)
+        pieces = tn(member, jnp.concatenate(split3(spread), axis=1))
+        tiles = tiles + (pieces[:, :nc] + (pieces[:, nc : 2 * nc] + pieces[:, 2 * nc :]))
     same = iota((nc, nc), 0) == iota((nc, nc), 1)
     agg_col = jnp.sum(jnp.where(same, agg, 0.0), axis=1, keepdims=True)
     inv_row = 1.0 / jnp.sqrt(agg)
@@ -351,7 +370,8 @@
     rhs = jnp.zeros((half, nc), F32)
     for g in range(GROUPS):
         block_rhs = nt(combine, uw[:, g * width : (g + 1) * width], EXACT)
-        rhs = rhs + nn(block_rhs, hot[g], EXACT)
+        pieces = nn(jnp.concatenate(split3(block_rhs), axis=0), hot[g])
+        rhs = rhs + (pieces[:half] + (pieces[half : 2 * half] + pieces[2 * half :]))
     rhs = rhs * inv_row
 
     block = min(LANE, nc)
@@ -518,19 +538,35 @@
     both = run(stack_kernel, (vectors, directions), arr((vec, 2 * mine, slab)))
     both, start_s = lax.optimization_barrier((both, start_s))
     both = lax.all_to_all(both, "vec", 0, 0)
-    fc, col, info = run(
+    self_far = pltpu.with_memory_space_constraint(self_tiles, pltpu.HBM)
+    nodes, col, info, link_v = run(
         prep_kernel,
-        (links_s, coarse_row, start_s, self_tiles, link_tiles, both),
-        (arr((2 * k + 8, slab)), arr((4, count, size)), arr((count, LANE))),
+        (
+            links_s, coarse_row, start_s,
+            self_far,
+            pltpu.with_memory_space_constraint(link_tiles, pltpu.HBM),
+        ),
+        (
+            arr((8, slab)), arr((4, count, size)), arr((count, LANE)),
+            arr(link_tiles.shape, BF16),
+        ),
+        scratch=(pltpu.VMEM(self_tiles.shape, BF16), pltpu.SemaphoreType.DMA((2 * count,))),
         smem=3,
-    )
+        hbm=(3, 4),
+    )
+    fc = run(pack_kernel, (both, nodes), arr((2 * k + 8, slab)))
     fl, fh = halo(fc)
     ic, ip, gram = run(
         image_kernel,
-        (links_s, start_s, self_tiles, link_tiles, fc, fl, fh),
+        (links_s, start_s, self_far, link_v, fc, fl, fh),
         (arr((k, slab)), arr((k, slab)), arr((k, LANE))),
-        scratch=(pltpu.VMEM((3 * count, 2 * k, size), BF16),),
+        scratch=(
+            pltpu.VMEM((3 * count, 2 * k, size), BF16),
+            pltpu.VMEM(self_tiles.shape, BF16),
+            pltpu.SemaphoreType.DMA,
+        ),
         smem=2,
+        hbm=(2,),
     )
     il, ih = halo(ic)
     sent = run(
@@ -563,7 +599,7 @@
             pltpu.VMEM((blocks, LANE), F32),
             pltpu.VMEM((blocks, LANE), F32),
             pltpu.VMEM((coarse_count, coarse_count), F32),
-            pltpu.VMEM((GROUPS, blocks, coarse_count), F32),
+            pltpu.VMEM((GROUPS, blocks, coarse_count), BF16),
             pltpu.VMEM((coarse_count, coarse_count), F32),
             pltpu.VMEM((coarse_count, min(LANE, coarse_count)), F32),
         ),
@@ -571,7 +607,7 @@
     )
     residual, my_corrected, corrected, scaled = run(
         correct_kernel,
-        (links_s, start_s, self_tiles, link_tiles, fc, fl, fh, ic, il, ih, coef, gain),
+        (links_s, start_s, self_tiles, link_v, fc, fl, fh, ic, il, ih, coef, gain),
         (arr((mine, slab)), arr((mine, slab)), arr((k, slab)), arr((k, slab), BF16)),
         scratch=(
             pltpu.VMEM((3 * count, k, size), BF16),
@@ -583,7 +619,7 @@
     sl, sh = halo(scaled)
     sent = run(
         search_kernel,
-        (links_s, start_s, self_tiles, link_tiles, corrected, scaled, sl, sh, fc, ic, ip),
+        (links_s, start_s, self_tiles, link_v, corrected, scaled, sl, sh, fc, ic, ip),
         arr((n_one, k, LANE)),
         scratch=(pltpu.VMEM((3 * count, k, size), BF16), pltpu.VMEM((k, slab), F32)),
         smem=2,

time: 152 us -> 147 us (0.967)
  blocking collectives: 74.8 us -> 64.4 us
  starting transfers between devices: 21.8 us -> 26.6 us
  Pallas kernels: 41.2 us -> 44.9 us
  local copies, waits for them, and re-layouts: 6.05 us -> 2.93 us
    all_to_all x1 -> x0, blocking collectives: 10.2 us -> none  [body(): both = lax.all_to_all(both, 'vec', 0, 0)]
    all_to_all x0 -> x1, starting transfers between devices: none -> 4.83 us  [body(): both = lax.all_to_all(both, 'vec', 0, 0)]
    pallas_call x10 -> x11, Pallas kernels: 41.2 us -> 44.9 us  [run(): pl.pallas_call(kernel, in_specs=in_specs, out_specs=specs[0] if single el...]
    unnamed x20 -> x14, local copies, waits for them, and re-layouts: 6.05 us -> 2.93 us
  transfers between devices with their start and end apart: 6 -> 7, of which waited for: 5 -> 4; matrix products, arithmetic and copies ran while one was open for 0% -> 0% of each run, Pallas kernels for 0% -> 3%
where the time goes in v5:
time: 147 us
  blocking collectives  64.4 us (44%)
  Pallas kernels  44.9 us (31%)
  starting transfers between devices  26.6 us (18%)
  waiting for transfers between devices  7 us (5%)
  local copies, waits for them, and re-layouts  2.93 us (2%)
    pallas_call x11, Pallas kernels, run(): pl.pallas_call(kernel, in_specs=in_specs, out_specs=specs[0] if single el...  44.9 us
    all_to_all x2, blocking collectives, body(): got = lax.all_to_all(sent, stage_one, 0, 0)  40.4 us
    all_to_all x2, blocking collectives, body(): got = lax.all_to_all(sent, 'y', 0, 0)  24.1 us
    ppermute x3, starting transfers between devices, halo(): lax.ppermute(a, row_axes, backward)  12 us
    ppermute x3, starting transfers between devices, halo(): lax.ppermute(a, row_axes, forward)  9.76 us
    ppermute x3, waiting for transfers between devices, halo(): lax.ppermute(a, row_axes, forward)  6.28 us
    all_to_all x1, starting transfers between devices, body(): both = lax.all_to_all(both, 'vec', 0, 0)  4.83 us
  transfers between devices with their start and end apart: 7, of which 4 were waited for; matrix products, arithmetic and copies ran while one was open for 0% of the time, Pallas kernels for 3%

profile of v5, /device:TPU:1, one launch (start us, length us, event | category | flops | bytes accessed | tf_op | source)
XLA Modules:
  0.0 146.7 jit_solution(3826046789997134023)
XLA Ops:
  0.6 0.0 copy-start.2
  0.7 0.1 pad_add_fusion.start_s
  0.7 0.8 copy-done.3
  1.5 0.8 copy-done.4
  2.2 0.7 shard_map.85
  3.0 4.8 %all-to-all-start = ((f32[4,8,2048]{2,1,0:T(8,128)}), f32[4,8,2048]{2,1,0:T(8,128)S(1)}, u32[]{:S(2)}, u32[]{:S(2)}) async-start(f32[4,8,2048]{2,1,0:T(8,128)} %shard_map.85), calls=%async_computation | async-start | bytes 524288 | tf_op jit(solution)/shard_map/all_to_all | solution.py:540
  7.8 0.7 copy-done.1
  8.5 0.7 copy-done.5
  9.2 4.7 %shard_map.86 = (f32[8,2048]{1,0:T(8,128)S(1)}, f32[4,8,256]{2,1,0:T(8,128)S(1)}, f32[8,128]{1,0:T(8,128)S(1)}, bf16[8,3,256,256]{3,2,1,0:T(8,128)(2,1)S(1)}) custom-call(s32[3,1024]{1,0:T(4,128)S(1)} %bitcast.3, s32[1024]{0:T(1024)S(1)} %copy-done.5, s32[2]{0:T(128)S(1)} %pad_add_fusion.start_s, bf16[8,256,256]{2,1,0:T(8,128)(2,1)} %self_t.3, ...), custom_call_target="tpu_custom_call" | custom-call | tf_op jit(solution)/shard_map/pallas_call | solution.py:51
  14.0 0.0 all-to-all-done.both
  14.0 0.1 shard_map.87.fc
  14.0 7.8 %collective-permute-start.1 = (f32[40,2048]{1,0:T(8,128)S(1)}, f32[40,2048]{1,0:T(8,128)S(1)}, u32[]{:S(2)}, u32[]{:S(2)}) collective-permute-start(f32[40,2048]{1,0:T(8,128)S(1)} %shard_map.87.fc), channel_id=1, source_target_pairs={{4,0},{8,4},{12,8},{16,12},{20,16},{24,20},{28,24},{32,28},{36,32}... | collective-permute-start | bytes 983048 | tf_op jit(solution)/shard_map/ppermute | solution.py:534
  21.9 1.9 %collective-permute-start = (f32[40,2048]{1,0:T(8,128)S(1)}, f32[40,2048]{1,0:T(8,128)S(1)}, u32[]{:S(2)}, u32[]{:S(2)}) collective-permute-start(f32[40,2048]{1,0:T(8,128)S(1)} %shard_map.87.fc), channel_id=1, source_target_pairs={{0,4},{4,8},{8,12},{12,16},{16,20},{20,24},{24,28},{28,32},{32,36}... | collective-permute-start | bytes 983048 | tf_op jit(solution)/shard_map/ppermute | solution.py:534
  23.8 4.0 %collective-permute-done.fl = f32[40,2048]{1,0:T(8,128)S(1)} collective-permute-done((f32[40,2048]{1,0:T(8,128)S(1)}, f32[40,2048]{1,0:T(8,128)S(1)}, u32[]{:S(2)}, u32[]{:S(2)}) %collective-permute-start) | collective-permute-done | bytes 327712 | tf_op jit(solution)/shard_map/ppermute | solution.py:534
  27.8 4.4 %shard_map.88 = (f32[16,2048]{1,0:T(8,128)S(1)}, f32[16,2048]{1,0:T(8,128)S(1)}, f32[16,128]{1,0:T(8,128)S(1)}) custom-call(s32[3,1024]{1,0:T(4,128)S(1)} %bitcast.4, s32[2]{0:T(128)S(1)} %pad_add_fusion.start_s, bf16[8,256,256]{2,1,0:T(8,128)(2,1)} %self_t.3, bf16[8,3,256,256]{3,2,1,0:T(8,128)(2,1)S(1)} %get-tuple-element.20.link_t, ...), custom_call_target="tpu_custom_call" | custom-call | tf_op jit(solution)/shard_map/pallas_call | solution.py:51
  32.2 1.9 %collective-permute-start.3 = (f32[16,2048]{1,0:T(8,128)S(1)}, f32[16,2048]{1,0:T(8,128)S(1)}, u32[]{:S(2)}, u32[]{:S(2)}) collective-permute-start(f32[16,2048]{1,0:T(8,128)S(1)} %get-tuple-element.23.ic.ix), channel_id=1, source_target_pairs={{4,0},{8,4},{12,8},{16,12},{20,16},{24,20},{28,24},{32,28},{36,32}... | collective-permute-start | bytes 393224 | tf_op jit(solution)/shard_map/ppermute | solution.py:534
  34.1 4.4 %collective-permute-start.2 = (f32[16,2048]{1,0:T(8,128)S(1)}, f32[16,2048]{1,0:T(8,128)S(1)}, u32[]{:S(2)}, u32[]{:S(2)}) collective-permute-start(f32[16,2048]{1,0:T(8,128)S(1)} %get-tuple-element.23.ic.ix), channel_id=1, source_target_pairs={{0,4},{4,8},{8,12},{12,16},{16,20},{20,24},{24,28},{28,32},{32,36}... | collective-permute-start | bytes 393224 | tf_op jit(solution)/shard_map/ppermute | solution.py:534
  38.5 0.7 collective-permute-done.3.ih
  39.2 1.2 collective-permute-done.2.il
  40.4 1.4 shard_map.89
  41.8 24.8 %all_to_all.25.got = f32[16,16,128]{2,1,0:T(8,128)S(1)} all-to-all(f32[16,16,128]{2,1,0:T(8,128)S(1)} %shard_map.89), channel_id=1, replica_groups=mesh['z'=8,'y'=8,'core'=2,'vec'=4] {'z','core'}, dimensions={0} | all-to-all | bytes 262144 | tf_op jit(solution)/shard_map/all_to_all | solution.py:583
  66.6 0.1 shard_map.90
  66.7 14.1 %all_to_all.26.got = f32[8,56,128]{2,1,0:T(8,128)S(1)} all-to-all(f32[8,56,128]{2,1,0:T(8,128)S(1)} %shard_map.90), channel_id=1, replica_groups=mesh['z'=8,'y'=8,'core'=2,'vec'=4] {'y'}, dimensions={0} | all-to-all | bytes 458752 | tf_op jit(solution)/shard_map/all_to_all | solution.py:591
  80.9 24.4 %shard_map.91 = (f32[16,16]{1,0:T(8,128)S(1)}, f32[16,32]{1,0:T(8,128)S(1)}, f32[16,128]{1,0:T(8,128)S(1)}) custom-call(s32[1024]{0:T(1024)S(1)} %copy-done.6, s32[2]{0:T(128)S(1)} %pad_add_fusion.start_s, f32[8,56,128]{2,1,0:T(8,128)S(1)} %all_to_all.26.got), custom_call_target="tpu_custom_call" | custom-call | tf_op jit(solution)/shard_map/pallas_call | solution.py:51
  105.3 3.5 %shard_map.92 = (f32[4,2048]{1,0:T(4,128)}, f32[4,2048]{1,0:T(4,128)}, f32[16,2048]{1,0:T(8,128)S(1)}, bf16[16,2048]{1,0:T(8,128)(2,1)S(1)}) custom-call(s32[3,1024]{1,0:T(4,128)S(1)} %bitcast.6, s32[2]{0:T(128)S(1)} %pad_add_fusion.start_s, bf16[8,256,256]{2,1,0:T(8,128)(2,1)S(1)} %copy-done, bf16[8,3,256,256]{3,2,1,0:T(8,128)(2,1)S(1)} %get-tuple-element.20.link_t, ...), custom_call_target="tpu_custom_call" | custom-call | tf_op jit(solution)/shard_map/pallas_call | solution.py:51
  108.8 2.3 %collective-permute-start.5 = (bf16[16,2048]{1,0:T(8,128)(2,1)S(1)}, bf16[16,2048]{1,0:T(8,128)(2,1)S(1)}, u32[]{:S(2)}, u32[]{:S(2)}) collective-permute-start(bf16[16,2048]{1,0:T(8,128)(2,1)S(1)} %get-tuple-element.32.sc), channel_id=1, source_target_pairs={{4,0},{8,4},{12,8},{16,12},{20,16},{24,20},{28,24},{32,28},{36,32}... | collective-permute-start | bytes 196616 | tf_op jit(solution)/shard_map/ppermute | solution.py:534
  111.1 3.5 %collective-permute-start.4 = (bf16[16,2048]{1,0:T(8,128)(2,1)S(1)}, bf16[16,2048]{1,0:T(8,128)(2,1)S(1)}, u32[]{:S(2)}, u32[]{:S(2)}) collective-permute-start(bf16[16,2048]{1,0:T(8,128)(2,1)S(1)} %get-tuple-element.32.sc), channel_id=1, source_target_pairs={{0,4},{4,8},{8,12},{12,16},{16,20},{20,24},{24,28},{28,32},{32,36}... | collective-permute-start | bytes 196616 | tf_op jit(solution)/shard_map/ppermute | solution.py:534
  114.6 1.1 collective-permute-done.4.sl
  115.6 3.1 %shard_map.93 = f32[16,16,128]{2,1,0:T(8,128)S(1)} custom-call(s32[3,1024]{1,0:T(4,128)S(1)} %bitcast.7, s32[2]{0:T(128)S(1)} %pad_add_fusion.start_s, bf16[8,256,256]{2,1,0:T(8,128)(2,1)S(1)} %copy-done, bf16[8,3,256,256]{3,2,1,0:T(8,128)(2,1)S(1)} %get-tuple-element.20.link_t, f32[16,2048]{1,0:T(8,128)S(1)} %get-tuple-element.31.w, ...), custom_call_target="tpu_custom_call" | custom-call | tf_op jit(solution)/shard_map/pallas_call | solution.py:51
  118.8 15.5 %all_to_all.27.got = f32[16,16,128]{2,1,0:T(8,128)S(1)} all-to-all(f32[16,16,128]{2,1,0:T(8,128)S(1)} %shard_map.93), channel_id=1, replica_groups=mesh['z'=8,'y'=8,'core'=2,'vec'=4] {'z','core'}, dimensions={0} | all-to-all | bytes 262144 | tf_op jit(solution)/shard_map/all_to_all | solution.py:627
  134.3 9.9 %all_to_all.28.got = f32[8,16,128]{2,1,0:T(8,128)S(1)} all-to-all(f32[8,16,128]{2,1,0:T(8,128)S(1)} %shard_map.94), channel_id=1, replica_groups=mesh['z'=8,'y'=8,'core'=2,'vec'=4] {'y'}, dimensions={0} | all-to-all | bytes 131072 | tf_op jit(solution)/shard_map/all_to_all | solution.py:629
  144.3 2.4 %shard_map.95 = f32[48,48]{1,0:T(8,128)} custom-call(f32[8,16,128]{2,1,0:T(8,128)S(1)} %all_to_all.28.got, f32[16,128]{1,0:T(8,128)S(1)} %get-tuple-element.34.gram), custom_call_target="tpu_custom_call" | custom-call | tf_op jit(solution)/shard_map/pallas_call | solution.py:51
  (12 shorter events, 0.0 us)
Async XLA Ops:
  0.6 27.2 %copy-start.2 = (s32[1024,3]{0,1:T(4,128)S(1)}, s32[1024,3]{0,1:T(4,128)}, u32[]{:S(2)}) copy-start(s32[1024,3]{0,1:T(4,128)} %param.8) | copy-start | bytes 36868
  0.7 0.8 copy-start.3
  1.5 0.8 copy-start.4
  3.0 11.0 %all-to-all-start = ((f32[4,8,2048]{2,1,0:T(8,128)}), f32[4,8,2048]{2,1,0:T(8,128)S(1)}, u32[]{:S(2)}, u32[]{:S(2)}) async-start(f32[4,8,2048]{2,1,0:T(8,128)} %shard_map.85), calls=%async_computation | async-start | bytes 524288 | tf_op jit(solution)/shard_map/all_to_all | solution.py:540
  7.8 0.7 copy-start.1
  8.5 0.7 copy-start.5
  14.0 9.7 %collective-permute-start.1 = (f32[40,2048]{1,0:T(8,128)S(1)}, f32[40,2048]{1,0:T(8,128)S(1)}, u32[]{:S(2)}, u32[]{:S(2)}) collective-permute-start(f32[40,2048]{1,0:T(8,128)S(1)} %shard_map.87.fc), channel_id=1, source_target_pairs={{4,0},{8,4},{12,8},{16,12},{20,16},{24,20},{28,24},{32,28},{36,32}... | collective-permute-start | bytes 983048 | tf_op jit(solution)/shard_map/ppermute | solution.py:534
  21.9 5.9 %collective-permute-start = (f32[40,2048]{1,0:T(8,128)S(1)}, f32[40,2048]{1,0:T(8,128)S(1)}, u32[]{:S(2)}, u32[]{:S(2)}) collective-permute-start(f32[40,2048]{1,0:T(8,128)S(1)} %shard_map.87.fc), channel_id=1, source_target_pairs={{0,4},{4,8},{8,12},{12,16},{16,20},{20,24},{24,28},{28,32},{32,36}... | collective-permute-start | bytes 983048 | tf_op jit(solution)/shard_map/ppermute | solution.py:534
  27.8 53.1 %copy-start.6 = (s32[1024]{0:T(1024)S(1)}, s32[1024]{0:T(1024)}, u32[]{:S(2)}) copy-start(s32[1024]{0:T(1024)} %coarse_s.3) | copy-start | bytes 12292
  27.8 77.5 %copy-start = (bf16[8,256,256]{2,1,0:T(8,128)(2,1)S(1)}, bf16[8,256,256]{2,1,0:T(8,128)(2,1)}, u32[]{:S(2)}) copy-start(bf16[8,256,256]{2,1,0:T(8,128)(2,1)} %self_t.3) | copy-start | bytes 3145732
  32.2 7.0 %collective-permute-start.3 = (f32[16,2048]{1,0:T(8,128)S(1)}, f32[16,2048]{1,0:T(8,128)S(1)}, u32[]{:S(2)}, u32[]{:S(2)}) collective-permute-start(f32[16,2048]{1,0:T(8,128)S(1)} %get-tuple-element.23.ic.ix), channel_id=1, source_target_pairs={{4,0},{8,4},{12,8},{16,12},{20,16},{24,20},{28,24},{32,28},{36,32}... | collective-permute-start | bytes 393224 | tf_op jit(solution)/shard_map/ppermute | solution.py:534
  34.1 6.3 %collective-permute-start.2 = (f32[16,2048]{1,0:T(8,128)S(1)}, f32[16,2048]{1,0:T(8,128)S(1)}, u32[]{:S(2)}, u32[]{:S(2)}) collective-permute-start(f32[16,2048]{1,0:T(8,128)S(1)} %get-tuple-element.23.ic.ix), channel_id=1, source_target_pairs={{0,4},{4,8},{8,12},{12,16},{16,20},{20,24},{24,28},{28,32},{32,36}... | collective-permute-start | bytes 393224 | tf_op jit(solution)/shard_map/ppermute | solution.py:534
  108.8 5.8 %collective-permute-start.5 = (bf16[16,2048]{1,0:T(8,128)(2,1)S(1)}, bf16[16,2048]{1,0:T(8,128)(2,1)S(1)}, u32[]{:S(2)}, u32[]{:S(2)}) collective-permute-start(bf16[16,2048]{1,0:T(8,128)(2,1)S(1)} %get-tuple-element.32.sc), channel_id=1, source_target_pairs={{4,0},{8,4},{12,8},{16,12},{20,16},{24,20},{28,24},{32,28},{36,32}... | collective-permute-start | bytes 196616 | tf_op jit(solution)/shard_map/ppermute | solution.py:534
  111.1 4.5 %collective-permute-start.4 = (bf16[16,2048]{1,0:T(8,128)(2,1)S(1)}, bf16[16,2048]{1,0:T(8,128)(2,1)S(1)}, u32[]{:S(2)}, u32[]{:S(2)}) collective-permute-start(bf16[16,2048]{1,0:T(8,128)(2,1)S(1)} %get-tuple-element.32.sc), channel_id=1, source_target_pairs={{0,4},{4,8},{8,12},{12,16},{16,20},{20,24},{24,28},{28,32},{32,36}... | collective-permute-start | bytes 196616 | tf_op jit(solution)/shard_map/ppermute | solution.py:534

commit v6 on v5

--- a/solution.py
+++ b/solution.py
@@ -66,8 +66,14 @@
     return jnp.where(value > 0.0, value, 1.0)
 
 
-def stack_kernel(vectors, directions, out):
+def stack_kernel(far_vectors, far_directions, out, vectors, directions, arrived):
     mine = vectors.shape[0]
+    first = pltpu.make_async_copy(far_vectors, vectors, arrived.at[0])
+    second = pltpu.make_async_copy(far_directions, directions, arrived.at[1])
+    first.start()
+    second.start()
+    first.wait()
+    second.wait()
     for v in range(out.shape[0]):
         out[v, :mine] = vectors[...]
         out[v, mine:] = directions[...]
@@ -535,7 +541,20 @@
 
     start_s = jnp.stack([row_index * count, lax.axis_index("vec")]).astype(jnp.int32)
     links_s = links.T
-    both = run(stack_kernel, (vectors, directions), arr((vec, 2 * mine, slab)))
+    both = run(
+        stack_kernel,
+        (
+            pltpu.with_memory_space_constraint(vectors, pltpu.HBM),
+            pltpu.with_memory_space_constraint(directions, pltpu.HBM),
+        ),
+        arr((vec, 2 * mine, slab)),
+        scratch=(
+            pltpu.VMEM((mine, slab), F32),
+            pltpu.VMEM((mine, slab), F32),
+            pltpu.SemaphoreType.DMA((2,)),
+        ),
+        hbm=(0, 1),
+    )
     both, start_s = lax.optimization_barrier((both, start_s))
     both = lax.all_to_all(both, "vec", 0, 0)
     self_far = pltpu.with_memory_space_constraint(self_tiles, pltpu.HBM)

time: 147 us -> 147 us (level)
  local copies, waits for them, and re-layouts: 2.93 us -> 1.42 us
    unnamed x14 -> x10, local copies, waits for them, and re-layouts: 2.93 us -> 1.42 us
where the time goes in v6:
time: 147 us; the launch traced here: 146 us
  blocking collectives  64.4 us (44%)
  Pallas kernels  45.7 us (31%)
  starting transfers between devices  26.6 us (18%)
  waiting for transfers between devices  7 us (5%)
    pallas_call x11, Pallas kernels, run(): pl.pallas_call(kernel, in_specs=in_specs, out_specs=specs[0] if single el...  45.7 us
    all_to_all x2, blocking collectives, body(): got = lax.all_to_all(sent, stage_one, 0, 0)  40.4 us
    all_to_all x2, blocking collectives, body(): got = lax.all_to_all(sent, 'y', 0, 0)  24.1 us
    ppermute x3, starting transfers between devices, halo(): lax.ppermute(a, row_axes, backward)  12 us
    ppermute x3, starting transfers between devices, halo(): lax.ppermute(a, row_axes, forward)  9.76 us
    ppermute x3, waiting for transfers between devices, halo(): lax.ppermute(a, row_axes, forward)  6.28 us
    all_to_all x1, starting transfers between devices, body(): both = lax.all_to_all(both, 'vec', 0, 0)  4.84 us
  transfers between devices with their start and end apart: 7, of which 4 were waited for; matrix products, arithmetic and copies ran while one was open for 0% of the time, Pallas kernels for 3%

profile of v6, /device:TPU:1, one launch (start us, length us, event | category | flops | bytes accessed | tf_op | source)
XLA Modules:
  0.0 146.0 jit_solution(7592507999472390011)
XLA Ops:
  0.6 0.0 copy-start.2
  0.7 0.1 pad_add_fusion.start_s
  0.7 1.5 %shard_map.85 = f32[4,8,2048]{2,1,0:T(8,128)} custom-call(f32[4,2048]{1,0:T(4,128)} %far_vectors.1, f32[4,2048]{1,0:T(4,128)} %far_directions.1), custom_call_target="tpu_custom_call" | custom-call | tf_op jit(solution)/shard_map/pallas_call | solution.py:51
  2.3 4.8 %all-to-all-start = ((f32[4,8,2048]{2,1,0:T(8,128)}), f32[4,8,2048]{2,1,0:T(8,128)S(1)}, u32[]{:S(2)}, u32[]{:S(2)}) async-start(f32[4,8,2048]{2,1,0:T(8,128)} %shard_map.85), calls=%async_computation | async-start | bytes 524288 | tf_op jit(solution)/shard_map/all_to_all | solution.py:559
  7.1 0.7 copy-done.1
  7.8 0.7 copy-done.3
  8.5 4.7 %shard_map.86 = (f32[8,2048]{1,0:T(8,128)S(1)}, f32[4,8,256]{2,1,0:T(8,128)S(1)}, f32[8,128]{1,0:T(8,128)S(1)}, bf16[8,3,256,256]{3,2,1,0:T(8,128)(2,1)S(1)}) custom-call(s32[3,1024]{1,0:T(4,128)S(1)} %bitcast.3, s32[1024]{0:T(1024)S(1)} %copy-done.3, s32[2]{0:T(128)S(1)} %pad_add_fusion.start_s, bf16[8,256,256]{2,1,0:T(8,128)(2,1)} %self_t.3, ...), custom_call_target="tpu_custom_call" | custom-call | tf_op jit(solution)/shard_map/pallas_call | solution.py:51
  13.3 0.0 all-to-all-done.both
  13.3 0.1 shard_map.87.fc
  13.3 7.8 %collective-permute-start.1 = (f32[40,2048]{1,0:T(8,128)S(1)}, f32[40,2048]{1,0:T(8,128)S(1)}, u32[]{:S(2)}, u32[]{:S(2)}) collective-permute-start(f32[40,2048]{1,0:T(8,128)S(1)} %shard_map.87.fc), channel_id=1, source_target_pairs={{4,0},{8,4},{12,8},{16,12},{20,16},{24,20},{28,24},{32,28},{36,32}... | collective-permute-start | bytes 983048 | tf_op jit(solution)/shard_map/ppermute | solution.py:540
  21.1 1.9 %collective-permute-start = (f32[40,2048]{1,0:T(8,128)S(1)}, f32[40,2048]{1,0:T(8,128)S(1)}, u32[]{:S(2)}, u32[]{:S(2)}) collective-permute-start(f32[40,2048]{1,0:T(8,128)S(1)} %shard_map.87.fc), channel_id=1, source_target_pairs={{0,4},{4,8},{8,12},{12,16},{16,20},{20,24},{24,28},{28,32},{32,36}... | collective-permute-start | bytes 983048 | tf_op jit(solution)/shard_map/ppermute | solution.py:540
  23.1 0.0 collective-permute-done.1.fh
  23.1 4.0 %collective-permute-done.fl = f32[40,2048]{1,0:T(8,128)S(1)} collective-permute-done((f32[40,2048]{1,0:T(8,128)S(1)}, f32[40,2048]{1,0:T(8,128)S(1)}, u32[]{:S(2)}, u32[]{:S(2)}) %collective-permute-start) | collective-permute-done | bytes 327712 | tf_op jit(solution)/shard_map/ppermute | solution.py:540
  27.1 4.4 %shard_map.88 = (f32[16,2048]{1,0:T(8,128)S(1)}, f32[16,2048]{1,0:T(8,128)S(1)}, f32[16,128]{1,0:T(8,128)S(1)}) custom-call(s32[3,1024]{1,0:T(4,128)S(1)} %bitcast.4, s32[2]{0:T(128)S(1)} %pad_add_fusion.start_s, bf16[8,256,256]{2,1,0:T(8,128)(2,1)} %self_t.3, bf16[8,3,256,256]{3,2,1,0:T(8,128)(2,1)S(1)} %get-tuple-element.20.link_t, ...), custom_call_target="tpu_custom_call" | custom-call | tf_op jit(solution)/shard_map/pallas_call | solution.py:51
  31.4 1.9 %collective-permute-start.3 = (f32[16,2048]{1,0:T(8,128)S(1)}, f32[16,2048]{1,0:T(8,128)S(1)}, u32[]{:S(2)}, u32[]{:S(2)}) collective-permute-start(f32[16,2048]{1,0:T(8,128)S(1)} %get-tuple-element.23.ic.ix), channel_id=1, source_target_pairs={{4,0},{8,4},{12,8},{16,12},{20,16},{24,20},{28,24},{32,28},{36,32}... | collective-permute-start | bytes 393224 | tf_op jit(solution)/shard_map/ppermute | solution.py:540
  33.4 4.4 %collective-permute-start.2 = (f32[16,2048]{1,0:T(8,128)S(1)}, f32[16,2048]{1,0:T(8,128)S(1)}, u32[]{:S(2)}, u32[]{:S(2)}) collective-permute-start(f32[16,2048]{1,0:T(8,128)S(1)} %get-tuple-element.23.ic.ix), channel_id=1, source_target_pairs={{0,4},{4,8},{8,12},{12,16},{16,20},{20,24},{24,28},{28,32},{32,36}... | collective-permute-start | bytes 393224 | tf_op jit(solution)/shard_map/ppermute | solution.py:540
  37.8 0.7 collective-permute-done.3.ih
  38.5 1.2 collective-permute-done.2.il
  39.7 1.4 shard_map.89
  41.1 24.8 %all_to_all.25.got = f32[16,16,128]{2,1,0:T(8,128)S(1)} all-to-all(f32[16,16,128]{2,1,0:T(8,128)S(1)} %shard_map.89), channel_id=1, replica_groups=mesh['z'=8,'y'=8,'core'=2,'vec'=4] {'z','core'}, dimensions={0} | all-to-all | bytes 262144 | tf_op jit(solution)/shard_map/all_to_all | solution.py:602
  65.9 0.1 shard_map.90
  66.0 14.1 %all_to_all.26.got = f32[8,56,128]{2,1,0:T(8,128)S(1)} all-to-all(f32[8,56,128]{2,1,0:T(8,128)S(1)} %shard_map.90), channel_id=1, replica_groups=mesh['z'=8,'y'=8,'core'=2,'vec'=4] {'y'}, dimensions={0} | all-to-all | bytes 458752 | tf_op jit(solution)/shard_map/all_to_all | solution.py:610
  80.1 24.4 %shard_map.91 = (f32[16,16]{1,0:T(8,128)S(1)}, f32[16,32]{1,0:T(8,128)S(1)}, f32[16,128]{1,0:T(8,128)S(1)}) custom-call(s32[1024]{0:T(1024)S(1)} %copy-done.4, s32[2]{0:T(128)S(1)} %pad_add_fusion.start_s, f32[8,56,128]{2,1,0:T(8,128)S(1)} %all_to_all.26.got), custom_call_target="tpu_custom_call" | custom-call | tf_op jit(solution)/shard_map/pallas_call | solution.py:51
  104.6 3.5 %shard_map.92 = (f32[4,2048]{1,0:T(4,128)}, f32[4,2048]{1,0:T(4,128)}, f32[16,2048]{1,0:T(8,128)S(1)}, bf16[16,2048]{1,0:T(8,128)(2,1)S(1)}) custom-call(s32[3,1024]{1,0:T(4,128)S(1)} %bitcast.6, s32[2]{0:T(128)S(1)} %pad_add_fusion.start_s, bf16[8,256,256]{2,1,0:T(8,128)(2,1)S(1)} %copy-done, bf16[8,3,256,256]{3,2,1,0:T(8,128)(2,1)S(1)} %get-tuple-element.20.link_t, ...), custom_call_target="tpu_custom_call" | custom-call | tf_op jit(solution)/shard_map/pallas_call | solution.py:51
  108.0 2.3 %collective-permute-start.5 = (bf16[16,2048]{1,0:T(8,128)(2,1)S(1)}, bf16[16,2048]{1,0:T(8,128)(2,1)S(1)}, u32[]{:S(2)}, u32[]{:S(2)}) collective-permute-start(bf16[16,2048]{1,0:T(8,128)(2,1)S(1)} %get-tuple-element.32.sc), channel_id=1, source_target_pairs={{4,0},{8,4},{12,8},{16,12},{20,16},{24,20},{28,24},{32,28},{36,32}... | collective-permute-start | bytes 196616 | tf_op jit(solution)/shard_map/ppermute | solution.py:540
  110.4 3.5 %collective-permute-start.4 = (bf16[16,2048]{1,0:T(8,128)(2,1)S(1)}, bf16[16,2048]{1,0:T(8,128)(2,1)S(1)}, u32[]{:S(2)}, u32[]{:S(2)}) collective-permute-start(bf16[16,2048]{1,0:T(8,128)(2,1)S(1)} %get-tuple-element.32.sc), channel_id=1, source_target_pairs={{0,4},{4,8},{8,12},{12,16},{16,20},{20,24},{24,28},{28,32},{32,36}... | collective-permute-start | bytes 196616 | tf_op jit(solution)/shard_map/ppermute | solution.py:540
  113.8 0.0 collective-permute-done.5.sh
  113.8 1.1 collective-permute-done.4.sl
  114.9 3.1 %shard_map.93 = f32[16,16,128]{2,1,0:T(8,128)S(1)} custom-call(s32[3,1024]{1,0:T(4,128)S(1)} %bitcast.7, s32[2]{0:T(128)S(1)} %pad_add_fusion.start_s, bf16[8,256,256]{2,1,0:T(8,128)(2,1)S(1)} %copy-done, bf16[8,3,256,256]{3,2,1,0:T(8,128)(2,1)S(1)} %get-tuple-element.20.link_t, f32[16,2048]{1,0:T(8,128)S(1)} %get-tuple-element.31.w, ...), custom_call_target="tpu_custom_call" | custom-call | tf_op jit(solution)/shard_map/pallas_call | solution.py:51
  118.1 15.5 %all_to_all.27.got = f32[16,16,128]{2,1,0:T(8,128)S(1)} all-to-all(f32[16,16,128]{2,1,0:T(8,128)S(1)} %shard_map.93), channel_id=1, replica_groups=mesh['z'=8,'y'=8,'core'=2,'vec'=4] {'z','core'}, dimensions={0} | all-to-all | bytes 262144 | tf_op jit(solution)/shard_map/all_to_all | solution.py:646
  133.6 9.9 %all_to_all.28.got = f32[8,16,128]{2,1,0:T(8,128)S(1)} all-to-all(f32[8,16,128]{2,1,0:T(8,128)S(1)} %shard_map.94), channel_id=1, replica_groups=mesh['z'=8,'y'=8,'core'=2,'vec'=4] {'y'}, dimensions={0} | all-to-all | bytes 131072 | tf_op jit(solution)/shard_map/all_to_all | solution.py:648
  143.6 2.4 %shard_map.95 = f32[48,48]{1,0:T(8,128)} custom-call(f32[8,16,128]{2,1,0:T(8,128)S(1)} %all_to_all.28.got, f32[16,128]{1,0:T(8,128)S(1)} %get-tuple-element.34.gram), custom_call_target="tpu_custom_call" | custom-call | tf_op jit(solution)/shard_map/pallas_call | solution.py:51
  (8 shorter events, 0.0 us)
Async XLA Ops:
  0.6 26.4 %copy-start.2 = (s32[1024,3]{0,1:T(4,128)S(1)}, s32[1024,3]{0,1:T(4,128)}, u32[]{:S(2)}) copy-start(s32[1024,3]{0,1:T(4,128)} %param.8) | copy-start | bytes 36868
  2.3 11.0 %all-to-all-start = ((f32[4,8,2048]{2,1,0:T(8,128)}), f32[4,8,2048]{2,1,0:T(8,128)S(1)}, u32[]{:S(2)}, u32[]{:S(2)}) async-start(f32[4,8,2048]{2,1,0:T(8,128)} %shard_map.85), calls=%async_computation | async-start | bytes 524288 | tf_op jit(solution)/shard_map/all_to_all | solution.py:559
  7.1 0.7 copy-start.1
  7.8 0.7 copy-start.3
  13.3 9.7 %collective-permute-start.1 = (f32[40,2048]{1,0:T(8,128)S(1)}, f32[40,2048]{1,0:T(8,128)S(1)}, u32[]{:S(2)}, u32[]{:S(2)}) collective-permute-start(f32[40,2048]{1,0:T(8,128)S(1)} %shard_map.87.fc), channel_id=1, source_target_pairs={{4,0},{8,4},{12,8},{16,12},{20,16},{24,20},{28,24},{32,28},{36,32}... | collective-permute-start | bytes 983048 | tf_op jit(solution)/shard_map/ppermute | solution.py:540
  21.1 5.9 %collective-permute-start = (f32[40,2048]{1,0:T(8,128)S(1)}, f32[40,2048]{1,0:T(8,128)S(1)}, u32[]{:S(2)}, u32[]{:S(2)}) collective-permute-start(f32[40,2048]{1,0:T(8,128)S(1)} %shard_map.87.fc), channel_id=1, source_target_pairs={{0,4},{4,8},{8,12},{12,16},{16,20},{20,24},{24,28},{28,32},{32,36}... | collective-permute-start | bytes 983048 | tf_op jit(solution)/shard_map/ppermute | solution.py:540
  27.1 53.1 %copy-start.4 = (s32[1024]{0:T(1024)S(1)}, s32[1024]{0:T(1024)}, u32[]{:S(2)}) copy-start(s32[1024]{0:T(1024)} %coarse_s.3) | copy-start | bytes 12292
  27.1 77.5 %copy-start = (bf16[8,256,256]{2,1,0:T(8,128)(2,1)S(1)}, bf16[8,256,256]{2,1,0:T(8,128)(2,1)}, u32[]{:S(2)}) copy-start(bf16[8,256,256]{2,1,0:T(8,128)(2,1)} %self_t.3) | copy-start | bytes 3145732
  31.4 7.0 %collective-permute-start.3 = (f32[16,2048]{1,0:T(8,128)S(1)}, f32[16,2048]{1,0:T(8,128)S(1)}, u32[]{:S(2)}, u32[]{:S(2)}) collective-permute-start(f32[16,2048]{1,0:T(8,128)S(1)} %get-tuple-element.23.ic.ix), channel_id=1, source_target_pairs={{4,0},{8,4},{12,8},{16,12},{20,16},{24,20},{28,24},{32,28},{36,32}... | collective-permute-start | bytes 393224 | tf_op jit(solution)/shard_map/ppermute | solution.py:540
  33.4 6.3 %collective-permute-start.2 = (f32[16,2048]{1,0:T(8,128)S(1)}, f32[16,2048]{1,0:T(8,128)S(1)}, u32[]{:S(2)}, u32[]{:S(2)}) collective-permute-start(f32[16,2048]{1,0:T(8,128)S(1)} %get-tuple-element.23.ic.ix), channel_id=1, source_target_pairs={{0,4},{4,8},{8,12},{12,16},{16,20},{20,24},{24,28},{28,32},{32,36}... | collective-permute-start | bytes 393224 | tf_op jit(solution)/shard_map/ppermute | solution.py:540
  108.0 5.8 %collective-permute-start.5 = (bf16[16,2048]{1,0:T(8,128)(2,1)S(1)}, bf16[16,2048]{1,0:T(8,128)(2,1)S(1)}, u32[]{:S(2)}, u32[]{:S(2)}) collective-permute-start(bf16[16,2048]{1,0:T(8,128)(2,1)S(1)} %get-tuple-element.32.sc), channel_id=1, source_target_pairs={{4,0},{8,4},{12,8},{16,12},{20,16},{24,20},{28,24},{32,28},{36,32}... | collective-permute-start | bytes 196616 | tf_op jit(solution)/shard_map/ppermute | solution.py:540
  110.4 4.6 %collective-permute-start.4 = (bf16[16,2048]{1,0:T(8,128)(2,1)S(1)}, bf16[16,2048]{1,0:T(8,128)(2,1)S(1)}, u32[]{:S(2)}, u32[]{:S(2)}) collective-permute-start(bf16[16,2048]{1,0:T(8,128)(2,1)S(1)} %get-tuple-element.32.sc), channel_id=1, source_target_pairs={{0,4},{4,8},{8,12},{12,16},{16,20},{20,24},{24,28},{28,32},{32,36}... | collective-permute-start | bytes 196616 | tf_op jit(solution)/shard_map/ppermute | solution.py:540
